TPU v7x, 32 devices: a whole 2x2x4 slice. The times are simulated.
32 devices in a mesh: ctx: 2 (over x), tp: 4 (over y, core), dp: 4 (over z).
Axes of the slice: x: 2, y: 2, z: 4, core: 2. Of those that a mesh axis runs over, the one named last changes fastest.
Arguments:
- byte_embed: bfloat16 [8192, 1024], P(('dp', 'ctx', 'tp')), parts along dimension 0, may hold values from -6 to 6
- patch_start: int32 [8192], P(('dp', 'ctx', 'tp')), parts along dimension 0, may hold values from 0 to 1, as said below
- enc_gain: float32 [1024], replicated, may hold values from 0.1 to 1.9
- enc_qkv: bfloat16 [1024, 3072], replicated, may hold values from -4 to 4
- enc_out: bfloat16 [1024, 1024], replicated, may hold values from -0.1875 to 0.1875
- up_proj: bfloat16 [1024, 4096], P('ctx', 'tp'), may hold values from -0.1875 to 0.1875
- lat_gain: float32 [4096], replicated, may hold values from 0.1 to 1.9
- query_proj: bfloat16 [4096, 2048], P('ctx', 'tp'), may hold values from -4 to 4
- key_proj: bfloat16 [4096, 512], P('ctx', 'tp'), may hold values from -4 to 4
- value_matrix: bfloat16 [4096, 512], P('ctx', 'tp'), may hold values from -0.09375 to 0.09375
- out_proj: bfloat16 [2048, 4096], P('tp', 'ctx'), may hold values from -0.125 to 0.125
- down_proj: bfloat16 [4096, 1024], P('tp', 'ctx'), may hold values from -0.09375 to 0.09375
Outputs:
- byte_states: bfloat16 [8192, 1024], P(('dp', 'ctx', 'tp')), parts along dimension 0
There are 4 independent parts, one for each index of `dp`. A program takes and returns all parts, laid end to end along the dimension named above; an argument that names none is the same for every part. Nothing has to cross between parts.
Inputs may be any that keep to these rules, and one draw needn't show every extreme that they name: `patch_start`: byte 0 begins a patch; every patch spans 1 to 19 bytes; each aligned group of 1024 bytes holds at most 256 patch starts, and some group holds exactly 256.
All inputs are finite; a program needn't handle non-finite values.
Results may differ from a plain program's by a relative error of at most 0.015.
Values may be sent and summed in bfloat16 or wider, within the bound.
No kernel may reach another device: no remote copies, remote signals or barrier semaphores. Data moves between devices by JAX's collectives and lax.ppermute only.
A program may use at most 128 MiB of HBM per device.

v0:
```python
import jax
import jax.numpy as jnp
from jax import lax
from jax.experimental import pallas as pl
from jax.experimental.pallas import tpu as pltpu
from jax.sharding import PartitionSpec as P


HB = 64
HEAD_SIZE = 128
EPS = 1e-05
LEAD = 32
NEG = -1e30
VMEM_LIMIT = 24 << 20
F32 = jnp.float32
BF16 = jnp.bfloat16


def dot(a, b):
    return jnp.dot(a, b, preferred_element_type=F32)


def dot_nt(a, b):
    return lax.dot_general(a, b, (((1,), (1,)), ((), ())), preferred_element_type=F32)


def normed_rows(x, gain):
    floats = x.astype(F32)
    scale = lax.rsqrt(jnp.mean(floats * floats, axis=-1, keepdims=True) + EPS)
    return (floats * scale * gain).astype(BF16)


def call(body, ids, args, in_specs, outs, out_specs=None, grid=(1,), scratch=(), cost=(1e7, 1e6), limit=VMEM_LIMIT):
    whole = pl.BlockSpec(memory_space=pltpu.VMEM)
    flops, nbytes = cost
    return pl.pallas_call(
        body,
        out_shape=outs,
        grid_spec=pltpu.PrefetchScalarGridSpec(
            num_scalar_prefetch=1,
            grid=grid,
            in_specs=[whole if spec is None else spec for spec in in_specs],
            out_specs=[whole] * len(outs) if out_specs is None else out_specs,
            scratch_shapes=list(scratch),
        ),
        compiler_params=pltpu.CompilerParams(
            dimension_semantics=("arbitrary",) * len(grid), vmem_limit_bytes=limit
        ),
        cost_estimate=pl.CostEstimate(flops=int(flops), bytes_accessed=int(nbytes), transcendentals=0),
    )(ids, *args)


K, A, C, Z, PREV = range(5)
USED, LAST = range(2)
SMEM_SPEC = pl.BlockSpec(memory_space=pltpu.SMEM)


def rows_at(start, n):
    return pl.ds(pl.multiple_of(start, n), n)


def halves_kernel(ids, query, out, out_rest, down, q0, q1, o0, o1, o2, o3, d):
    w = q0.shape[1]
    q0[...] = query[:, :w]
    q1[...] = query[:, w:]
    w = o0.shape[1]
    n = o1.shape[0]
    o0[...] = out[:, :w]
    o1[...] = out[:n, w:]
    o2[...] = out[n:, w:]
    o3[...] = out_rest[...]
    d[...] = down[...]


def join_kernel(ids, own, other, o_ref):
    n = own.shape[1]
    k = ids[K]
    o_ref[:, rows_at(k * n, n)] = own[...]
    o_ref[:, rows_at((1 - k) * n, n)] = other[...]


def meta_kernel(ids, mine, other, extra0, extra1, slot_row, slot_col, totals):
    n = mine.shape[1]
    a = ids[A]
    lane = 128
    upper = (
        lax.broadcasted_iota(jnp.int32, (lane, lane), 0) <= lax.broadcasted_iota(jnp.int32, (lane, lane), 1)
    ).astype(F32).astype(BF16)

    def prefix(starts):
        return dot(jnp.broadcast_to(starts, (8, lane)).astype(BF16), upper)[:1]

    row_mine, row_other = mine[...].astype(F32), other[...].astype(F32)
    total_mine, total_other = jnp.sum(row_mine), jnp.sum(row_other)
    base = jnp.zeros((1, 1), F32) + jnp.where(a == 1, total_other, 0.0)
    for j in range(n // lane):
        at = slice(j * lane, (j + 1) * lane)
        sums = prefix(row_mine[:, at]) + base
        slot_row[:, at] = sums.astype(jnp.int32) - 1
        base = sums[:, lane - 1 :]
    own_used = (total_mine + total_other).astype(jnp.int32)
    follow = (extra0[LEAD:, :] + extra1[LEAD:, :])[:1].astype(F32)
    led = prefix(follow[:, :lane])[:, :LEAD]
    leads = (led < 0.5) & (follow[:, lane : lane + 1] > 0.5)
    slot_row[:, n:] = jnp.where(leads, own_used - 1, -1)
    row = lax.broadcasted_iota(jnp.int32, (n, n), 0)
    col = lax.broadcasted_iota(jnp.int32, (n, n), 1)
    slot_col[...] = jnp.sum(jnp.where(row == col, slot_row[:, :n].astype(F32), 0.0), axis=1, keepdims=True).astype(
        jnp.int32
    )
    totals[USED] = own_used
    totals[LAST] = own_used - 1


def qkv_kernel(ids, own, other, extra0, extra1, gain, w_hbm, q_ref, kt_ref, kx_ref, v_ref, wk, wv, normed, wq, sems):
    n, width = own.shape
    half = width // 2
    k = ids[K]
    copies = []
    for part, target in ((1, wk), (2, wv), (0, wq)):
        at = pl.ds(pl.multiple_of(part * width + k * half, half), half)
        copies.append(pltpu.make_async_copy(w_hbm.at[:, at], target, sems.at[part]))
        copies[-1].start()
    normed[rows_at(k * n, n), :] = normed_rows(own[...], gain[...])
    normed[rows_at((1 - k) * n, n), :] = normed_rows(other[...], gain[...])
    normed[2 * n :, :] = normed_rows(extra0[:LEAD, :] + extra1[:LEAD, :], gain[...])
    for copy in copies:
        copy.wait()
    w = 256
    for j in range(half // w):
        at = slice(j * w, (j + 1) * w)
        keys = dot(normed[...], wk[:, at])
        kx_ref[:, at] = keys[2 * n :].astype(BF16)
        kt_ref[at, :] = jnp.transpose(keys[: 2 * n]).astype(BF16)
        v_ref[:, at] = dot(normed[...], wv[:, at]).astype(BF16)
        q_ref[:, at] = (dot(normed[...], wq[:, at]).astype(BF16).astype(F32) * (1.0 / HB**0.5)).astype(BF16)


def window_kernel(ids, own, other, gain, wk, wv, q_ref, kt_ref, kx_ref, v_ref, o_ref, normed, kht, vh):
    n = own.shape[0]
    k = ids[K]
    normed[rows_at(k * n, n), :] = normed_rows(own[...], gain[...])
    normed[rows_at((1 - k) * n, n), :] = normed_rows(other[...], gain[...])
    rows = 2 * n
    n_extra = q_ref.shape[0] - rows
    blk = 128
    lanes = 2 * HB
    nblk = rows // blk
    bias = jnp.where(ids[PREV] == 1, 0.0, NEG).astype(F32)
    low = lax.broadcasted_iota(jnp.int32, (blk, lanes), 1) < HB
    r = lax.broadcasted_iota(jnp.int32, (2 * blk, blk), 0)
    causal = lax.broadcasted_iota(jnp.int32, (2 * blk, blk), 1) <= jnp.where(r >= blk, r - blk, r)
    re = lax.broadcasted_iota(jnp.int32, (2 * n_extra, rows), 0)
    re = jnp.where(re >= n_extra, re - n_extra, re)
    ok_own = lax.broadcasted_iota(jnp.int32, (2 * n_extra, rows), 1) > re
    ok_new = lax.broadcasted_iota(jnp.int32, (2 * n_extra, n_extra), 1) <= re[:, :n_extra]

    def split(qb):
        keep = low[: qb.shape[0]]
        none = jnp.zeros_like(qb)
        return jnp.concatenate([jnp.where(keep, qb, none), jnp.where(keep, none, qb)], axis=0)

    def join(mixed):
        m = mixed.shape[0] // 2
        mixed = mixed[:, :lanes] / mixed[:, lanes:]
        return jnp.where(low[:m], mixed[:m], mixed[m:]).astype(BF16)

    def weighted(e, v):
        return dot(e.astype(BF16), jnp.concatenate([v, jnp.ones_like(v)], axis=1))

    def group(g, _):
        w = kht.shape[0]
        wide = pl.ds(pl.multiple_of(g * w, w), w)
        kht[...] = jnp.transpose(dot(normed[...], wk[:, wide])).astype(BF16)
        vh[...] = dot(normed[...], wv[:, wide]).astype(BF16)
        for pair in range(w // lanes):
            cols = pl.ds(pl.multiple_of(g * w + pair * lanes, lanes), lanes)
            part = slice(pair * lanes, (pair + 1) * lanes)
            for b in range(nblk):
                q2 = split(q_ref[b * blk : (b + 1) * blk, cols])
                s_own = dot(q2, kt_ref[cols, : (b + 1) * blk])
                s_halo = dot(q2, kht[part, b * blk :]) + bias
                diag = jnp.where(causal, s_own[:, b * blk :], s_halo[:, :blk])
                peak = jnp.max(diag, axis=-1, keepdims=True)
                if b > 0:
                    peak = jnp.maximum(peak, jnp.max(s_own[:, : b * blk], axis=-1, keepdims=True))
                if b < nblk - 1:
                    peak = jnp.maximum(peak, jnp.max(s_halo[:, blk:], axis=-1, keepdims=True))
                e_diag = jnp.exp(diag - peak)
                e_own = jnp.where(causal, e_diag, 0.0)
                e_halo = jnp.where(causal, 0.0, e_diag)
                if b > 0:
                    e_own = jnp.concatenate([jnp.exp(s_own[:, : b * blk] - peak), e_own], axis=1)
                if b < nblk - 1:
                    e_halo = jnp.concatenate([e_halo, jnp.exp(s_halo[:, blk:] - peak)], axis=1)
                mixed = weighted(e_own, v_ref[: (b + 1) * blk, cols]) + weighted(e_halo, vh[b * blk :, part])
                o_ref[b * blk : (b + 1) * blk, cols] = join(mixed)
            q2 = split(q_ref[rows:, cols])
            s_own = jnp.where(ok_own, dot(q2, kt_ref[cols, :]), NEG)
            s_new = jnp.where(ok_new, dot_nt(q2, kx_ref[:, cols]), NEG)
            peak = jnp.maximum(jnp.max(s_own, axis=-1, keepdims=True), jnp.max(s_new, axis=-1, keepdims=True))
            mixed = weighted(jnp.exp(s_own - peak), v_ref[:rows, cols]) + weighted(
                jnp.exp(s_new - peak), v_ref[rows:, cols]
            )
            o_ref[rows:, cols] = join(mixed)
        return 0

    lax.fori_loop(0, q_ref.shape[1] // kht.shape[0], group, 0)


def hidden_kernel(ids, ctx_own, ctx_other, w_out, emb_own, emb_other, extra0, extra1, slot, h_ref, p_ref, n_ref, send, acc):
    n = emb_own.shape[0]
    half = acc.shape[1]
    k = ids[K]
    mine = pl.ds(pl.multiple_of(k * half, half), half)
    rest = rows_at((1 - k) * half, half)
    acc[rows_at(k * n, n), :] = emb_own[:, mine].astype(F32)
    acc[rows_at((1 - k) * n, n), :] = emb_other[:, mine].astype(F32)
    acc[2 * n :, :] = (extra0[:LEAD, mine] + extra1[:LEAD, mine]).astype(F32)
    mixed = dot(ctx_own[...], w_out[rows_at(k * half, half), mine]) + dot(ctx_other[...], w_out[rest, mine])
    hidden = (acc[...] + mixed).astype(BF16)
    h_ref[...] = hidden[: 2 * n]
    hot = (lax.broadcasted_iota(jnp.int32, (p_ref.shape[0], acc.shape[0]), 0) == slot[...]).astype(F32)
    count = jnp.broadcast_to(jnp.sum(hot, axis=1, keepdims=True), n_ref.shape)
    part = dot(hot.astype(BF16), hidden)
    p_ref[...] = part
    n_ref[...] = count
    send[:, :half] = part.astype(BF16)
    send[:, half:] = count.astype(BF16)


def pool_kernel(ids, part, count, recv, o_ref):
    half = part.shape[1]
    total = part[...] + recv[:, :half].astype(F32)
    number = count[:, :1] + recv[:, half : half + 1].astype(F32)
    o_ref[...] = (total / jnp.maximum(number, 1.0)).astype(BF16)


def up_kernel(ids, half, other, w_own, w_x, w_z, o_ref, pool):
    n = half.shape[1]
    k, c, z = ids[K], ids[C], ids[Z]
    pool[:, pl.ds(pl.multiple_of(k * n, n), n)] = half[...]
    pool[:, pl.ds(pl.multiple_of((1 - k) * n, n), n)] = other[...]
    rows = w_own.shape[0]
    part = rows // 2
    own = dot(pool[:, pl.ds(pl.multiple_of(c * rows, rows), rows)], w_own[...])
    base = (1 - c) * rows
    at_x = pl.multiple_of(base + z * part, part)
    at_z = pl.multiple_of(base + (1 - z) * part, part)
    total = own + dot(pool[:, pl.ds(at_x, part)], w_x[...]) + dot(pool[:, pl.ds(at_z, part)], w_z[...])
    o_ref[...] = total.astype(BF16)


def kv_kernel(ids, totals, l0, l1, l2, l3, gain, wk, wv, w_x, w_z, s_ref, scale_ref, kv_ref):
    n = l0.shape[1]
    t = ids[A] * 2 + ids[K]
    step = 32

    def rows_step(i, _):
        rows = pl.ds(pl.multiple_of(i * step, step), step)
        square = jnp.zeros((step, 1), F32)
        for j, piece in enumerate((l0, l1, l2, l3)):
            at = pl.multiple_of((t ^ j) * n, n)
            floats = piece[rows, :].astype(F32)
            square = square + jnp.sum(floats * floats, axis=-1, keepdims=True)
            s_ref[rows, pl.ds(at, n)] = (floats * gain[:, pl.ds(at, n)]).astype(BF16)
        scale_ref[rows, :] = jnp.broadcast_to(lax.rsqrt(square / (4 * n) + EPS), (step, scale_ref.shape[1]))
        return 0

    lax.fori_loop(0, l0.shape[0] // step, rows_step, 0)
    scale = scale_ref[:, :1]
    rows = wk.shape[0]
    c, z = ids[C], ids[Z]
    mine = s_ref[:, pl.ds(pl.multiple_of(c * rows, rows), rows)]
    base = (1 - c) * rows
    rest = s_ref[:, rows_at(base, rows)]
    slots = l0.shape[0]
    w = wk.shape[1]
    for parity, key, value in ((0, w_x, w_z), (1, w_z, w_x)):

        @pl.when(z == parity)
        def _(key=key, value=value):
            kv_ref[:slots, :w] = ((dot(mine, wk[...]) + dot(rest, key[...])) * scale).astype(BF16)
            kv_ref[:slots, w:] = ((dot(mine, wv[...]) + dot(rest, value[...])) * scale).astype(BF16)

    count = jnp.zeros((kv_ref.shape[0] - slots, 2 * w), F32) + totals[USED].astype(F32)
    kv_ref[slots:, :] = count.astype(BF16)


def q_kernel(ids, s_ref, scale, w_own, x0, z0, x1, z1, q_ref):
    rows = w_own.shape[0]
    part = rows // 2
    w = x0.shape[1]
    c, z = ids[C], ids[Z]
    base = (1 - c) * rows
    mine = s_ref[:, pl.ds(pl.multiple_of(c * rows, rows), rows)]
    sx = s_ref[:, pl.ds(pl.multiple_of(base + z * part, part), part)]
    sz = s_ref[:, pl.ds(pl.multiple_of(base + (1 - z) * part, part), part)]
    for j, (wx, wz) in enumerate(((x0, z0), (x1, z1))):
        total = dot(mine, w_own[:, j * w : (j + 1) * w]) + dot(sx, wx[...]) + dot(sz, wz[...])
        q_ref[:, j * w : (j + 1) * w] = (total * scale[:, :1]).astype(BF16)


def latent_attend(ids, totals, q_ref, kv_own, kv_other, attn):
    slots = q_ref.shape[0]
    d = HEAD_SIZE
    blk = 128
    scale = 1.0 / HEAD_SIZE**0.5
    col = lax.broadcasted_iota(jnp.int32, (blk, slots), 1)
    row = lax.broadcasted_iota(jnp.int32, (blk, slots), 0)
    used_other = kv_other[slots:, :][:1, :1].astype(F32)
    ok_other = col.astype(F32) < jnp.where(ids[C] == 1, used_other, 0.0)
    ones = jnp.ones((slots, d), BF16)
    v_own = jnp.concatenate([kv_own[:slots, d:], ones], axis=1)
    v_other = jnp.concatenate([kv_other[:slots, d:], ones], axis=1)
    for b in range(slots // blk):
        ok_own = (col <= row + b * blk) & (col < totals[USED])
        for h in range(q_ref.shape[1] // d):
            qh = q_ref[b * blk : (b + 1) * blk, h * d : (h + 1) * d]
            s0 = jnp.where(ok_own, dot_nt(qh, kv_own[:slots, :d]) * scale, NEG)
            s1 = jnp.where(ok_other, dot_nt(qh, kv_other[:slots, :d]) * scale, NEG)
            peak = jnp.maximum(jnp.max(s0, axis=-1, keepdims=True), jnp.max(s1, axis=-1, keepdims=True))
            e0 = jnp.exp(s0 - peak).astype(BF16)
            e1 = jnp.exp(s1 - peak).astype(BF16)
            mixed = dot(e0, v_own) + dot(e1, v_other)
            attn[b * blk : (b + 1) * blk, h * d : (h + 1) * d] = (mixed[:, :d] / mixed[:, d:]).astype(BF16)


def project(ids, attn, w_own, x0, z0, pieces, chip, send, keep):
    w = x0.shape[1]
    part = x0.shape[0]
    k, c, z = ids[K], ids[C], ids[Z]

    def store(j, value):
        @pl.when(k == j)
        def _():
            keep[...] = value.astype(keep.dtype)

        @pl.when(k != j)
        def _():
            send[...] = value.astype(send.dtype)

    @pl.when(chip == c)
    def _():
        for j in range(2):
            store(j, dot(attn[...], w_own[:, j * w : (j + 1) * w]))

    @pl.when(chip != c)
    def _():
        at_x, at_z = z * part, (1 - z) * part
        store(0, dot(attn[:, rows_at(at_x, part)], x0[...]) + dot(attn[:, rows_at(at_z, part)], z0[...]))
        n = part // 2
        total = 0.0
        for at, piece in zip((at_x, at_x + n, at_z + n, at_z), pieces):
            total = total + dot(attn[:, rows_at(at, n)], piece[...])
        store(1, total)


def out_far_kernel(ids, totals, q_ref, kv_own, kv_other, w_own, x0, z0, x1, x2, x3, z1, send, keep, attn):
    latent_attend(ids, totals, q_ref, kv_own, kv_other, attn)
    project(ids, attn, w_own, x0, z0, (x1, x2, x3, z1), 1 - ids[A], send, keep)


def out_near_kernel(ids, attn, w_own, x0, z0, x1, x2, x3, z1, send, keep):
    project(ids, attn, w_own, x0, z0, (x1, x2, x3, z1), ids[A], send, keep)


def far_kernel(ids, keep, recv, o_ref):
    o_ref[...] = (keep[...] + recv[...].astype(F32)).astype(BF16)


def down_kernel(ids, latent, near_keep, near_recv, far_recv, w_own, w_x, w_z, send, keep, lo):
    k, c, z = ids[K], ids[C], ids[Z]
    near = latent[...].astype(F32) + near_keep[...] + near_recv[...].astype(F32)
    lo[...] = (near + far_recv[...].astype(F32)).astype(BF16)
    part = w_x.shape[0]
    own = dot(lo[...], w_own[...])
    rest = dot(lo[:, rows_at(z * part, part)], w_x[...]) + dot(lo[:, rows_at((1 - z) * part, part)], w_z[...])

    @pl.when(c == k)
    def _():
        keep[...] = own
        send[...] = rest.astype(BF16)

    @pl.when(c != k)
    def _():
        keep[...] = rest
        send[...] = own.astype(BF16)


def sum_kernel(ids, totals, keep, recv, full, low, trailing):
    full[...] = keep[...] + recv[...].astype(F32)
    low[...] = full[...].astype(BF16)
    trailing[...] = full[pl.ds(totals[LAST], 1), :].astype(BF16)


def final_kernel(ids, hidden, patch, recv, slot, carry0, carry1, kept, send, states):
    patch_out = (patch[...] + recv[...].astype(F32)).astype(BF16)
    rows = hidden.shape[0]
    n = rows // 2
    hot = lax.broadcasted_iota(jnp.int32, (rows, patch.shape[0]), 1) == slot[...]
    spread = dot(hot.astype(F32).astype(BF16), patch_out)
    carried = (carry0[...].astype(F32) + carry1[...].astype(F32)).astype(BF16).astype(F32)
    lead = (slot[...] < 0).astype(F32)
    states[...] = (hidden[...].astype(F32) + spread + lead * carried).astype(BF16)
    k = ids[K]
    kept[...] = states[rows_at(k * n, n), :]
    send[...] = states[rows_at((1 - k) * n, n), :]


def shape(dims, dtype=BF16):
    return jax.ShapeDtypeStruct(dims, dtype)


def local(
    byte_embed,
    patch_start,
    enc_gain,
    enc_qkv,
    enc_out,
    up_proj,
    lat_gain,
    query_proj,
    key_proj,
    value_matrix,
    out_proj,
    down_proj,
):
    nbytes, width = byte_embed.shape
    n_tp = lax.axis_size("tp")
    n_ctx = lax.axis_size("ctx")
    n_dp = lax.axis_size("dp")
    half = width // 2
    slots = n_tp * nbytes // 4
    t = lax.axis_index("tp")
    c = lax.axis_index("ctx")
    zp = lax.axis_index("dp") % 2
    a, k = t // 2, t % 2
    where_k = lambda first, second: jnp.where(k == 0, first, second)

    def swap(x):
        return lax.ppermute(x, "tp", [(i, i ^ 1) for i in range(n_tp)])

    def cross(x):
        return lax.ppermute(x, "tp", [(i, i ^ 2) for i in range(n_tp)])

    def forward(x):
        n = n_ctx * n_tp
        return lax.ppermute(x, ("ctx", "tp"), [(i, i + 2) for i in range(n - 2)])

    def flip(x):
        return lax.ppermute(x, "ctx", [(0, 1), (1, 0)])

    def pair(x):
        return lax.ppermute(x, "dp", [(i, i ^ 1) for i in range(n_dp)])

    paired = n_ctx == 2

    emb_halo = forward(byte_embed)
    emb_other = swap(byte_embed)
    emb_halo_other = swap(emb_halo)

    starts = patch_start.astype(BF16)
    lane = 128
    note = jnp.concatenate([starts[:lane], jnp.ones((width - lane,), BF16)])
    head = jnp.concatenate([byte_embed[:LEAD], jnp.broadcast_to(note[None, :], (16, width))], axis=0)
    extras = []
    for j in range(2):
        extras.append(
            lax.ppermute(head, ("ctx", "tp"), [(g * n_tp, g * n_tp - 2 + j) for g in range(1, n_ctx)])
        )

    one = lambda x: x.astype(jnp.int32)
    place = jnp.stack([one(k), one(a), one(c), one(zp), one(c * 2 + a > 0)])

    starts = starts.reshape(1, nbytes)
    chip_starts = call(join_kernel, place, (starts, swap(starts)), (None,) * 2, [shape((1, 2 * nbytes))])[0]
    chip_far = cross(chip_starts)
    slot_row, slot_col, totals = call(
        meta_kernel,
        place,
        (chip_starts, chip_far, *extras),
        (None,) * 4,
        [shape((1, 2 * nbytes + LEAD), jnp.int32), shape((2 * nbytes, 1), jnp.int32), shape((2,), jnp.int32)],
        [pl.BlockSpec(memory_space=pltpu.VMEM)] * 2 + [SMEM_SPEC],
    )

    if paired:
        rows = lambda w: w.shape[0] // 2
        part = lambda w: pl.BlockSpec((rows(w), w.shape[1]), lambda p, ids: (ids[Z], 0))
        q_cols, o_cols = query_proj.shape[1] // 2, out_proj.shape[1] // 2
        q_rows, o_rows = rows(query_proj), rows(out_proj)
        sizes = [
            *[(q_rows, q_cols)] * 2,
            (o_rows, o_cols),
            *[(o_rows // 2, o_cols)] * 3,
            (rows(down_proj), down_proj.shape[1]),
        ]

        o_rest = pl.BlockSpec((o_rows // 2, o_cols), lambda p, ids: (2 * (1 - ids[Z]) + 1, 1))
        pieces = [
            jnp.where(zp == 0, key_proj, value_matrix),
            lax.dynamic_slice_in_dim(up_proj, zp * rows(up_proj), rows(up_proj), 0),
        ]
        pieces += call(
            halves_kernel,
            place,
            (query_proj, out_proj, out_proj, down_proj),
            [part(query_proj), part(out_proj), o_rest, part(down_proj)],
            [shape(d) for d in sizes],
            [pl.BlockSpec(d, lambda p, ids: (0, 0)) for d in sizes],
            cost=(1e6, 5e6),
        )
        from_x = [flip(p) for p in pieces]
        from_z = [pair(p) if i not in (6, 7) else None for i, p in enumerate(from_x)]

    gain = enc_gain.reshape(1, width)
    n_rows = 2 * nbytes + LEAD
    q, kt, kx, v, wk, wv = call(
        qkv_kernel,
        place,
        (byte_embed, emb_other, *extras, gain, enc_qkv),
        (None, None, None, None, None, pl.BlockSpec(memory_space=pltpu.HBM)),
        [
            shape((n_rows, half)),
            shape((half, 2 * nbytes)),
            shape((LEAD, half)),
            shape((n_rows, half)),
            shape((width, half)),
            shape((width, half)),
        ],
        scratch=[
            pltpu.VMEM((n_rows, width), BF16),
            pltpu.VMEM((width, half), BF16),
            pltpu.SemaphoreType.DMA((3,)),
        ],
        cost=(2 * n_rows * width * 3 * half, 3e6),
    )
    context = call(
        window_kernel,
        place,
        (emb_halo, emb_halo_other, gain, wk, wv, q, kt, kx, v),
        (None,) * 9,
        [shape((n_rows, half))],
        scratch=[
            pltpu.VMEM((2 * nbytes, width), BF16),
            pltpu.VMEM((256, 2 * nbytes), BF16),
            pltpu.VMEM((2 * nbytes, 256), BF16),
        ],
        cost=(8e9, 6e6),
    )[0]
    context_other = swap(context)
    hidden, part_sum, part_count, part_send = call(
        hidden_kernel,
        place,
        (context, context_other, enc_out, byte_embed, emb_other, *extras, slot_row),
        (None,) * 8,
        [
            shape((2 * nbytes, half)),
            shape((slots, half), F32),
            shape((slots, 128), F32),
            shape((slots, half + 128)),
        ],
        scratch=[pltpu.VMEM((n_rows, half), F32)],
        cost=(1.5e9, 4e6),
    )

    part_recv = cross(part_send)
    pooled = call(pool_kernel, place, (part_sum, part_count, part_recv), (None,) * 3, [shape((slots, half))])[0]
    pooled_other = swap(pooled)

    out_cols = out_proj.shape[1] * n_ctx // n_tp
    lat_cols = up_proj.shape[1]
    if paired:
        latent = call(
            up_kernel,
            place,
            (pooled, pooled_other, up_proj, from_x[1], from_z[1]),
            (None,) * 5,
            [shape((slots, lat_cols))],
            scratch=[pltpu.VMEM((slots, width), BF16)],
            cost=(0.6e9, 4e6),
        )[0]
    else:
        whole = where_k(
            jnp.concatenate([pooled, pooled_other], axis=1), jnp.concatenate([pooled_other, pooled], axis=1)
        )
        latent = dot(whole, lax.all_gather(up_proj, "ctx", axis=0, tiled=True)).astype(BF16)

    l2 = cross(latent)
    l1 = swap(latent)
    l3 = swap(l2)
    heads = query_proj.shape[1] // HEAD_SIZE
    kv_w = key_proj.shape[1]
    if paired:
        scaled, scale, kv = call(
            kv_kernel,
            place,
            (totals, latent, l1, l2, l3, lat_gain.reshape(1, -1), key_proj, value_matrix, from_x[0], from_z[0]),
            (SMEM_SPEC, *(None,) * 9),
            [shape((slots, 4 * lat_cols)), shape((slots, 128), F32), shape((slots + 16, 2 * kv_w))],
            cost=(1e9, 6e6),
        )
        kv_far = flip(kv)
        query = call(
            q_kernel,
            place,
            (scaled, scale, query_proj, from_x[2], from_z[2], from_x[3], from_z[3]),
            (None,) * 7,
            [shape((slots, heads * HEAD_SIZE))],
            cost=(1.2e9, 6e6),
        )[0]
        o_weights = (out_proj, from_x[4], from_z[4], from_x[5], from_x[6], from_x[7], from_z[5])
        far_send, far_keep, attn = call(
            out_far_kernel,
            place,
            (totals, query, kv, kv_far, *o_weights),
            (SMEM_SPEC, *(None,) * 10),
            [shape((slots, out_cols)), shape((slots, out_cols), F32), shape((slots, heads * HEAD_SIZE))],
            cost=(1e9, 3e6),
        )
        near_send, near_keep = call(
            out_near_kernel,
            place,
            (attn, *o_weights),
            (None,) * 8,
            [shape((slots, out_cols)), shape((slots, out_cols), F32)],
            cost=(1e9, 3e6),
        )
    else:
        stacked = jnp.stack([latent, l1, l2, l3])
        lat = jnp.concatenate(
            [lax.dynamic_index_in_dim(stacked, t ^ i, 0, keepdims=False) for i in range(n_tp)], axis=1
        )
        lnorm = normed_rows(lat, lat_gain)
        used = lax.all_gather(totals[:1], "ctx", axis=0, tiled=True)
        rows_iota = jnp.arange(slots, dtype=jnp.int32)
        gather = lambda w, axis: lax.all_gather(w, "ctx", axis=axis, tiled=True)
        query = dot(lnorm, gather(query_proj, 0)).astype(BF16)
        kv = jnp.concatenate([dot(lnorm, gather(key_proj, 0)), dot(lnorm, gather(value_matrix, 0))], axis=1)
        keys = gather(kv.astype(BF16), 0)
        key_rows = jnp.arange(keys.shape[0], dtype=jnp.int32)
        allowed = (key_rows % slots < used[key_rows // slots])[None, :] & (
            key_rows[None, :] <= (c * slots + rows_iota)[:, None]
        )
        qh = jnp.transpose(query.reshape(slots, heads, HEAD_SIZE), (1, 0, 2))
        scores = jnp.einsum("hqd,kd->hqk", qh, keys[:, :kv_w], preferred_element_type=F32) / HEAD_SIZE**0.5
        scores = jnp.where(allowed[None], scores, NEG)
        expo = jnp.where(allowed[None], jnp.exp(scores - jnp.max(scores, axis=-1, keepdims=True)), 0.0)
        total = jnp.sum(expo, axis=-1, keepdims=True)
        mixed = jnp.einsum("hqk,kd->hqd", expo.astype(BF16), keys[:, kv_w:], preferred_element_type=F32) / total
        attn = jnp.transpose(mixed, (1, 0, 2)).reshape(slots, heads * HEAD_SIZE).astype(BF16)
        full = dot(attn, gather(out_proj, 1))
        pick = lambda j: lax.dynamic_slice_in_dim(full, (t ^ j) * out_cols, out_cols, 1)
        near_keep, near_send, far_keep, far_send = pick(0), pick(1).astype(BF16), pick(2), pick(3).astype(BF16)

    far = call(far_kernel, place, (far_keep, swap(far_send)), (None,) * 2, [shape((slots, out_cols))])[0]
    far_recv = cross(far)
    near_recv = swap(near_send)
    if paired:
        down_send, down_keep = call(
            down_kernel,
            place,
            (latent, near_keep, near_recv, far_recv, down_proj, from_x[8], from_z[8]),
            (None,) * 7,
            [shape((slots, half)), shape((slots, half), F32)],
            scratch=[pltpu.VMEM((slots, lat_cols), BF16)],
            cost=(0.6e9, 4e6),
        )
    else:
        base = latent.astype(F32) + near_keep + near_recv.astype(F32)
        latent_out = (base + far_recv.astype(F32)).astype(BF16)
        full = dot(latent_out, gather(down_proj, 1))
        down_keep = lax.dynamic_slice_in_dim(full, k * half, half, 1)
        down_send = lax.dynamic_slice_in_dim(full, (1 - k) * half, half, 1).astype(BF16)

    chip_sum, chip_low, trailing = call(
        sum_kernel,
        place,
        (totals, down_keep, swap(down_send)),
        (SMEM_SPEC, None, None),
        [shape((slots, half), F32), shape((slots, half)), shape((1, half))],
    )
    sum_recv = cross(chip_low)
    ahead = lambda at: [(g * n_tp + at * 2 + j, (g + 1) * n_tp + j) for g in range(n_ctx - 1) for j in range(2)]
    carry0 = lax.ppermute(trailing, ("ctx", "tp"), ahead(0))
    carry1 = lax.ppermute(trailing, ("ctx", "tp"), ahead(1))
    kept, send = call(
        final_kernel,
        place,
        (hidden, chip_sum, sum_recv, slot_col, carry0, carry1),
        (None,) * 6,
        [shape((nbytes, half))] * 2,
        scratch=[pltpu.VMEM((2 * nbytes, half), BF16)],
        cost=(0.4e9, 3e6),
    )
    got = swap(send)
    return where_k(jnp.concatenate([kept, got], axis=1), jnp.concatenate([got, kept], axis=1))


def solution(mesh):
    placed = (
        P(("dp", "ctx", "tp"), None),
        P(("dp", "ctx", "tp")),
        P(),
        P(),
        P(),
        P("ctx", "tp"),
        P(),
        P("ctx", "tp"),
        P("ctx", "tp"),
        P("ctx", "tp"),
        P("tp", "ctx"),
        P("tp", "ctx"),
    )

    return jax.shard_map(local, mesh=mesh, in_specs=placed, out_specs=P(("dp", "ctx", "tp"), None), check_vma=False)
```

profile of v0, /device:TPU:2, one launch (start us, length us, event | category | flops | bytes accessed | tf_op | source)
XLA Modules:
  0.0 194.1 jit_solution(5817321697408089477)
XLA Ops:
  0.0 3.4 %collective-permute-start = (bf16[256,1024]{1,0:T(8,128)(2,1)}, bf16[256,1024]{1,0:T(8,128)(2,1)S(1)}, u32[]{:S(2)}, u32[]{:S(2)}) collective-permute-start(bf16[256,1024]{1,0:T(8,128)(2,1)} %emb_own.1), channel_id=1, source_target_pairs={{0,8},{4,12},{8,16},{12,20},{16,24},{20,28},{1,9},{5,13},{9,17},{1... | collective-permute-start | bytes 1572872 | tf_op jit(solution)/shard_map/ppermute | solution.py:449
  3.5 13.2 %collective-permute-done.own = bf16[256,1024]{1,0:T(8,128)(2,1)S(1)} collective-permute-done((bf16[256,1024]{1,0:T(8,128)(2,1)}, bf16[256,1024]{1,0:T(8,128)(2,1)S(1)}, u32[]{:S(2)}, u32[]{:S(2)}) %collective-permute-start) | collective-permute-done | bytes 524320 | tf_op jit(solution)/shard_map/ppermute | solution.py:449
  18.2 2.5 %collective-permute-start.3 = (bf16[48,1024]{1,0:T(8,128)(2,1)S(1)}, bf16[48,1024]{1,0:T(8,128)(2,1)S(1)}, u32[]{:S(2)}, u32[]{:S(2)}) collective-permute-start(bf16[48,1024]{1,0:T(8,128)(2,1)S(1)} %pad_maximum_fusion), channel_id=1, source_target_pairs={{16,8},{17,9},{18,10},{19,11}} | collective-permute-start | bytes 294920 | tf_op jit(solution)/shard_map/ppermute | solution.py:470
  20.7 1.3 collective-permute-start.4
  22.9 1.3 collective-permute-done.4.extra1
  24.2 2.8 %copy-done.3 = bf16[1024,3072]{1,0:T(8,128)(2,1)S(1)} copy-done((bf16[1024,3072]{1,0:T(8,128)(2,1)S(1)}, bf16[1024,3072]{1,0:T(8,128)(2,1)}, u32[]{:S(2)}) %copy-start.3) | copy-done | bytes 6291480
  28.7 3.3 %shard_map.118 = (bf16[544,512]{1,0:T(8,128)(2,1)S(1)}, bf16[512,512]{1,0:T(8,128)(2,1)S(1)}, bf16[32,512]{1,0:T(8,128)(2,1)S(1)}, bf16[544,512]{1,0:T(8,128)(2,...) custom-call(s32[5]{0:T(128)S(1)} %stack.27.ids, bf16[256,1024]{1,0:T(8,128)(2,1)S(1)} %copy-done.9, ...), custom_call_target="tpu_custom_call" | custom-call | flops 1711276032 | bytes 3000000 | tf_op jit(solution)/shard_map/pallas_call | solution.py:36
  33.9 7.9 %shard_map.119.ctx_own = bf16[544,512]{1,0:T(8,128)(2,1)S(1)} custom-call(s32[5]{0:T(128)S(1)} %stack.27.ids, bf16[256,1024]{1,0:T(8,128)(2,1)S(1)} %collective-permute-done.own, bf16[256,1024]{1,0:T(8,128)(2,1)S(1)} %copy-done.23, f32[1,1024]{1,0:T(1,128)S(1)} %bitcast.10, bf16[1024,512]{1,0:T(8,128)(2,1)S(1)} %get-tuple-element.40.wk, ...), custom_call_target="tpu_custom_call" | custom-call | flops 8000000000 | bytes 6000000 | tf_op jit(solution)/shard_map/pallas_call | solution.py:36
  44.6 3.6 %collective-permute-start.7 = (bf16[1,512]{1,0:T(2,128)(2,1)S(1)}, bf16[1,512]{1,0:T(2,128)(2,1)S(1)}, u32[]{:S(2)}, u32[]{:S(2)}) collective-permute-start(bf16[1,512]{1,0:T(2,128)(2,1)S(1)} %shard_map.120.mine), channel_id=1, source_target_pairs={{0,8},{4,12},{8,0},{12,4},{1,9},{5,13},{9,1},{13,5},{2,10},{6,14},... | collective-permute-start | bytes 3080 | tf_op jit(solution)/shard_map/ppermute | solution.py:445
  48.1 1.6 collective-permute-done.7.other
  51.7 1.6 copy-done.21
  53.3 2.3 %shard_map.122 = (bf16[512,512]{1,0:T(8,128)(2,1)S(1)}, f32[256,512]{1,0:T(8,128)S(1)}, f32[256,128]{1,0:T(8,128)S(1)}, bf16[256,640]{1,0:T(8,128)(2,1)}) custom-call(s32[5]{0:T(128)S(1)} %stack.27.ids, bf16[544,512]{1,0:T(8,128)(2,1)S(1)} %shard_map.119.ctx_own, bf16[544,512]{1,0:T(8,128)(2,1)S(1)} %collective-permute-done.5.ctx_other, ...), custom_call_target="tpu_custom_call" | custom-call | flops 1500000000 | bytes 4000000 | tf_op jit(solution)/shard_map/pallas_call | solution.py:36
  57.8 2.0 %collective-permute-start.8 = (bf16[256,640]{1,0:T(8,128)(2,1)}, bf16[256,640]{1,0:T(8,128)(2,1)S(1)}, u32[]{:S(2)}, u32[]{:S(2)}) collective-permute-start(bf16[256,640]{1,0:T(8,128)(2,1)} %get-tuple-element.51), channel_id=1, source_target_pairs={{0,8},{4,12},{8,0},{12,4},{1,9},{5,13},{9,1},{13,5},{2,10},{6,14},... | collective-permute-start | bytes 983048 | tf_op jit(solution)/shard_map/ppermute | solution.py:445
  59.9 1.6 collective-permute-start.11
  61.4 5.9 %collective-permute-done.8.recv = bf16[256,640]{1,0:T(8,128)(2,1)S(1)} collective-permute-done((bf16[256,640]{1,0:T(8,128)(2,1)}, bf16[256,640]{1,0:T(8,128)(2,1)S(1)}, u32[]{:S(2)}, u32[]{:S(2)}) %collective-permute-start.8) | collective-permute-done | bytes 327712 | tf_op jit(solution)/shard_map/ppermute | solution.py:445
  71.4 1.6 copy-done.1
  73.7 2.0 %collective-permute-start.24 = (bf16[128,1024]{1,0:T(8,128)(2,1)S(1)}, bf16[128,1024]{1,0:T(8,128)(2,1)S(1)}, u32[]{:S(2)}, u32[]{:S(2)}) collective-permute-start(bf16[128,1024]{1,0:T(8,128)(2,1)S(1)} %get-tuple-element.58), channel_id=1, source_target_pairs={{0,16},{16,0},{1,17},{17,1},{2,18},{18,2},{3,19},{19,3},{4,20},{20... | collective-permute-start | bytes 786440 | tf_op jit(solution)/shard_map/ppermute | solution.py:452
  75.8 1.9 collective-permute-start.19
  77.7 2.3 %shard_map.124.l0.latent = bf16[256,1024]{1,0:T(8,128)(2,1)S(1)} custom-call(s32[5]{0:T(128)S(1)} %stack.27.ids, bf16[256,512]{1,0:T(8,128)(2,1)S(1)} %shard_map.123.half, bf16[256,512]{1,0:T(8,128)(2,1)S(1)} %collective-permute-done.9.other, bf16[512,1024]{1,0:T(8,128)(2,1)S(1)} %copy-done.6, bf16[256,1024]{1,0:T(8,128)(2,1)} %collective-permute-done.10.w_x, ...), custom_call_target="tpu_custom_call" | custom-call | flops 600000000 | bytes 4000000 | tf_op jit(solution)/shard_map/pallas_call | solution.py:36
  80.1 1.8 collective-permute-start.13
  81.9 9.8 %collective-permute-done.24.x1 = bf16[128,1024]{1,0:T(8,128)(2,1)S(1)} collective-permute-done((bf16[128,1024]{1,0:T(8,128)(2,1)S(1)}, bf16[128,1024]{1,0:T(8,128)(2,1)S(1)}, u32[]{:S(2)}, u32[]{:S(2)}) %collective-permute-start.24) | collective-permute-done | bytes 262176 | tf_op jit(solution)/shard_map/ppermute | solution.py:452
  91.8 1.6 collective-permute-start.16
  93.4 9.5 %collective-permute-done.17.x0 = bf16[1024,256]{1,0:T(8,128)(2,1)S(1)} collective-permute-done((bf16[1024,256]{1,0:T(8,128)(2,1)S(1)}, bf16[1024,256]{1,0:T(8,128)(2,1)S(1)}, u32[]{:S(2)}, u32[]{:S(2)}) %collective-permute-start.17) | collective-permute-done | bytes 524320 | tf_op jit(solution)/shard_map/ppermute | solution.py:452
  102.9 1.6 collective-permute-start.18
  104.5 9.7 %collective-permute-done.19.x1 = bf16[1024,256]{1,0:T(8,128)(2,1)S(1)} collective-permute-done((bf16[1024,256]{1,0:T(8,128)(2,1)S(1)}, bf16[1024,256]{1,0:T(8,128)(2,1)S(1)}, u32[]{:S(2)}, u32[]{:S(2)}) %collective-permute-start.19) | collective-permute-done | bytes 524320 | tf_op jit(solution)/shard_map/ppermute | solution.py:452
  114.6 10.2 %collective-permute-done.22.x0 = bf16[256,1024]{1,0:T(8,128)(2,1)S(1)} collective-permute-done((bf16[256,1024]{1,0:T(8,128)(2,1)S(1)}, bf16[256,1024]{1,0:T(8,128)(2,1)S(1)}, u32[]{:S(2)}, u32[]{:S(2)}) %collective-permute-start.22) | collective-permute-done | bytes 524320 | tf_op jit(solution)/shard_map/ppermute | solution.py:452
  124.9 1.6 collective-permute-start.20
  127.2 1.7 collective-permute-start.26
  128.9 1.6 collective-permute-start.27
  130.5 4.0 %shard_map.125 = (bf16[256,4096]{1,0:T(8,128)(2,1)S(1)}, f32[256,128]{1,0:T(8,128)S(1)}, bf16[272,256]{1,0:T(8,128)(2,1)S(1)}) custom-call(s32[5]{0:T(128)S(1)} %stack.27.ids, s32[2]{0:T(128)S(1)} %get-tuple-element.48.totals, bf16[256,1024]{1,0:T(8,128)(2,1)S(1)} %shard_map.124.l0.latent, bf16[256,1024]{1,0:T(8,128)(2,1)S(1)} %collective-permute-done.12.l1, ...), custom_call_target="tpu_custom_call" | custom-call | flops 1000000000 | bytes 6000000 | tf_op jit(solution)/shard_map/pallas_call | solution.py:36
  134.5 5.2 %collective-permute-done.20.z1 = bf16[1024,256]{1,0:T(8,128)(2,1)S(1)} collective-permute-done((bf16[1024,256]{1,0:T(8,128)(2,1)S(1)}, bf16[1024,256]{1,0:T(8,128)(2,1)S(1)}, u32[]{:S(2)}, u32[]{:S(2)}) %collective-permute-start.20) | collective-permute-done | bytes 524320 | tf_op jit(solution)/shard_map/ppermute | solution.py:455
  140.0 1.8 shard_map.127.q_ref
  141.8 1.8 collective-permute-start.31
  143.6 11.6 %collective-permute-done.27.z1 = bf16[128,1024]{1,0:T(8,128)(2,1)S(1)} collective-permute-done((bf16[128,1024]{1,0:T(8,128)(2,1)S(1)}, bf16[128,1024]{1,0:T(8,128)(2,1)S(1)}, u32[]{:S(2)}, u32[]{:S(2)}) %collective-permute-start.27) | collective-permute-done | bytes 262176 | tf_op jit(solution)/shard_map/ppermute | solution.py:455
  155.2 3.1 %shard_map.128 = (bf16[256,1024]{1,0:T(8,128)(2,1)S(1)}, f32[256,1024]{1,0:T(8,128)S(1)}, bf16[256,512]{1,0:T(8,128)(2,1)S(1)}) custom-call(s32[5]{0:T(128)S(1)} %stack.27.ids, s32[2]{0:T(128)S(1)} %get-tuple-element.48.totals, bf16[256,512]{1,0:T(8,128)(2,1)S(1)} %shard_map.127.q_ref, bf16[272,256]{1,0:T(8,128)(2,1)S(1)} %get-tuple-element.56.kv_own, ...), custom_call_target="tpu_custom_call" | custom-call | flops 1000000000 | bytes 3000000 | tf_op jit(solution)/shard_map/pallas_call | solution.py:36
  158.4 1.6 collective-permute-start.32
  160.0 1.8 shard_map.129
  162.7 1.8 collective-permute-start.30
  164.5 8.2 %collective-permute-done.32.w_z = bf16[512,512]{1,0:T(8,128)(2,1)S(1)} collective-permute-done((bf16[512,512]{1,0:T(8,128)(2,1)S(1)}, bf16[512,512]{1,0:T(8,128)(2,1)S(1)}, u32[]{:S(2)}, u32[]{:S(2)}) %collective-permute-start.32) | collective-permute-done | bytes 524320 | tf_op jit(solution)/shard_map/ppermute | solution.py:455
  172.7 4.2 %collective-permute-done.30.far_recv = bf16[256,1024]{1,0:T(8,128)(2,1)S(1)} collective-permute-done((bf16[256,1024]{1,0:T(8,128)(2,1)S(1)}, bf16[256,1024]{1,0:T(8,128)(2,1)S(1)}, u32[]{:S(2)}, u32[]{:S(2)}) %collective-permute-start.30) | collective-permute-done | bytes 524320 | tf_op jit(solution)/shard_map/ppermute | solution.py:445
  176.9 1.4 shard_map.131
  178.4 1.5 collective-permute-done.33.recv
  181.1 1.8 collective-permute-start.34
  182.9 1.3 collective-permute-start.35
  184.2 1.3 collective-permute-start.36
  185.5 2.9 %collective-permute-done.35.carry0 = bf16[1,512]{1,0:T(2,128)(2,1)S(1)} collective-permute-done((bf16[1,512]{1,0:T(2,128)(2,1)S(1)}, bf16[1,512]{1,0:T(2,128)(2,1)S(1)}, u32[]{:S(2)}, u32[]{:S(2)}) %collective-permute-start.35) | collective-permute-done | bytes 1056 | tf_op jit(solution)/shard_map/ppermute | solution.py:686
  188.4 2.2 %collective-permute-done.36.carry1 = bf16[1,512]{1,0:T(2,128)(2,1)S(1)} collective-permute-done((bf16[1,512]{1,0:T(2,128)(2,1)S(1)}, bf16[1,512]{1,0:T(2,128)(2,1)S(1)}, u32[]{:S(2)}, u32[]{:S(2)}) %collective-permute-start.36) | collective-permute-done | bytes 1056 | tf_op jit(solution)/shard_map/ppermute | solution.py:687
  191.6 1.5 collective-permute-done.37
  (102 shorter events, 23.8 us)
Async XLA Ops:
  0.0 16.7 %collective-permute-start = (bf16[256,1024]{1,0:T(8,128)(2,1)}, bf16[256,1024]{1,0:T(8,128)(2,1)S(1)}, u32[]{:S(2)}, u32[]{:S(2)}) collective-permute-start(bf16[256,1024]{1,0:T(8,128)(2,1)} %emb_own.1), channel_id=1, source_target_pairs={{0,8},{4,12},{8,16},{12,20},{16,24},{20,28},{1,9},{5,13},{9,17},{1... | collective-permute-start | bytes 1572872 | tf_op jit(solution)/shard_map/ppermute | solution.py:449
  3.4 20.8 %collective-permute-start.2 = (bf16[256,1024]{1,0:T(8,128)(2,1)}, bf16[256,1024]{1,0:T(8,128)(2,1)S(1)}, u32[]{:S(2)}, u32[]{:S(2)}) collective-permute-start(bf16[256,1024]{1,0:T(8,128)(2,1)} %emb_own.1), channel_id=1, source_target_pairs={{0,4},{4,0},{8,12},{12,8},{1,5},{5,1},{9,13},{13,9},{2,6},{6,2},{1... | collective-permute-start | bytes 1572872 | tf_op jit(solution)/shard_map/ppermute | solution.py:442
  16.7 15.4 %collective-permute-start.1 = (bf16[256,1024]{1,0:T(8,128)(2,1)S(1)}, bf16[256,1024]{1,0:T(8,128)(2,1)S(1)}, u32[]{:S(2)}, u32[]{:S(2)}) collective-permute-start(bf16[256,1024]{1,0:T(8,128)(2,1)S(1)} %collective-permute-done.own), channel_id=1, source_target_pairs={{0,4},{4,0},{8,12},{12,8},{1,5},{5,1},{9,13},{13,9},{2,6},{6,2},{1... | collective-permute-start | bytes 1572872 | tf_op jit(solution)/shard_map/ppermute | solution.py:442
  18.2 4.7 %collective-permute-start.3 = (bf16[48,1024]{1,0:T(8,128)(2,1)S(1)}, bf16[48,1024]{1,0:T(8,128)(2,1)S(1)}, u32[]{:S(2)}, u32[]{:S(2)}) collective-permute-start(bf16[48,1024]{1,0:T(8,128)(2,1)S(1)} %pad_maximum_fusion), channel_id=1, source_target_pairs={{16,8},{17,9},{18,10},{19,11}} | collective-permute-start | bytes 294920 | tf_op jit(solution)/shard_map/ppermute | solution.py:470
  20.7 3.5 %collective-permute-start.4 = (bf16[48,1024]{1,0:T(8,128)(2,1)S(1)}, bf16[48,1024]{1,0:T(8,128)(2,1)S(1)}, u32[]{:S(2)}, u32[]{:S(2)}) collective-permute-start(bf16[48,1024]{1,0:T(8,128)(2,1)S(1)} %pad_maximum_fusion), channel_id=1, source_target_pairs={{16,12},{17,13},{18,14},{19,15}} | collective-permute-start | bytes 294920 | tf_op jit(solution)/shard_map/ppermute | solution.py:470
  33.9 8.0 %copy-start.5 = (bf16[512,1024]{1,0:T(8,128)(2,1)S(1)}, bf16[512,1024]{1,0:T(8,128)(2,1)}, u32[]{:S(2)}) copy-start(bf16[512,1024]{1,0:T(8,128)(2,1)} %w_own.5) | copy-start | bytes 3145732
  33.9 17.8 %copy-start.10 = (bf16[256,1024]{1,0:T(8,128)(2,1)S(1)}, bf16[256,1024]{1,0:T(8,128)(2,1)}, u32[]{:S(2)}) copy-start(bf16[256,1024]{1,0:T(8,128)(2,1)} %emb_own.1) | copy-start | bytes 1572868
  41.8 9.9 %collective-permute-start.5 = (bf16[544,512]{1,0:T(8,128)(2,1)S(1)}, bf16[544,512]{1,0:T(8,128)(2,1)S(1)}, u32[]{:S(2)}, u32[]{:S(2)}) collective-permute-start(bf16[544,512]{1,0:T(8,128)(2,1)S(1)} %shard_map.119.ctx_own), channel_id=1, source_target_pairs={{0,4},{4,0},{8,12},{12,8},{1,5},{5,1},{9,13},{13,9},{2,6},{6,2},{1... | collective-permute-start | bytes 1671176 | tf_op jit(solution)/shard_map/ppermute | solution.py:442
  42.7 17.2 %collective-permute-start.10 = (bf16[256,1024]{1,0:T(8,128)(2,1)}, bf16[256,1024]{1,0:T(8,128)(2,1)}, u32[]{:S(2)}, u32[]{:S(2)}) collective-permute-start(bf16[256,1024]{1,0:T(8,128)(2,1)} %constant_dynamic-slice_fusion), channel_id=1, source_target_pairs={{0,16},{16,0},{1,17},{17,1},{2,18},{18,2},{3,19},{19,3},{4,20},{20... | collective-permute-start | bytes 1572872 | tf_op jit(solution)/shard_map/ppermute | solution.py:452
  42.7 1.3 collective-permute-start.6
  44.6 5.2 %collective-permute-start.7 = (bf16[1,512]{1,0:T(2,128)(2,1)S(1)}, bf16[1,512]{1,0:T(2,128)(2,1)S(1)}, u32[]{:S(2)}, u32[]{:S(2)}) collective-permute-start(bf16[1,512]{1,0:T(2,128)(2,1)S(1)} %shard_map.120.mine), channel_id=1, source_target_pairs={{0,8},{4,12},{8,0},{12,4},{1,9},{5,13},{9,1},{13,5},{2,10},{6,14},... | collective-permute-start | bytes 3080 | tf_op jit(solution)/shard_map/ppermute | solution.py:445
  53.3 18.1 %copy-start.4 = (bf16[1024,512]{1,0:T(8,128)(2,1)S(1)}, bf16[1024,512]{1,0:T(8,128)(2,1)}, u32[]{:S(2)}) copy-start(bf16[1024,512]{1,0:T(8,128)(2,1)} %w_own.9) | copy-start | bytes 3145732
  57.8 13.5 %copy-start = (bf16[512,2048]{1,0:T(8,128)(2,1)S(1)}, bf16[512,2048]{1,0:T(8,128)(2,1)}, u32[]{:S(2)}) copy-start(bf16[512,2048]{1,0:T(8,128)(2,1)} %w_own.8) | copy-start | bytes 6291460
  57.8 9.5 %collective-permute-start.8 = (bf16[256,640]{1,0:T(8,128)(2,1)}, bf16[256,640]{1,0:T(8,128)(2,1)S(1)}, u32[]{:S(2)}, u32[]{:S(2)}) collective-permute-start(bf16[256,640]{1,0:T(8,128)(2,1)} %get-tuple-element.51), channel_id=1, source_target_pairs={{0,8},{4,12},{8,0},{12,4},{1,9},{5,13},{9,1},{13,5},{2,10},{6,14},... | collective-permute-start | bytes 983048 | tf_op jit(solution)/shard_map/ppermute | solution.py:445
  59.9 16.0 %collective-permute-start.11 = (bf16[256,1024]{1,0:T(8,128)(2,1)}, bf16[256,1024]{1,0:T(8,128)(2,1)S(1)}, u32[]{:S(2)}, u32[]{:S(2)}) collective-permute-start(bf16[256,1024]{1,0:T(8,128)(2,1)} %collective-permute-done.10.w_x), channel_id=1, source_target_pairs={{0,1},{1,0},{2,3},{3,2},{4,5},{5,4},{6,7},{7,6},{8,9},{9,8},{10,11... | collective-permute-start | bytes 1572872 | tf_op jit(solution)/shard_map/ppermute | solution.py:455
  70.0 7.8 %collective-permute-start.9 = (bf16[256,512]{1,0:T(8,128)(2,1)S(1)}, bf16[256,512]{1,0:T(8,128)(2,1)S(1)}, u32[]{:S(2)}, u32[]{:S(2)}) collective-permute-start(bf16[256,512]{1,0:T(8,128)(2,1)S(1)} %shard_map.123.half), channel_id=1, source_target_pairs={{0,4},{4,0},{8,12},{12,8},{1,5},{5,1},{9,13},{13,9},{2,6},{6,2},{1... | collective-permute-start | bytes 786440 | tf_op jit(solution)/shard_map/ppermute | solution.py:442
  71.2 20.6 %collective-permute-start.15 = (bf16[2048,128]{1,0:T(8,128)(2,1)S(1)}, bf16[2048,128]{1,0:T(8,128)(2,1)S(1)}, u32[]{:S(2)}, u32[]{:S(2)}) collective-permute-start(bf16[2048,128]{1,0:T(8,128)(2,1)S(1)} %broadcast_select_fusion), channel_id=1, source_target_pairs={{0,16},{16,0},{1,17},{17,1},{2,18},{18,2},{3,19},{19,3},{4,20},{20... | collective-permute-start | bytes 1572872 | tf_op jit(solution)/shard_map/ppermute | solution.py:452
  73.7 56.8 %copy-start.7 = (bf16[2048,128]{1,0:T(8,128)(2,1)S(1)}, bf16[2048,128]{1,0:T(8,128)(2,1)}, u32[]{:S(2)}) copy-start(bf16[2048,128]{1,0:T(8,128)(2,1)} %wk.1) | copy-start | bytes 1572868
  73.7 56.8 %copy-start.8 = (bf16[2048,128]{1,0:T(8,128)(2,1)S(1)}, bf16[2048,128]{1,0:T(8,128)(2,1)}, u32[]{:S(2)}) copy-start(bf16[2048,128]{1,0:T(8,128)(2,1)} %wv.1) | copy-start | bytes 1572868
  73.7 56.8 %copy-start.19 = (f32[4096]{0:T(1024)S(1)}, f32[4096]{0:T(1024)}, u32[]{:S(2)}) copy-start(f32[4096]{0:T(1024)} %param.18) | copy-start | bytes 49156
  73.7 17.9 %collective-permute-start.24 = (bf16[128,1024]{1,0:T(8,128)(2,1)S(1)}, bf16[128,1024]{1,0:T(8,128)(2,1)S(1)}, u32[]{:S(2)}, u32[]{:S(2)}) collective-permute-start(bf16[128,1024]{1,0:T(8,128)(2,1)S(1)} %get-tuple-element.58), channel_id=1, source_target_pairs={{0,16},{16,0},{1,17},{17,1},{2,18},{18,2},{3,19},{19,3},{4,20},{20... | collective-permute-start | bytes 786440 | tf_op jit(solution)/shard_map/ppermute | solution.py:452
  75.7 27.2 %collective-permute-start.17 = (bf16[1024,256]{1,0:T(8,128)(2,1)S(1)}, bf16[1024,256]{1,0:T(8,128)(2,1)S(1)}, u32[]{:S(2)}, u32[]{:S(2)}) collective-permute-start(bf16[1024,256]{1,0:T(8,128)(2,1)S(1)} %get-tuple-element.54), channel_id=1, source_target_pairs={{0,16},{16,0},{1,17},{17,1},{2,18},{18,2},{3,19},{19,3},{4,20},{20... | collective-permute-start | bytes 1572872 | tf_op jit(solution)/shard_map/ppermute | solution.py:452
  75.8 38.3 %collective-permute-start.19 = (bf16[1024,256]{1,0:T(8,128)(2,1)S(1)}, bf16[1024,256]{1,0:T(8,128)(2,1)S(1)}, u32[]{:S(2)}, u32[]{:S(2)}) collective-permute-start(bf16[1024,256]{1,0:T(8,128)(2,1)S(1)} %get-tuple-element.55), channel_id=1, source_target_pairs={{0,16},{16,0},{1,17},{17,1},{2,18},{18,2},{3,19},{19,3},{4,20},{20... | collective-permute-start | bytes 1572872 | tf_op jit(solution)/shard_map/ppermute | solution.py:452
  80.1 34.1 %collective-permute-start.13 = (bf16[256,1024]{1,0:T(8,128)(2,1)S(1)}, bf16[256,1024]{1,0:T(8,128)(2,1)S(1)}, u32[]{:S(2)}, u32[]{:S(2)}) collective-permute-start(bf16[256,1024]{1,0:T(8,128)(2,1)S(1)} %shard_map.124.l0.latent), channel_id=1, source_target_pairs={{0,8},{4,12},{8,0},{12,4},{1,9},{5,13},{9,1},{13,5},{2,10},{6,14},... | collective-permute-start | bytes 1572872 | tf_op jit(solution)/shard_map/ppermute | solution.py:445
  91.6 33.2 %collective-permute-start.22 = (bf16[256,1024]{1,0:T(8,128)(2,1)S(1)}, bf16[256,1024]{1,0:T(8,128)(2,1)S(1)}, u32[]{:S(2)}, u32[]{:S(2)}) collective-permute-start(bf16[256,1024]{1,0:T(8,128)(2,1)S(1)} %get-tuple-element.57), channel_id=1, source_target_pairs={{0,16},{16,0},{1,17},{17,1},{2,18},{18,2},{3,19},{19,3},{4,20},{20... | collective-permute-start | bytes 1572872 | tf_op jit(solution)/shard_map/ppermute | solution.py:452
  91.8 34.7 %collective-permute-start.16 = (bf16[2048,128]{1,0:T(8,128)(2,1)S(1)}, bf16[2048,128]{1,0:T(8,128)(2,1)S(1)}, u32[]{:S(2)}, u32[]{:S(2)}) collective-permute-start(bf16[2048,128]{1,0:T(8,128)(2,1)S(1)} %collective-permute-done.15.w_x), channel_id=1, source_target_pairs={{0,1},{1,0},{2,3},{3,2},{4,5},{5,4},{6,7},{7,6},{8,9},{9,8},{10,11... | collective-permute-start | bytes 1572872 | tf_op jit(solution)/shard_map/ppermute | solution.py:455
  102.9 24.0 %collective-permute-start.18 = (bf16[1024,256]{1,0:T(8,128)(2,1)S(1)}, bf16[1024,256]{1,0:T(8,128)(2,1)S(1)}, u32[]{:S(2)}, u32[]{:S(2)}) collective-permute-start(bf16[1024,256]{1,0:T(8,128)(2,1)S(1)} %collective-permute-done.17.x0), channel_id=1, source_target_pairs={{0,1},{1,0},{2,3},{3,2},{4,5},{5,4},{6,7},{7,6},{8,9},{9,8},{10,11... | collective-permute-start | bytes 1572872 | tf_op jit(solution)/shard_map/ppermute | solution.py:455
  114.1 13.1 %collective-permute-start.12 = (bf16[256,1024]{1,0:T(8,128)(2,1)S(1)}, bf16[256,1024]{1,0:T(8,128)(2,1)S(1)}, u32[]{:S(2)}, u32[]{:S(2)}) collective-permute-start(bf16[256,1024]{1,0:T(8,128)(2,1)S(1)} %shard_map.124.l0.latent), channel_id=1, source_target_pairs={{0,4},{4,0},{8,12},{12,8},{1,5},{5,1},{9,13},{13,9},{2,6},{6,2},{1... | collective-permute-start | bytes 1572872 | tf_op jit(solution)/shard_map/ppermute | solution.py:442
  114.1 14.8 %collective-permute-start.14 = (bf16[256,1024]{1,0:T(8,128)(2,1)S(1)}, bf16[256,1024]{1,0:T(8,128)(2,1)S(1)}, u32[]{:S(2)}, u32[]{:S(2)}) collective-permute-start(bf16[256,1024]{1,0:T(8,128)(2,1)S(1)} %collective-permute-done.13.l2), channel_id=1, source_target_pairs={{0,4},{4,0},{8,12},{12,8},{1,5},{5,1},{9,13},{13,9},{2,6},{6,2},{1... | collective-permute-start | bytes 1572872 | tf_op jit(solution)/shard_map/ppermute | solution.py:442
  124.9 14.8 %collective-permute-start.20 = (bf16[1024,256]{1,0:T(8,128)(2,1)S(1)}, bf16[1024,256]{1,0:T(8,128)(2,1)S(1)}, u32[]{:S(2)}, u32[]{:S(2)}) collective-permute-start(bf16[1024,256]{1,0:T(8,128)(2,1)S(1)} %collective-permute-done.19.x1), channel_id=1, source_target_pairs={{0,1},{1,0},{2,3},{3,2},{4,5},{5,4},{6,7},{7,6},{8,9},{9,8},{10,11... | collective-permute-start | bytes 1572872 | tf_op jit(solution)/shard_map/ppermute | solution.py:455
  126.5 28.7 %collective-permute-start.23 = (bf16[256,1024]{1,0:T(8,128)(2,1)S(1)}, bf16[256,1024]{1,0:T(8,128)(2,1)S(1)}, u32[]{:S(2)}, u32[]{:S(2)}) collective-permute-start(bf16[256,1024]{1,0:T(8,128)(2,1)S(1)} %collective-permute-done.22.x0), channel_id=1, source_target_pairs={{0,1},{1,0},{2,3},{3,2},{4,5},{5,4},{6,7},{7,6},{8,9},{9,8},{10,11... | collective-permute-start | bytes 1572872 | tf_op jit(solution)/shard_map/ppermute | solution.py:455
  126.9 14.8 %collective-permute-start.25 = (bf16[128,1024]{1,0:T(8,128)(2,1)S(1)}, bf16[128,1024]{1,0:T(8,128)(2,1)S(1)}, u32[]{:S(2)}, u32[]{:S(2)}) collective-permute-start(bf16[128,1024]{1,0:T(8,128)(2,1)S(1)} %get-tuple-element.59), channel_id=1, source_target_pairs={{0,16},{16,0},{1,17},{17,1},{2,18},{18,2},{3,19},{19,3},{4,20},{20... | collective-permute-start | bytes 786440 | tf_op jit(solution)/shard_map/ppermute | solution.py:452
  127.2 16.4 %collective-permute-start.26 = (bf16[128,1024]{1,0:T(8,128)(2,1)S(1)}, bf16[128,1024]{1,0:T(8,128)(2,1)S(1)}, u32[]{:S(2)}, u32[]{:S(2)}) collective-permute-start(bf16[128,1024]{1,0:T(8,128)(2,1)S(1)} %get-tuple-element.60), channel_id=1, source_target_pairs={{0,16},{16,0},{1,17},{17,1},{2,18},{18,2},{3,19},{19,3},{4,20},{20... | collective-permute-start | bytes 786440 | tf_op jit(solution)/shard_map/ppermute | solution.py:452
  128.9 26.2 %collective-permute-start.27 = (bf16[128,1024]{1,0:T(8,128)(2,1)S(1)}, bf16[128,1024]{1,0:T(8,128)(2,1)S(1)}, u32[]{:S(2)}, u32[]{:S(2)}) collective-permute-start(bf16[128,1024]{1,0:T(8,128)(2,1)S(1)} %collective-permute-done.24.x1), channel_id=1, source_target_pairs={{0,1},{1,0},{2,3},{3,2},{4,5},{5,4},{6,7},{7,6},{8,9},{9,8},{10,11... | collective-permute-start | bytes 786440 | tf_op jit(solution)/shard_map/ppermute | solution.py:455
  130.5 9.4 %copy-start.2 = (bf16[2048,512]{1,0:T(8,128)(2,1)S(1)}, bf16[2048,512]{1,0:T(8,128)(2,1)}, u32[]{:S(2)}) copy-start(bf16[2048,512]{1,0:T(8,128)(2,1)} %w_own.6) | copy-start | bytes 6291460
  139.7 15.5 %collective-permute-start.21 = (bf16[272,256]{1,0:T(8,128)(2,1)S(1)}, bf16[272,256]{1,0:T(8,128)(2,1)S(1)}, u32[]{:S(2)}, u32[]{:S(2)}) collective-permute-start(bf16[272,256]{1,0:T(8,128)(2,1)S(1)} %get-tuple-element.56.kv_own), channel_id=1, source_target_pairs={{0,16},{16,0},{1,17},{17,1},{2,18},{18,2},{3,19},{19,3},{4,20},{20... | collective-permute-start | bytes 417800 | tf_op jit(solution)/shard_map/ppermute | solution.py:452
  141.8 16.6 %collective-permute-start.31 = (bf16[512,512]{1,0:T(8,128)(2,1)S(1)}, bf16[512,512]{1,0:T(8,128)(2,1)S(1)}, u32[]{:S(2)}, u32[]{:S(2)}) collective-permute-start(bf16[512,512]{1,0:T(8,128)(2,1)S(1)} %get-tuple-element.66), channel_id=1, source_target_pairs={{0,16},{16,0},{1,17},{17,1},{2,18},{18,2},{3,19},{19,3},{4,20},{20... | collective-permute-start | bytes 1572872 | tf_op jit(solution)/shard_map/ppermute | solution.py:452
  158.3 3.7 %collective-permute-start.29 = (bf16[256,1024]{1,0:T(8,128)(2,1)S(1)}, bf16[256,1024]{1,0:T(8,128)(2,1)S(1)}, u32[]{:S(2)}, u32[]{:S(2)}) collective-permute-start(bf16[256,1024]{1,0:T(8,128)(2,1)S(1)} %get-tuple-element.65), channel_id=1, source_target_pairs={{0,4},{4,0},{8,12},{12,8},{1,5},{5,1},{9,13},{13,9},{2,6},{6,2},{1... | collective-permute-start | bytes 1572872 | tf_op jit(solution)/shard_map/ppermute | solution.py:442
  158.4 14.3 %collective-permute-start.32 = (bf16[512,512]{1,0:T(8,128)(2,1)S(1)}, bf16[512,512]{1,0:T(8,128)(2,1)S(1)}, u32[]{:S(2)}, u32[]{:S(2)}) collective-permute-start(bf16[512,512]{1,0:T(8,128)(2,1)S(1)} %collective-permute-done.31.w_x), channel_id=1, source_target_pairs={{0,1},{1,0},{2,3},{3,2},{4,5},{5,4},{6,7},{7,6},{8,9},{9,8},{10,11... | collective-permute-start | bytes 1572872 | tf_op jit(solution)/shard_map/ppermute | solution.py:455
  161.8 10.9 %collective-permute-start.28 = (bf16[256,1024]{1,0:T(8,128)(2,1)S(1)}, bf16[256,1024]{1,0:T(8,128)(2,1)S(1)}, u32[]{:S(2)}, u32[]{:S(2)}) collective-permute-start(bf16[256,1024]{1,0:T(8,128)(2,1)S(1)} %get-tuple-element.63), channel_id=1, source_target_pairs={{0,4},{4,0},{8,12},{12,8},{1,5},{5,1},{9,13},{13,9},{2,6},{6,2},{1... | collective-permute-start | bytes 1572872 | tf_op jit(solution)/shard_map/ppermute | solution.py:442
  162.7 14.3 %collective-permute-start.30 = (bf16[256,1024]{1,0:T(8,128)(2,1)S(1)}, bf16[256,1024]{1,0:T(8,128)(2,1)S(1)}, u32[]{:S(2)}, u32[]{:S(2)}) collective-permute-start(bf16[256,1024]{1,0:T(8,128)(2,1)S(1)} %shard_map.130), channel_id=1, source_target_pairs={{0,8},{4,12},{8,0},{12,4},{1,9},{5,13},{9,1},{13,5},{2,10},{6,14},... | collective-permute-start | bytes 1572872 | tf_op jit(solution)/shard_map/ppermute | solution.py:445
  176.9 13.7 %copy-start.12 = (bf16[512,512]{1,0:T(8,128)(2,1)S(1)}, bf16[512,512]{1,0:T(8,128)(2,1)}, u32[]{:S(2)}) copy-start(bf16[512,512]{1,0:T(8,128)(2,1)} %copy-done.11) | copy-start | bytes 1572868
  176.9 13.7 %copy-start.16 = (s32[512,1]{1,0:T(8,128)S(1)}, s32[512,1]{1,0:T(8,128)}, u32[]{:S(2)}) copy-start(s32[512,1]{1,0:T(8,128)} %copy-done.15) | copy-start | bytes 6148
  178.3 1.6 collective-permute-start.33
  181.1 9.5 %collective-permute-start.34 = (bf16[256,512]{1,0:T(8,128)(2,1)S(1)}, bf16[256,512]{1,0:T(8,128)(2,1)S(1)}, u32[]{:S(2)}, u32[]{:S(2)}) collective-permute-start(bf16[256,512]{1,0:T(8,128)(2,1)S(1)} %get-tuple-element.70), channel_id=1, source_target_pairs={{0,8},{4,12},{8,0},{12,4},{1,9},{5,13},{9,1},{13,5},{2,10},{6,14},... | collective-permute-start | bytes 786440 | tf_op jit(solution)/shard_map/ppermute | solution.py:445
  182.9 5.5 %collective-permute-start.35 = (bf16[1,512]{1,0:T(2,128)(2,1)S(1)}, bf16[1,512]{1,0:T(2,128)(2,1)S(1)}, u32[]{:S(2)}, u32[]{:S(2)}) collective-permute-start(bf16[1,512]{1,0:T(2,128)(2,1)S(1)} %get-tuple-element.72), channel_id=1, source_target_pairs={{0,16},{4,20},{1,17},{5,21},{2,18},{6,22},{3,19},{7,23}} | collective-permute-start | bytes 3080 | tf_op jit(solution)/shard_map/ppermute | solution.py:686
  184.2 6.4 %collective-permute-start.36 = (bf16[1,512]{1,0:T(2,128)(2,1)S(1)}, bf16[1,512]{1,0:T(2,128)(2,1)S(1)}, u32[]{:S(2)}, u32[]{:S(2)}) collective-permute-start(bf16[1,512]{1,0:T(2,128)(2,1)S(1)} %get-tuple-element.72), channel_id=1, source_target_pairs={{8,16},{12,20},{9,17},{13,21},{10,18},{14,22},{11,19},{15,23}} | collective-permute-start | bytes 3080 | tf_op jit(solution)/shard_map/ppermute | solution.py:687
  191.5 1.6 collective-permute-start.37
  (14 other events, 19.2 us)
where the time goes:
time: 195 us; the launch traced here: 194 us
  waiting for transfers between devices  100 us (51%)
  starting transfers between devices  40.8 us (21%)
  Pallas kernels  33.8 us (17%)
  local copies, waits for them, and re-layouts  16.2 us (8%)
  other arithmetic  2.73 us (1%)
    ppermute x10, waiting for transfers between devices, flip(): return lax.ppermute(x, 'ctx', [(0, 1), (1, 0)])  39.2 us
    pallas_call x16, Pallas kernels, call(): pl.pallas_call(body, out_shape=outs, grid_spec=pltpu.PrefetchScalarGridSp...  33.8 us
    ppermute x7, waiting for transfers between devices, pair(): return lax.ppermute(x, 'dp', [(i, i ^ 1) for i in range(n_dp)])  25 us
    unnamed x48, local copies, waits for them, and re-layouts  14.5 us
    ppermute x1, waiting for transfers between devices, forward(): return lax.ppermute(x, ('ctx', 'tp'), [(i, i + 2) for i in range(n - 2)])  13.2 us
    ppermute x5, waiting for transfers between devices, cross(): return lax.ppermute(x, 'tp', [(i, i ^ 2) for i in range(n_tp)])  11.7 us
    ppermute x5, starting transfers between devices, cross(): return lax.ppermute(x, 'tp', [(i, i ^ 2) for i in range(n_tp)])  11 us
    ppermute x7, starting transfers between devices, pair(): return lax.ppermute(x, 'dp', [(i, i ^ 1) for i in range(n_dp)])  9.98 us
  transfers between devices with their start and end apart: 38, of which 18 were waited for; matrix products, arithmetic and copies ran while one was open for 2% of the time, Pallas kernels for 12%

commit v1 on v0

--- a/solution.py
+++ b/solution.py
@@ -1,3 +1,5 @@
+import functools
+
 import jax
 import jax.numpy as jnp
 from jax import lax
@@ -59,7 +61,25 @@
     return pl.ds(pl.multiple_of(start, n), n)
 
 
-def halves_kernel(ids, query, out, out_rest, down, q0, q1, o0, o1, o2, o3, d):
+def first_kernel(ids, emb, starts, key, value, up, head, starts_out, kv_out, up_out):
+    n, lane = LEAD, 128
+    floats = starts[...].astype(F32)
+    starts_out[...] = floats.astype(BF16)
+    head[:n, :] = emb[...]
+    head[n:, :] = jnp.ones((head.shape[0] - n, head.shape[1]), BF16)
+    head[n:, :lane] = jnp.broadcast_to(floats[:, :lane], (head.shape[0] - n, lane)).astype(BF16)
+    up_out[...] = up[...]
+
+    @pl.when(ids[Z] == 0)
+    def _():
+        kv_out[...] = key[...]
+
+    @pl.when(ids[Z] != 0)
+    def _():
+        kv_out[...] = value[...]
+
+
+def halves_kernel(ids, query, out, out_rest, down, q0, q1, o0, o1, o2, o3, d0, d1):
     w = q0.shape[1]
     q0[...] = query[:, :w]
     q1[...] = query[:, w:]
@@ -69,7 +89,9 @@
     o1[...] = out[:n, w:]
     o2[...] = out[n:, w:]
     o3[...] = out_rest[...]
-    d[...] = down[...]
+    n = d0.shape[0]
+    d0[...] = down[:n]
+    d1[...] = down[n:]
 
 
 def join_kernel(ids, own, other, o_ref):
@@ -136,11 +158,15 @@
         q_ref[:, at] = (dot(normed[...], wq[:, at]).astype(BF16).astype(F32) * (1.0 / HB**0.5)).astype(BF16)
 
 
-def window_kernel(ids, own, other, gain, wk, wv, q_ref, kt_ref, kx_ref, v_ref, o_ref, normed, kht, vh):
+def halo_kernel(ids, own, other, gain, normed):
     n = own.shape[0]
     k = ids[K]
     normed[rows_at(k * n, n), :] = normed_rows(own[...], gain[...])
     normed[rows_at((1 - k) * n, n), :] = normed_rows(other[...], gain[...])
+
+
+def window_kernel(ids, normed, wk, wv, q_ref, kt_ref, kx_ref, v_ref, o_ref, kht, vh, *, g):
+    n = normed.shape[0] // 2
     rows = 2 * n
     n_extra = q_ref.shape[0] - rows
     blk = 128
@@ -168,56 +194,54 @@
     def weighted(e, v):
         return dot(e.astype(BF16), jnp.concatenate([v, jnp.ones_like(v)], axis=1))
 
-    def group(g, _):
-        w = kht.shape[0]
-        wide = pl.ds(pl.multiple_of(g * w, w), w)
-        kht[...] = jnp.transpose(dot(normed[...], wk[:, wide])).astype(BF16)
-        vh[...] = dot(normed[...], wv[:, wide]).astype(BF16)
-        for pair in range(w // lanes):
-            cols = pl.ds(pl.multiple_of(g * w + pair * lanes, lanes), lanes)
-            part = slice(pair * lanes, (pair + 1) * lanes)
-            for b in range(nblk):
-                q2 = split(q_ref[b * blk : (b + 1) * blk, cols])
-                s_own = dot(q2, kt_ref[cols, : (b + 1) * blk])
-                s_halo = dot(q2, kht[part, b * blk :]) + bias
-                diag = jnp.where(causal, s_own[:, b * blk :], s_halo[:, :blk])
-                peak = jnp.max(diag, axis=-1, keepdims=True)
-                if b > 0:
-                    peak = jnp.maximum(peak, jnp.max(s_own[:, : b * blk], axis=-1, keepdims=True))
-                if b < nblk - 1:
-                    peak = jnp.maximum(peak, jnp.max(s_halo[:, blk:], axis=-1, keepdims=True))
-                e_diag = jnp.exp(diag - peak)
-                e_own = jnp.where(causal, e_diag, 0.0)
-                e_halo = jnp.where(causal, 0.0, e_diag)
-                if b > 0:
-                    e_own = jnp.concatenate([jnp.exp(s_own[:, : b * blk] - peak), e_own], axis=1)
-                if b < nblk - 1:
-                    e_halo = jnp.concatenate([e_halo, jnp.exp(s_halo[:, blk:] - peak)], axis=1)
-                mixed = weighted(e_own, v_ref[: (b + 1) * blk, cols]) + weighted(e_halo, vh[b * blk :, part])
-                o_ref[b * blk : (b + 1) * blk, cols] = join(mixed)
-            q2 = split(q_ref[rows:, cols])
-            s_own = jnp.where(ok_own, dot(q2, kt_ref[cols, :]), NEG)
-            s_new = jnp.where(ok_new, dot_nt(q2, kx_ref[:, cols]), NEG)
-            peak = jnp.maximum(jnp.max(s_own, axis=-1, keepdims=True), jnp.max(s_new, axis=-1, keepdims=True))
-            mixed = weighted(jnp.exp(s_own - peak), v_ref[:rows, cols]) + weighted(
-                jnp.exp(s_new - peak), v_ref[rows:, cols]
-            )
-            o_ref[rows:, cols] = join(mixed)
-        return 0
-
-    lax.fori_loop(0, q_ref.shape[1] // kht.shape[0], group, 0)
-
-
-def hidden_kernel(ids, ctx_own, ctx_other, w_out, emb_own, emb_other, extra0, extra1, slot, h_ref, p_ref, n_ref, send, acc):
+    w = kht.shape[0]
+    wide = slice(g * w, (g + 1) * w)
+    kht[...] = jnp.transpose(dot(normed[...], wk[:, wide])).astype(BF16)
+    vh[...] = dot(normed[...], wv[:, wide]).astype(BF16)
+    for pair in range(w // lanes):
+        cols = slice(g * w + pair * lanes, g * w + (pair + 1) * lanes)
+        part = slice(pair * lanes, (pair + 1) * lanes)
+        for b in range(nblk):
+            q2 = split(q_ref[b * blk : (b + 1) * blk, cols])
+            s_own = dot(q2, kt_ref[cols, : (b + 1) * blk])
+            s_halo = dot(q2, kht[part, b * blk :]) + bias
+            diag = jnp.where(causal, s_own[:, b * blk :], s_halo[:, :blk])
+            peak = jnp.max(diag, axis=-1, keepdims=True)
+            if b > 0:
+                peak = jnp.maximum(peak, jnp.max(s_own[:, : b * blk], axis=-1, keepdims=True))
+            if b < nblk - 1:
+                peak = jnp.maximum(peak, jnp.max(s_halo[:, blk:], axis=-1, keepdims=True))
+            e_diag = jnp.exp(diag - peak)
+            e_own = jnp.where(causal, e_diag, 0.0)
+            e_halo = jnp.where(causal, 0.0, e_diag)
+            if b > 0:
+                e_own = jnp.concatenate([jnp.exp(s_own[:, : b * blk] - peak), e_own], axis=1)
+            if b < nblk - 1:
+                e_halo = jnp.concatenate([e_halo, jnp.exp(s_halo[:, blk:] - peak)], axis=1)
+            mixed = weighted(e_own, v_ref[: (b + 1) * blk, cols]) + weighted(e_halo, vh[b * blk :, part])
+            o_ref[b * blk : (b + 1) * blk, part] = join(mixed)
+        q2 = split(q_ref[rows:, cols])
+        s_own = jnp.where(ok_own, dot(q2, kt_ref[cols, :]), NEG)
+        s_new = jnp.where(ok_new, dot_nt(q2, kx_ref[:, cols]), NEG)
+        peak = jnp.maximum(jnp.max(s_own, axis=-1, keepdims=True), jnp.max(s_new, axis=-1, keepdims=True))
+        mixed = weighted(jnp.exp(s_own - peak), v_ref[:rows, cols]) + weighted(
+            jnp.exp(s_new - peak), v_ref[rows:, cols]
+        )
+        o_ref[rows:, part] = join(mixed)
+
+
+def hidden_kernel(ids, own0, own1, other0, other1, w_out, emb_own, emb_other, extra0, extra1, slot, h_ref, p_ref, n_ref, send, acc):
     n = emb_own.shape[0]
     half = acc.shape[1]
     k = ids[K]
     mine = pl.ds(pl.multiple_of(k * half, half), half)
-    rest = rows_at((1 - k) * half, half)
     acc[rows_at(k * n, n), :] = emb_own[:, mine].astype(F32)
     acc[rows_at((1 - k) * n, n), :] = emb_other[:, mine].astype(F32)
     acc[2 * n :, :] = (extra0[:LEAD, mine] + extra1[:LEAD, mine]).astype(F32)
-    mixed = dot(ctx_own[...], w_out[rows_at(k * half, half), mine]) + dot(ctx_other[...], w_out[rest, mine])
+    w = own0.shape[1]
+    mixed = 0.0
+    for at, shift, piece in ((k, 0, own0), (k, w, own1), (1 - k, 0, other0), (1 - k, w, other1)):
+        mixed = mixed + dot(piece[...], w_out[rows_at(at * half + shift, w), mine])
     hidden = (acc[...] + mixed).astype(BF16)
     h_ref[...] = hidden[: 2 * n]
     hot = (lax.broadcasted_iota(jnp.int32, (p_ref.shape[0], acc.shape[0]), 0) == slot[...]).astype(F32)
@@ -326,10 +350,49 @@
             attn[b * blk : (b + 1) * blk, h * d : (h + 1) * d] = (mixed[:, :d] / mixed[:, d:]).astype(BF16)
 
 
-def project(ids, attn, w_own, x0, z0, pieces, chip, send, keep):
-    w = x0.shape[1]
-    part = x0.shape[0]
-    k, c, z = ids[K], ids[C], ids[Z]
+def blocks_of(attn, w_own, x0, z0, pieces, chip, c, z, store, which):
+    w, part = x0.shape[1], x0.shape[0]
+
+    @pl.when(chip == c)
+    def _():
+        for j in which:
+            store(j, dot(attn[...], w_own[:, j * w : (j + 1) * w]))
+
+    @pl.when(chip != c)
+    def _():
+        at_x, at_z = z * part, (1 - z) * part
+        if 0 in which:
+            store(0, dot(attn[:, rows_at(at_x, part)], x0[...]) + dot(attn[:, rows_at(at_z, part)], z0[...]))
+        if 1 in which:
+            n = part // 2
+            total = 0.0
+            for at, piece in zip((at_x, at_x + n, at_z + n, at_z), pieces):
+                total = total + dot(attn[:, rows_at(at, n)], piece[...])
+            store(1, total)
+
+
+def attend_kernel(ids, totals, q_ref, kv_own, kv_other, attn):
+    latent_attend(ids, totals, q_ref, kv_own, kv_other, attn)
+
+
+def far0_kernel(ids, attn, w_own, x0, z0, full, low):
+    def store(j, value):
+        full[...] = value
+        low[...] = value.astype(BF16)
+
+    blocks_of(attn, w_own, x0, z0, (), 1 - ids[A], ids[C], ids[Z], store, (0,))
+
+
+def far1_kernel(ids, attn, w_own, x0, x1, x2, x3, z1, full, low):
+    def store(j, value):
+        full[...] = value
+        low[...] = value.astype(BF16)
+
+    blocks_of(attn, w_own, x0, None, (x1, x2, x3, z1), 1 - ids[A], ids[C], ids[Z], store, (1,))
+
+
+def near_kernel(ids, attn, w_own, x0, z0, x1, x2, x3, z1, send, keep):
+    k = ids[K]
 
     def store(j, value):
         @pl.when(k == j)
@@ -340,42 +403,24 @@
         def _():
             send[...] = value.astype(send.dtype)
 
-    @pl.when(chip == c)
-    def _():
-        for j in range(2):
-            store(j, dot(attn[...], w_own[:, j * w : (j + 1) * w]))
-
-    @pl.when(chip != c)
-    def _():
-        at_x, at_z = z * part, (1 - z) * part
-        store(0, dot(attn[:, rows_at(at_x, part)], x0[...]) + dot(attn[:, rows_at(at_z, part)], z0[...]))
-        n = part // 2
-        total = 0.0
-        for at, piece in zip((at_x, at_x + n, at_z + n, at_z), pieces):
-            total = total + dot(attn[:, rows_at(at, n)], piece[...])
-        store(1, total)
-
-
-def out_far_kernel(ids, totals, q_ref, kv_own, kv_other, w_own, x0, z0, x1, x2, x3, z1, send, keep, attn):
-    latent_attend(ids, totals, q_ref, kv_own, kv_other, attn)
-    project(ids, attn, w_own, x0, z0, (x1, x2, x3, z1), 1 - ids[A], send, keep)
-
-
-def out_near_kernel(ids, attn, w_own, x0, z0, x1, x2, x3, z1, send, keep):
-    project(ids, attn, w_own, x0, z0, (x1, x2, x3, z1), ids[A], send, keep)
+    blocks_of(attn, w_own, x0, z0, (x1, x2, x3, z1), ids[A], ids[C], ids[Z], store, (0, 1))
 
 
 def far_kernel(ids, keep, recv, o_ref):
     o_ref[...] = (keep[...] + recv[...].astype(F32)).astype(BF16)
 
 
-def down_kernel(ids, latent, near_keep, near_recv, far_recv, w_own, w_x, w_z, send, keep, lo):
+def down_kernel(ids, latent, near_keep, near_recv, far0, far1, w_own, x0, x1, z0, z1, send, keep, lo):
     k, c, z = ids[K], ids[C], ids[Z]
     near = latent[...].astype(F32) + near_keep[...] + near_recv[...].astype(F32)
-    lo[...] = (near + far_recv[...].astype(F32)).astype(BF16)
-    part = w_x.shape[0]
+    lo[...] = (near + far0[...].astype(F32) + far1[...].astype(F32)).astype(BF16)
+    n = x0.shape[0]
+    part = 2 * n
     own = dot(lo[...], w_own[...])
-    rest = dot(lo[:, rows_at(z * part, part)], w_x[...]) + dot(lo[:, rows_at((1 - z) * part, part)], w_z[...])
+    at_x, at_z = z * part, (1 - z) * part
+    rest = 0.0
+    for at, piece in ((at_x, x0), (at_x + n, x1), (at_z, z0), (at_z + n, z1)):
+        rest = rest + dot(lo[:, rows_at(at, n)], piece[...])
 
     @pl.when(c == k)
     def _():
@@ -460,20 +505,34 @@
     emb_other = swap(byte_embed)
     emb_halo_other = swap(emb_halo)
 
-    starts = patch_start.astype(BF16)
-    lane = 128
-    note = jnp.concatenate([starts[:lane], jnp.ones((width - lane,), BF16)])
-    head = jnp.concatenate([byte_embed[:LEAD], jnp.broadcast_to(note[None, :], (16, width))], axis=0)
+    one = lambda x: x.astype(jnp.int32)
+    place = jnp.stack([one(k), one(a), one(c), one(zp), one(c * 2 + a > 0)])
+
+    in_hbm = lambda x: pltpu.with_memory_space_constraint(x, pltpu.HBM)
+
+    up_rows = up_proj.shape[0] // 2
+    block_of = lambda rows, cols, at: pl.BlockSpec((rows, cols), lambda p, ids: (at(ids), 0))
+    origin = lambda ids: 0
+    head, starts, kv_piece, up_piece = call(
+        first_kernel,
+        place,
+        (in_hbm(byte_embed), in_hbm(patch_start.reshape(1, nbytes)), in_hbm(key_proj), in_hbm(value_matrix), in_hbm(up_proj)),
+        [
+            block_of(LEAD, width, origin),
+            block_of(1, nbytes, origin),
+            block_of(*key_proj.shape, origin),
+            block_of(*value_matrix.shape, origin),
+            block_of(up_rows, up_proj.shape[1], lambda ids: ids[Z]),
+        ],
+        [shape((LEAD + 16, width)), shape((1, nbytes)), shape(key_proj.shape), shape((up_rows, up_proj.shape[1]))],
+        cost=(1e6, 3e6),
+    )
     extras = []
     for j in range(2):
         extras.append(
             lax.ppermute(head, ("ctx", "tp"), [(g * n_tp, g * n_tp - 2 + j) for g in range(1, n_ctx)])
         )
 
-    one = lambda x: x.astype(jnp.int32)
-    place = jnp.stack([one(k), one(a), one(c), one(zp), one(c * 2 + a > 0)])
-
-    starts = starts.reshape(1, nbytes)
     chip_starts = call(join_kernel, place, (starts, swap(starts)), (None,) * 2, [shape((1, 2 * nbytes))])[0]
     chip_far = cross(chip_starts)
     slot_row, slot_col, totals = call(
@@ -494,14 +553,11 @@
             *[(q_rows, q_cols)] * 2,
             (o_rows, o_cols),
             *[(o_rows // 2, o_cols)] * 3,
-            (rows(down_proj), down_proj.shape[1]),
+            *[(rows(down_proj) // 2, down_proj.shape[1])] * 2,
         ]
 
         o_rest = pl.BlockSpec((o_rows // 2, o_cols), lambda p, ids: (2 * (1 - ids[Z]) + 1, 1))
-        pieces = [
-            jnp.where(zp == 0, key_proj, value_matrix),
-            lax.dynamic_slice_in_dim(up_proj, zp * rows(up_proj), rows(up_proj), 0),
-        ]
+        pieces = [up_piece, kv_piece]
         pieces += call(
             halves_kernel,
             place,
@@ -519,7 +575,7 @@
     q, kt, kx, v, wk, wv = call(
         qkv_kernel,
         place,
-        (byte_embed, emb_other, *extras, gain, enc_qkv),
+        (byte_embed, emb_other, *extras, gain, in_hbm(enc_qkv)),
         (None, None, None, None, None, pl.BlockSpec(memory_space=pltpu.HBM)),
         [
             shape((n_rows, half)),
@@ -536,25 +592,28 @@
         ],
         cost=(2 * n_rows * width * 3 * half, 3e6),
     )
-    context = call(
-        window_kernel,
-        place,
-        (emb_halo, emb_halo_other, gain, wk, wv, q, kt, kx, v),
-        (None,) * 9,
-        [shape((n_rows, half))],
-        scratch=[
-            pltpu.VMEM((2 * nbytes, width), BF16),
-            pltpu.VMEM((256, 2 * nbytes), BF16),
-            pltpu.VMEM((2 * nbytes, 256), BF16),
-        ],
-        cost=(8e9, 6e6),
+    normed = call(
+        halo_kernel, place, (emb_halo, emb_halo_other, gain), (None,) * 3, [shape((2 * nbytes, width))], cost=(1e7, 2e6)
     )[0]
-    context_other = swap(context)
+    context, context_other = [], []
+    for g in range(half // 256):
+        context.append(
+            call(
+                functools.partial(window_kernel, g=g),
+                place,
+                (normed, wk, wv, q, kt, kx, v),
+                (None,) * 7,
+                [shape((n_rows, 256))],
+                scratch=[pltpu.VMEM((256, 2 * nbytes), BF16), pltpu.VMEM((2 * nbytes, 256), BF16)],
+                cost=(4e9, 3e6),
+            )[0]
+        )
+        context_other.append(swap(context[-1]))
     hidden, part_sum, part_count, part_send = call(
         hidden_kernel,
         place,
-        (context, context_other, enc_out, byte_embed, emb_other, *extras, slot_row),
-        (None,) * 8,
+        (*context, *context_other, enc_out, byte_embed, emb_other, *extras, slot_row),
+        (None,) * 10,
         [
             shape((2 * nbytes, half)),
             shape((slots, half), F32),
@@ -575,7 +634,7 @@
         latent = call(
             up_kernel,
             place,
-            (pooled, pooled_other, up_proj, from_x[1], from_z[1]),
+            (pooled, pooled_other, up_proj, from_x[0], from_z[0]),
             (None,) * 5,
             [shape((slots, lat_cols))],
             scratch=[pltpu.VMEM((slots, width), BF16)],
@@ -596,7 +655,7 @@
         scaled, scale, kv = call(
             kv_kernel,
             place,
-            (totals, latent, l1, l2, l3, lat_gain.reshape(1, -1), key_proj, value_matrix, from_x[0], from_z[0]),
+            (totals, latent, l1, l2, l3, lat_gain.reshape(1, -1), key_proj, value_matrix, from_x[1], from_z[1]),
             (SMEM_SPEC, *(None,) * 9),
             [shape((slots, 4 * lat_cols)), shape((slots, 128), F32), shape((slots + 16, 2 * kv_w))],
             cost=(1e9, 6e6),
@@ -610,19 +669,22 @@
             [shape((slots, heads * HEAD_SIZE))],
             cost=(1.2e9, 6e6),
         )[0]
-        o_weights = (out_proj, from_x[4], from_z[4], from_x[5], from_x[6], from_x[7], from_z[5])
-        far_send, far_keep, attn = call(
-            out_far_kernel,
+        attn = call(
+            attend_kernel,
             place,
-            (totals, query, kv, kv_far, *o_weights),
-            (SMEM_SPEC, *(None,) * 10),
-            [shape((slots, out_cols)), shape((slots, out_cols), F32), shape((slots, heads * HEAD_SIZE))],
-            cost=(1e9, 3e6),
-        )
+            (totals, query, kv, kv_far),
+            (SMEM_SPEC, None, None, None),
+            [shape((slots, heads * HEAD_SIZE))],
+            cost=(5e8, 1e6),
+        )[0]
+        o1 = (from_x[5], from_x[6], from_x[7], from_z[5])
+        block_out = [shape((slots, out_cols), F32), shape((slots, out_cols))]
+        far0 = call(far0_kernel, place, (attn, out_proj, from_x[4], from_z[4]), (None,) * 4, block_out, cost=(3e8, 2e6))
+        far1 = call(far1_kernel, place, (attn, out_proj, from_x[4], *o1), (None,) * 7, block_out, cost=(3e8, 2e6))
         near_send, near_keep = call(
-            out_near_kernel,
+            near_kernel,
             place,
-            (attn, *o_weights),
+            (attn, out_proj, from_x[4], from_z[4], *o1),
             (None,) * 8,
             [shape((slots, out_cols)), shape((slots, out_cols), F32)],
             cost=(1e9, 3e6),
@@ -652,24 +714,29 @@
         attn = jnp.transpose(mixed, (1, 0, 2)).reshape(slots, heads * HEAD_SIZE).astype(BF16)
         full = dot(attn, gather(out_proj, 1))
         pick = lambda j: lax.dynamic_slice_in_dim(full, (t ^ j) * out_cols, out_cols, 1)
-        near_keep, near_send, far_keep, far_send = pick(0), pick(1).astype(BF16), pick(2), pick(3).astype(BF16)
-
-    far = call(far_kernel, place, (far_keep, swap(far_send)), (None,) * 2, [shape((slots, out_cols))])[0]
-    far_recv = cross(far)
+        near_keep, near_send = pick(0), pick(1).astype(BF16)
+        far_block = lambda j: lax.dynamic_slice_in_dim(full, (2 * (1 - a) + j) * out_cols, out_cols, 1)
+        far0, far1 = [(far_block(j), far_block(j).astype(BF16)) for j in range(2)]
+
+    far_recv = []
+    for j, (full_block, low_block) in enumerate((far0, far1)):
+        got = lax.ppermute(low_block, "tp", [(i ^ 1, i) for i in range(n_tp) if i % 2 == j])
+        far = call(far_kernel, place, (full_block, got), (None,) * 2, [shape((slots, out_cols))])[0]
+        far_recv.append(lax.ppermute(far, "tp", [(i, i ^ 2) for i in range(n_tp) if i % 2 == j]))
     near_recv = swap(near_send)
     if paired:
         down_send, down_keep = call(
             down_kernel,
             place,
-            (latent, near_keep, near_recv, far_recv, down_proj, from_x[8], from_z[8]),
-            (None,) * 7,
+            (latent, near_keep, near_recv, *far_recv, down_proj, from_x[8], from_x[9], from_z[8], from_z[9]),
+            (None,) * 10,
             [shape((slots, half)), shape((slots, half), F32)],
             scratch=[pltpu.VMEM((slots, lat_cols), BF16)],
             cost=(0.6e9, 4e6),
         )
     else:
         base = latent.astype(F32) + near_keep + near_recv.astype(F32)
-        latent_out = (base + far_recv.astype(F32)).astype(BF16)
+        latent_out = (base + far_recv[0].astype(F32) + far_recv[1].astype(F32)).astype(BF16)
         full = dot(latent_out, gather(down_proj, 1))
         down_keep = lax.dynamic_slice_in_dim(full, k * half, half, 1)
         down_send = lax.dynamic_slice_in_dim(full, (1 - k) * half, half, 1).astype(BF16)

time: 195 us -> 188 us (0.964)
  local copies, waits for them, and re-layouts: 16.2 us -> 0.14 us
  Pallas kernels: 33.8 us -> 38.1 us
  starting transfers between devices: 40.8 us -> 44.9 us
    unnamed x48 -> x20, local copies, waits for them, and re-layouts: 14.5 us -> 0.06 us
    ppermute x5 -> x4, starting transfers between devices: 11 us -> 0.93 us  [cross(): return lax.ppermute(x, 'tp', [(i, i ^ 2) for i in range(n_tp)])]
    ppermute x0 -> x4, starting transfers between devices: none -> 7.08 us  [the longest x2 4.46 us: local(): lax.ppermute(far, 'tp', [(i, i ^ 2) for i in range(n_tp) if i % 2 == j])]
    ppermute x10 -> x11, starting transfers between devices: 8.44 us -> 13.9 us  [flip(): return lax.ppermute(x, 'ctx', [(0, 1), (1, 0)])]
    ppermute x7 -> x8, waiting for transfers between devices: 25 us -> 20.3 us  [pair(): return lax.ppermute(x, 'dp', [(i, i ^ 1) for i in range(n_dp)])]
    pallas_call x16 -> x22, Pallas kernels: 33.8 us -> 38.1 us  [call(): pl.pallas_call(body, out_shape=outs, grid_spec=pltpu.PrefetchScalarGridSp...]
    ppermute x10 -> x11, waiting for transfers between devices: 39.2 us -> 43.1 us  [flip(): return lax.ppermute(x, 'ctx', [(0, 1), (1, 0)])]
    ppermute x7 -> x8, starting transfers between devices: 9.98 us -> 11.6 us  [pair(): return lax.ppermute(x, 'dp', [(i, i ^ 1) for i in range(n_dp)])]
  transfers between devices with their start and end apart: 38 -> 43, of which waited for: 18 -> 22; matrix products, arithmetic and copies ran while one was open for 2% -> 0% of each run, Pallas kernels for 12% -> 19%
where the time goes in v1:
time: 188 us; the launch traced here: 185 us
  waiting for transfers between devices  101 us (54%)
  starting transfers between devices  44.9 us (24%)
  Pallas kernels  38.1 us (20%)
    ppermute x11, waiting for transfers between devices, flip(): return lax.ppermute(x, 'ctx', [(0, 1), (1, 0)])  43.1 us
    pallas_call x22, Pallas kernels, call(): pl.pallas_call(body, out_shape=outs, grid_spec=pltpu.PrefetchScalarGridSp...  38.1 us
    ppermute x8, waiting for transfers between devices, pair(): return lax.ppermute(x, 'dp', [(i, i ^ 1) for i in range(n_dp)])  20.3 us
    ppermute x11, starting transfers between devices, flip(): return lax.ppermute(x, 'ctx', [(0, 1), (1, 0)])  13.9 us
    ppermute x1, waiting for transfers between devices, forward(): return lax.ppermute(x, ('ctx', 'tp'), [(i, i + 2) for i in range(n - 2)])  13.2 us
    ppermute x8, starting transfers between devices, pair(): return lax.ppermute(x, 'dp', [(i, i ^ 1) for i in range(n_dp)])  11.6 us
    ppermute x4, waiting for transfers between devices, cross(): return lax.ppermute(x, 'tp', [(i, i ^ 2) for i in range(n_tp)])  10.9 us
    ppermute x2, starting transfers between devices, local(): lax.ppermute(far, 'tp', [(i, i ^ 2) for i in range(n_tp) if i % 2 == j])  4.46 us
  transfers between devices with their start and end apart: 43, of which 22 were waited for; matrix products, arithmetic and copies ran while one was open for 0% of the time, Pallas kernels for 19%

profile of v1, /device:TPU:2, one launch (start us, length us, event | category | flops | bytes accessed | tf_op | source)
XLA Modules:
  0.0 185.4 jit_solution(16215032434634611533)
XLA Ops:
  0.0 3.5 %collective-permute-start = (bf16[256,1024]{1,0:T(8,128)(2,1)}, bf16[256,1024]{1,0:T(8,128)(2,1)S(1)}, u32[]{:S(2)}, u32[]{:S(2)}) collective-permute-start(bf16[256,1024]{1,0:T(8,128)(2,1)} %emb_own.1), channel_id=1, source_target_pairs={{0,8},{4,12},{8,16},{12,20},{16,24},{20,28},{1,9},{5,13},{9,17},{1... | collective-permute-start | bytes 1572872 | tf_op jit(solution)/shard_map/ppermute | solution.py:494
  3.6 13.2 %collective-permute-done.own = bf16[256,1024]{1,0:T(8,128)(2,1)S(1)} collective-permute-done((bf16[256,1024]{1,0:T(8,128)(2,1)}, bf16[256,1024]{1,0:T(8,128)(2,1)S(1)}, u32[]{:S(2)}, u32[]{:S(2)}) %collective-permute-start) | collective-permute-done | bytes 524320 | tf_op jit(solution)/shard_map/ppermute | solution.py:494
  16.9 2.0 %shard_map.119 = (bf16[48,1024]{1,0:T(8,128)(2,1)S(1)}, bf16[1,256]{1,0:T(2,128)(2,1)S(1)}, bf16[2048,128]{1,0:T(8,128)(2,1)S(1)}, bf16[256,1024]{1,0:T(8,128)(2,1)S(1)}) custom-call(s32[5]{0:T(128)S(1)} %stack.27.ids, bf16[256,1024]{1,0:T(8,128)(2,1)} %emb_own.1, s32[1,256]{1,0:T(1,128)} %bitcast.11, bf16[2048,128]{1,0:T(8,128)(2,1)} %wk.1, ...), custom_call_target="tpu_custom_call" | custom-call | flops 1000000 | bytes 3000000 | tf_op jit(solution)/shard_map/pallas_call | solution.py:38
  18.9 2.5 %collective-permute-start.3 = (bf16[48,1024]{1,0:T(8,128)(2,1)S(1)}, bf16[48,1024]{1,0:T(8,128)(2,1)S(1)}, u32[]{:S(2)}, u32[]{:S(2)}) collective-permute-start(bf16[48,1024]{1,0:T(8,128)(2,1)S(1)} %get-tuple-element.46), channel_id=1, source_target_pairs={{16,8},{17,9},{18,10},{19,11}} | collective-permute-start | bytes 294920 | tf_op jit(solution)/shard_map/ppermute | solution.py:533
  22.8 1.8 collective-permute-done.3.extra0
  24.6 2.1 %collective-permute-done.4.extra1 = bf16[48,1024]{1,0:T(8,128)(2,1)S(1)} collective-permute-done((bf16[48,1024]{1,0:T(8,128)(2,1)S(1)}, bf16[48,1024]{1,0:T(8,128)(2,1)S(1)}, u32[]{:S(2)}, u32[]{:S(2)}) %collective-permute-start.4) | collective-permute-done | bytes 98336 | tf_op jit(solution)/shard_map/ppermute | solution.py:533
  26.7 4.7 %shard_map.120 = (bf16[544,512]{1,0:T(8,128)(2,1)S(1)}, bf16[512,512]{1,0:T(8,128)(2,1)S(1)}, bf16[32,512]{1,0:T(8,128)(2,1)S(1)}, bf16[544,512]{1,0:T(8,128)(2,...) custom-call(s32[5]{0:T(128)S(1)} %stack.27.ids, bf16[256,1024]{1,0:T(8,128)(2,1)S(1)} %copy-done.4, ...), custom_call_target="tpu_custom_call" | custom-call | flops 1711276032 | bytes 3000000 | tf_op jit(solution)/shard_map/pallas_call | solution.py:38
  32.4 4.0 %shard_map.121.own0 = bf16[544,256]{1,0:T(8,128)(2,1)S(1)} custom-call(s32[5]{0:T(128)S(1)} %stack.27.ids, bf16[512,1024]{1,0:T(8,128)(2,1)S(1)} %shard_map.118.normed, bf16[1024,512]{1,0:T(8,128)(2,1)S(1)} %get-tuple-element.47.wk, bf16[1024,512]{1,0:T(8,128)(2,1)S(1)} %get-tuple-element.48.wv, bf16[544,512]{1,0:T(8,128)(2,1)S(1)} %get-tuple-element.49.q_ref, ...), custom_call_target="tpu_custom_call" | custom-call | flops 4000000000 | bytes 3000000 | tf_op jit(solution)/shard_map/pallas_call | solution.py:38
  36.4 4.0 %shard_map.122.own1 = bf16[544,256]{1,0:T(8,128)(2,1)S(1)} custom-call(s32[5]{0:T(128)S(1)} %stack.27.ids, bf16[512,1024]{1,0:T(8,128)(2,1)S(1)} %shard_map.118.normed, bf16[1024,512]{1,0:T(8,128)(2,1)S(1)} %get-tuple-element.47.wk, bf16[1024,512]{1,0:T(8,128)(2,1)S(1)} %get-tuple-element.48.wv, bf16[544,512]{1,0:T(8,128)(2,1)S(1)} %get-tuple-element.49.q_ref, ...), custom_call_target="tpu_custom_call" | custom-call | flops 4000000000 | bytes 3000000 | tf_op jit(solution)/shard_map/pallas_call | solution.py:38
  41.0 1.4 collective-permute-done.7.other
  43.0 3.6 %collective-permute-done.8.other = bf16[1,512]{1,0:T(2,128)(2,1)S(1)} collective-permute-done((bf16[1,512]{1,0:T(2,128)(2,1)S(1)}, bf16[1,512]{1,0:T(2,128)(2,1)S(1)}, u32[]{:S(2)}, u32[]{:S(2)}) %collective-permute-start.8) | collective-permute-done | bytes 1056 | tf_op jit(solution)/shard_map/ppermute | solution.py:490
  48.0 1.6 shard_map.125
  49.6 1.6 collective-permute-start.12
  51.3 6.9 %collective-permute-done.9.recv = bf16[256,640]{1,0:T(8,128)(2,1)S(1)} collective-permute-done((bf16[256,640]{1,0:T(8,128)(2,1)S(1)}, bf16[256,640]{1,0:T(8,128)(2,1)S(1)}, u32[]{:S(2)}, u32[]{:S(2)}) %collective-permute-start.9) | collective-permute-done | bytes 327712 | tf_op jit(solution)/shard_map/ppermute | solution.py:490
  59.0 2.0 %collective-permute-start.16 = (bf16[2048,128]{1,0:T(8,128)(2,1)S(1)}, bf16[2048,128]{1,0:T(8,128)(2,1)S(1)}, u32[]{:S(2)}, u32[]{:S(2)}) collective-permute-start(bf16[2048,128]{1,0:T(8,128)(2,1)S(1)} %get-tuple-element.61), channel_id=1, source_target_pairs={{0,16},{16,0},{1,17},{17,1},{2,18},{18,2},{3,19},{19,3},{4,20},{20... | collective-permute-start | bytes 1572872 | tf_op jit(solution)/shard_map/ppermute | solution.py:497
  61.9 1.9 %collective-permute-start.18 = (bf16[1024,256]{1,0:T(8,128)(2,1)S(1)}, bf16[1024,256]{1,0:T(8,128)(2,1)S(1)}, u32[]{:S(2)}, u32[]{:S(2)}) collective-permute-start(bf16[1024,256]{1,0:T(8,128)(2,1)S(1)} %get-tuple-element.64), channel_id=1, source_target_pairs={{0,16},{16,0},{1,17},{17,1},{2,18},{18,2},{3,19},{19,3},{4,20},{20... | collective-permute-start | bytes 1572872 | tf_op jit(solution)/shard_map/ppermute | solution.py:497
  63.8 2.0 %collective-permute-start.20 = (bf16[1024,256]{1,0:T(8,128)(2,1)S(1)}, bf16[1024,256]{1,0:T(8,128)(2,1)S(1)}, u32[]{:S(2)}, u32[]{:S(2)}) collective-permute-start(bf16[1024,256]{1,0:T(8,128)(2,1)S(1)} %get-tuple-element.65), channel_id=1, source_target_pairs={{0,16},{16,0},{1,17},{17,1},{2,18},{18,2},{3,19},{19,3},{4,20},{20... | collective-permute-start | bytes 1572872 | tf_op jit(solution)/shard_map/ppermute | solution.py:497
  67.5 11.9 %collective-permute-done.25.x1 = bf16[128,1024]{1,0:T(8,128)(2,1)S(1)} collective-permute-done((bf16[128,1024]{1,0:T(8,128)(2,1)S(1)}, bf16[128,1024]{1,0:T(8,128)(2,1)S(1)}, u32[]{:S(2)}, u32[]{:S(2)}) %collective-permute-start.25) | collective-permute-done | bytes 262176 | tf_op jit(solution)/shard_map/ppermute | solution.py:497
  79.4 1.9 %collective-permute-start.23 = (bf16[256,1024]{1,0:T(8,128)(2,1)S(1)}, bf16[256,1024]{1,0:T(8,128)(2,1)S(1)}, u32[]{:S(2)}, u32[]{:S(2)}) collective-permute-start(bf16[256,1024]{1,0:T(8,128)(2,1)S(1)} %get-tuple-element.67), channel_id=1, source_target_pairs={{0,16},{16,0},{1,17},{17,1},{2,18},{18,2},{3,19},{19,3},{4,20},{20... | collective-permute-start | bytes 1572872 | tf_op jit(solution)/shard_map/ppermute | solution.py:497
  81.3 1.6 collective-permute-start.17
  82.9 7.8 %collective-permute-done.18.x0 = bf16[1024,256]{1,0:T(8,128)(2,1)S(1)} collective-permute-done((bf16[1024,256]{1,0:T(8,128)(2,1)S(1)}, bf16[1024,256]{1,0:T(8,128)(2,1)S(1)}, u32[]{:S(2)}, u32[]{:S(2)}) %collective-permute-start.18) | collective-permute-done | bytes 524320 | tf_op jit(solution)/shard_map/ppermute | solution.py:497
  90.7 1.6 collective-permute-start.19
  92.2 9.7 %collective-permute-done.20.x1 = bf16[1024,256]{1,0:T(8,128)(2,1)S(1)} collective-permute-done((bf16[1024,256]{1,0:T(8,128)(2,1)S(1)}, bf16[1024,256]{1,0:T(8,128)(2,1)S(1)}, u32[]{:S(2)}, u32[]{:S(2)}) %collective-permute-start.20) | collective-permute-done | bytes 524320 | tf_op jit(solution)/shard_map/ppermute | solution.py:497
  102.4 10.3 %collective-permute-done.23.x0 = bf16[256,1024]{1,0:T(8,128)(2,1)S(1)} collective-permute-done((bf16[256,1024]{1,0:T(8,128)(2,1)S(1)}, bf16[256,1024]{1,0:T(8,128)(2,1)S(1)}, u32[]{:S(2)}, u32[]{:S(2)}) %collective-permute-start.23) | collective-permute-done | bytes 524320 | tf_op jit(solution)/shard_map/ppermute | solution.py:497
  112.8 1.6 collective-permute-start.21
  114.8 1.7 collective-permute-start.26
  116.8 1.6 collective-permute-start.28
  118.4 4.0 %shard_map.128 = (bf16[256,4096]{1,0:T(8,128)(2,1)S(1)}, f32[256,128]{1,0:T(8,128)S(1)}, bf16[272,256]{1,0:T(8,128)(2,1)S(1)}) custom-call(s32[5]{0:T(128)S(1)} %stack.27.ids, s32[2]{0:T(128)S(1)} %get-tuple-element.56.totals, bf16[256,1024]{1,0:T(8,128)(2,1)S(1)} %shard_map.127.l0.latent, bf16[256,1024]{1,0:T(8,128)(2,1)S(1)} %collective-permute-done.13.l1, ...), custom_call_target="tpu_custom_call" | custom-call | flops 1000000000 | bytes 6000000 | tf_op jit(solution)/shard_map/pallas_call | solution.py:38
  122.4 5.2 %collective-permute-done.21.z1 = bf16[1024,256]{1,0:T(8,128)(2,1)S(1)} collective-permute-done((bf16[1024,256]{1,0:T(8,128)(2,1)S(1)}, bf16[1024,256]{1,0:T(8,128)(2,1)S(1)}, u32[]{:S(2)}, u32[]{:S(2)}) %collective-permute-start.21) | collective-permute-done | bytes 524320 | tf_op jit(solution)/shard_map/ppermute | solution.py:500
  127.6 1.7 collective-permute-start.22
  129.3 1.8 shard_map.130.q_ref
  131.1 1.5 collective-permute-done.22.kv_other
  132.6 2.1 %shard_map.131.attn = bf16[256,512]{1,0:T(8,128)(2,1)S(1)} custom-call(s32[5]{0:T(128)S(1)} %stack.27.ids, s32[2]{0:T(128)S(1)} %get-tuple-element.56.totals, bf16[256,512]{1,0:T(8,128)(2,1)S(1)} %shard_map.130.q_ref, bf16[272,256]{1,0:T(8,128)(2,1)S(1)} %get-tuple-element.66.kv_own, bf16[272,256]{1,0:T(8,128)(2,1)S(1)} %collective-permute-done.22.kv_other), custom_call_target="tpu_custom_call" | custom-call | flops 500000000 | bytes 1000000 | tf_op jit(solution)/shard_map/pallas_call | solution.py:38
  134.7 4.1 %collective-permute-done.24.z0 = bf16[256,1024]{1,0:T(8,128)(2,1)S(1)} collective-permute-done((bf16[256,1024]{1,0:T(8,128)(2,1)S(1)}, bf16[256,1024]{1,0:T(8,128)(2,1)S(1)}, u32[]{:S(2)}, u32[]{:S(2)}) %collective-permute-start.24) | collective-permute-done | bytes 524320 | tf_op jit(solution)/shard_map/ppermute | solution.py:500
  141.1 2.1 %collective-permute-done.28.z1 = bf16[128,1024]{1,0:T(8,128)(2,1)S(1)} collective-permute-done((bf16[128,1024]{1,0:T(8,128)(2,1)S(1)}, bf16[128,1024]{1,0:T(8,128)(2,1)S(1)}, u32[]{:S(2)}, u32[]{:S(2)}) %collective-permute-start.28) | collective-permute-done | bytes 262176 | tf_op jit(solution)/shard_map/ppermute | solution.py:500
  145.5 1.9 %collective-permute-start.34 = (bf16[256,512]{1,0:T(8,128)(2,1)S(1)}, bf16[256,512]{1,0:T(8,128)(2,1)S(1)}, u32[]{:S(2)}, u32[]{:S(2)}) collective-permute-start(bf16[256,512]{1,0:T(8,128)(2,1)S(1)} %get-tuple-element.77), channel_id=1, source_target_pairs={{0,16},{16,0},{1,17},{17,1},{2,18},{18,2},{3,19},{19,3},{4,20},{20... | collective-permute-start | bytes 786440 | tf_op jit(solution)/shard_map/ppermute | solution.py:497
  147.6 1.7 shard_map.132
  150.1 3.8 %collective-permute-start.31 = (bf16[256,1024]{1,0:T(8,128)(2,1)S(1)}, bf16[256,1024]{1,0:T(8,128)(2,1)S(1)}, u32[]{:S(2)}, u32[]{:S(2)}) collective-permute-start(bf16[256,1024]{1,0:T(8,128)(2,1)S(1)} %shard_map.134), channel_id=1, source_target_pairs={{0,8},{8,0},{1,9},{9,1},{2,10},{10,2},{3,11},{11,3},{16,24},{24,16... | collective-permute-start | bytes 1572872 | tf_op jit(solution)/shard_map/ppermute | solution.py:725
  155.2 1.6 collective-permute-start.36
  156.8 1.9 %collective-permute-done.35.x1 = bf16[256,512]{1,0:T(8,128)(2,1)S(1)} collective-permute-done((bf16[256,512]{1,0:T(8,128)(2,1)S(1)}, bf16[256,512]{1,0:T(8,128)(2,1)S(1)}, u32[]{:S(2)}, u32[]{:S(2)}) %collective-permute-start.35) | collective-permute-done | bytes 262176 | tf_op jit(solution)/shard_map/ppermute | solution.py:497
  158.7 1.6 collective-permute-start.37
  160.3 4.1 %collective-permute-done.36.z0 = bf16[256,512]{1,0:T(8,128)(2,1)S(1)} collective-permute-done((bf16[256,512]{1,0:T(8,128)(2,1)S(1)}, bf16[256,512]{1,0:T(8,128)(2,1)S(1)}, u32[]{:S(2)}, u32[]{:S(2)}) %collective-permute-start.36) | collective-permute-done | bytes 262176 | tf_op jit(solution)/shard_map/ppermute | solution.py:500
  164.4 4.9 %collective-permute-done.37.z1 = bf16[256,512]{1,0:T(8,128)(2,1)S(1)} collective-permute-done((bf16[256,512]{1,0:T(8,128)(2,1)S(1)}, bf16[256,512]{1,0:T(8,128)(2,1)S(1)}, u32[]{:S(2)}, u32[]{:S(2)}) %collective-permute-start.37) | collective-permute-done | bytes 262176 | tf_op jit(solution)/shard_map/ppermute | solution.py:500
  169.3 1.4 shard_map.137
  170.8 1.5 collective-permute-done.38.recv
  176.4 2.9 %collective-permute-done.40.carry0 = bf16[1,512]{1,0:T(2,128)(2,1)S(1)} collective-permute-done((bf16[1,512]{1,0:T(2,128)(2,1)S(1)}, bf16[1,512]{1,0:T(2,128)(2,1)S(1)}, u32[]{:S(2)}, u32[]{:S(2)}) %collective-permute-start.40) | collective-permute-done | bytes 1056 | tf_op jit(solution)/shard_map/ppermute | solution.py:753
  179.3 2.3 %collective-permute-done.41.carry1 = bf16[1,512]{1,0:T(2,128)(2,1)S(1)} collective-permute-done((bf16[1,512]{1,0:T(2,128)(2,1)S(1)}, bf16[1,512]{1,0:T(2,128)(2,1)S(1)}, u32[]{:S(2)}, u32[]{:S(2)}) %collective-permute-start.41) | collective-permute-done | bytes 1056 | tf_op jit(solution)/shard_map/ppermute | solution.py:754
  183.0 1.5 collective-permute-done.42
  (82 shorter events, 23.0 us)
Async XLA Ops:
  0.0 26.7 %copy-start.4 = (bf16[256,1024]{1,0:T(8,128)(2,1)S(1)}, bf16[256,1024]{1,0:T(8,128)(2,1)}, u32[]{:S(2)}) copy-start(bf16[256,1024]{1,0:T(8,128)(2,1)} %emb_own.1) | copy-start | bytes 1572868
  0.0 26.7 %copy-start.7 = (f32[1024]{0:T(1024)S(1)}, f32[1024]{0:T(1024)}, u32[]{:S(2)}) copy-start(f32[1024]{0:T(1024)} %param.14) | copy-start | bytes 12292
  0.0 16.8 %collective-permute-start = (bf16[256,1024]{1,0:T(8,128)(2,1)}, bf16[256,1024]{1,0:T(8,128)(2,1)S(1)}, u32[]{:S(2)}, u32[]{:S(2)}) collective-permute-start(bf16[256,1024]{1,0:T(8,128)(2,1)} %emb_own.1), channel_id=1, source_target_pairs={{0,8},{4,12},{8,16},{12,20},{16,24},{20,28},{1,9},{5,13},{9,17},{1... | collective-permute-start | bytes 1572872 | tf_op jit(solution)/shard_map/ppermute | solution.py:494
  3.6 23.1 %collective-permute-start.2 = (bf16[256,1024]{1,0:T(8,128)(2,1)}, bf16[256,1024]{1,0:T(8,128)(2,1)S(1)}, u32[]{:S(2)}, u32[]{:S(2)}) collective-permute-start(bf16[256,1024]{1,0:T(8,128)(2,1)} %emb_own.1), channel_id=1, source_target_pairs={{0,4},{4,0},{8,12},{12,8},{1,5},{5,1},{9,13},{13,9},{2,6},{6,2},{1... | collective-permute-start | bytes 1572872 | tf_op jit(solution)/shard_map/ppermute | solution.py:487
  16.8 14.6 %collective-permute-start.1 = (bf16[256,1024]{1,0:T(8,128)(2,1)S(1)}, bf16[256,1024]{1,0:T(8,128)(2,1)S(1)}, u32[]{:S(2)}, u32[]{:S(2)}) collective-permute-start(bf16[256,1024]{1,0:T(8,128)(2,1)S(1)} %collective-permute-done.own), channel_id=1, source_target_pairs={{0,4},{4,0},{8,12},{12,8},{1,5},{5,1},{9,13},{13,9},{2,6},{6,2},{1... | collective-permute-start | bytes 1572872 | tf_op jit(solution)/shard_map/ppermute | solution.py:487
  18.9 5.7 %collective-permute-start.3 = (bf16[48,1024]{1,0:T(8,128)(2,1)S(1)}, bf16[48,1024]{1,0:T(8,128)(2,1)S(1)}, u32[]{:S(2)}, u32[]{:S(2)}) collective-permute-start(bf16[48,1024]{1,0:T(8,128)(2,1)S(1)} %get-tuple-element.46), channel_id=1, source_target_pairs={{16,8},{17,9},{18,10},{19,11}} | collective-permute-start | bytes 294920 | tf_op jit(solution)/shard_map/ppermute | solution.py:533
  21.4 5.3 %collective-permute-start.4 = (bf16[48,1024]{1,0:T(8,128)(2,1)S(1)}, bf16[48,1024]{1,0:T(8,128)(2,1)S(1)}, u32[]{:S(2)}, u32[]{:S(2)}) collective-permute-start(bf16[48,1024]{1,0:T(8,128)(2,1)S(1)} %get-tuple-element.46), channel_id=1, source_target_pairs={{16,12},{17,13},{18,14},{19,15}} | collective-permute-start | bytes 294920 | tf_op jit(solution)/shard_map/ppermute | solution.py:533
  22.7 26.9 %collective-permute-start.11 = (bf16[256,1024]{1,0:T(8,128)(2,1)S(1)}, bf16[256,1024]{1,0:T(8,128)(2,1)S(1)}, u32[]{:S(2)}, u32[]{:S(2)}) collective-permute-start(bf16[256,1024]{1,0:T(8,128)(2,1)S(1)} %get-tuple-element.60), channel_id=1, source_target_pairs={{0,16},{16,0},{1,17},{17,1},{2,18},{18,2},{3,19},{19,3},{4,20},{20... | collective-permute-start | bytes 1572872 | tf_op jit(solution)/shard_map/ppermute | solution.py:497
  40.4 7.5 %collective-permute-start.5 = (bf16[544,256]{1,0:T(8,128)(2,1)S(1)}, bf16[544,256]{1,0:T(8,128)(2,1)S(1)}, u32[]{:S(2)}, u32[]{:S(2)}) collective-permute-start(bf16[544,256]{1,0:T(8,128)(2,1)S(1)} %shard_map.121.own0), channel_id=1, source_target_pairs={{0,4},{4,0},{8,12},{12,8},{1,5},{5,1},{9,13},{13,9},{2,6},{6,2},{1... | collective-permute-start | bytes 835592 | tf_op jit(solution)/shard_map/ppermute | solution.py:487
  40.5 7.4 %collective-permute-start.6 = (bf16[544,256]{1,0:T(8,128)(2,1)S(1)}, bf16[544,256]{1,0:T(8,128)(2,1)S(1)}, u32[]{:S(2)}, u32[]{:S(2)}) collective-permute-start(bf16[544,256]{1,0:T(8,128)(2,1)S(1)} %shard_map.122.own1), channel_id=1, source_target_pairs={{0,4},{4,0},{8,12},{12,8},{1,5},{5,1},{9,13},{13,9},{2,6},{6,2},{1... | collective-permute-start | bytes 835592 | tf_op jit(solution)/shard_map/ppermute | solution.py:487
  41.0 1.4 collective-permute-start.7
  43.0 3.7 %collective-permute-start.8 = (bf16[1,512]{1,0:T(2,128)(2,1)S(1)}, bf16[1,512]{1,0:T(2,128)(2,1)S(1)}, u32[]{:S(2)}, u32[]{:S(2)}) collective-permute-start(bf16[1,512]{1,0:T(2,128)(2,1)S(1)} %shard_map.123.mine), channel_id=1, source_target_pairs={{0,8},{4,12},{8,0},{12,4},{1,9},{5,13},{9,1},{13,5},{2,10},{6,14},... | collective-permute-start | bytes 3080 | tf_op jit(solution)/shard_map/ppermute | solution.py:490
  49.5 8.7 %collective-permute-start.9 = (bf16[256,640]{1,0:T(8,128)(2,1)S(1)}, bf16[256,640]{1,0:T(8,128)(2,1)S(1)}, u32[]{:S(2)}, u32[]{:S(2)}) collective-permute-start(bf16[256,640]{1,0:T(8,128)(2,1)S(1)} %get-tuple-element.59), channel_id=1, source_target_pairs={{0,8},{4,12},{8,0},{12,4},{1,9},{5,13},{9,1},{13,5},{2,10},{6,14},... | collective-permute-start | bytes 983048 | tf_op jit(solution)/shard_map/ppermute | solution.py:490
  49.6 14.2 %collective-permute-start.12 = (bf16[256,1024]{1,0:T(8,128)(2,1)S(1)}, bf16[256,1024]{1,0:T(8,128)(2,1)S(1)}, u32[]{:S(2)}, u32[]{:S(2)}) collective-permute-start(bf16[256,1024]{1,0:T(8,128)(2,1)S(1)} %collective-permute-done.11.w_x), channel_id=1, source_target_pairs={{0,1},{1,0},{2,3},{3,2},{4,5},{5,4},{6,7},{7,6},{8,9},{9,8},{10,11... | collective-permute-start | bytes 1572872 | tf_op jit(solution)/shard_map/ppermute | solution.py:500
  58.9 6.9 %collective-permute-start.10 = (bf16[256,512]{1,0:T(8,128)(2,1)S(1)}, bf16[256,512]{1,0:T(8,128)(2,1)S(1)}, u32[]{:S(2)}, u32[]{:S(2)}) collective-permute-start(bf16[256,512]{1,0:T(8,128)(2,1)S(1)} %shard_map.126.half), channel_id=1, source_target_pairs={{0,4},{4,0},{8,12},{12,8},{1,5},{5,1},{9,13},{13,9},{2,6},{6,2},{1... | collective-permute-start | bytes 786440 | tf_op jit(solution)/shard_map/ppermute | solution.py:487
  59.0 22.4 %collective-permute-start.16 = (bf16[2048,128]{1,0:T(8,128)(2,1)S(1)}, bf16[2048,128]{1,0:T(8,128)(2,1)S(1)}, u32[]{:S(2)}, u32[]{:S(2)}) collective-permute-start(bf16[2048,128]{1,0:T(8,128)(2,1)S(1)} %get-tuple-element.61), channel_id=1, source_target_pairs={{0,16},{16,0},{1,17},{17,1},{2,18},{18,2},{3,19},{19,3},{4,20},{20... | collective-permute-start | bytes 1572872 | tf_op jit(solution)/shard_map/ppermute | solution.py:497
  61.7 56.7 %copy-start.5 = (bf16[2048,128]{1,0:T(8,128)(2,1)S(1)}, bf16[2048,128]{1,0:T(8,128)(2,1)}, u32[]{:S(2)}) copy-start(bf16[2048,128]{1,0:T(8,128)(2,1)} %wk.1) | copy-start | bytes 1572868
  61.7 56.7 %copy-start.6 = (bf16[2048,128]{1,0:T(8,128)(2,1)S(1)}, bf16[2048,128]{1,0:T(8,128)(2,1)}, u32[]{:S(2)}) copy-start(bf16[2048,128]{1,0:T(8,128)(2,1)} %wv.1) | copy-start | bytes 1572868
  61.7 56.7 %copy-start.8 = (f32[4096]{0:T(1024)S(1)}, f32[4096]{0:T(1024)}, u32[]{:S(2)}) copy-start(f32[4096]{0:T(1024)} %param.18) | copy-start | bytes 49156
  61.7 17.7 %collective-permute-start.25 = (bf16[128,1024]{1,0:T(8,128)(2,1)S(1)}, bf16[128,1024]{1,0:T(8,128)(2,1)S(1)}, u32[]{:S(2)}, u32[]{:S(2)}) collective-permute-start(bf16[128,1024]{1,0:T(8,128)(2,1)S(1)} %get-tuple-element.68), channel_id=1, source_target_pairs={{0,16},{16,0},{1,17},{17,1},{2,18},{18,2},{3,19},{19,3},{4,20},{20... | collective-permute-start | bytes 786440 | tf_op jit(solution)/shard_map/ppermute | solution.py:497
  61.9 28.8 %collective-permute-start.18 = (bf16[1024,256]{1,0:T(8,128)(2,1)S(1)}, bf16[1024,256]{1,0:T(8,128)(2,1)S(1)}, u32[]{:S(2)}, u32[]{:S(2)}) collective-permute-start(bf16[1024,256]{1,0:T(8,128)(2,1)S(1)} %get-tuple-element.64), channel_id=1, source_target_pairs={{0,16},{16,0},{1,17},{17,1},{2,18},{18,2},{3,19},{19,3},{4,20},{20... | collective-permute-start | bytes 1572872 | tf_op jit(solution)/shard_map/ppermute | solution.py:497
  63.8 38.1 %collective-permute-start.20 = (bf16[1024,256]{1,0:T(8,128)(2,1)S(1)}, bf16[1024,256]{1,0:T(8,128)(2,1)S(1)}, u32[]{:S(2)}, u32[]{:S(2)}) collective-permute-start(bf16[1024,256]{1,0:T(8,128)(2,1)S(1)} %get-tuple-element.65), channel_id=1, source_target_pairs={{0,16},{16,0},{1,17},{17,1},{2,18},{18,2},{3,19},{19,3},{4,20},{20... | collective-permute-start | bytes 1572872 | tf_op jit(solution)/shard_map/ppermute | solution.py:497
  67.1 34.8 %collective-permute-start.14 = (bf16[256,1024]{1,0:T(8,128)(2,1)S(1)}, bf16[256,1024]{1,0:T(8,128)(2,1)S(1)}, u32[]{:S(2)}, u32[]{:S(2)}) collective-permute-start(bf16[256,1024]{1,0:T(8,128)(2,1)S(1)} %shard_map.127.l0.latent), channel_id=1, source_target_pairs={{0,8},{4,12},{8,0},{12,4},{1,9},{5,13},{9,1},{13,5},{2,10},{6,14},... | collective-permute-start | bytes 1572872 | tf_op jit(solution)/shard_map/ppermute | solution.py:490
  79.4 33.3 %collective-permute-start.23 = (bf16[256,1024]{1,0:T(8,128)(2,1)S(1)}, bf16[256,1024]{1,0:T(8,128)(2,1)S(1)}, u32[]{:S(2)}, u32[]{:S(2)}) collective-permute-start(bf16[256,1024]{1,0:T(8,128)(2,1)S(1)} %get-tuple-element.67), channel_id=1, source_target_pairs={{0,16},{16,0},{1,17},{17,1},{2,18},{18,2},{3,19},{19,3},{4,20},{20... | collective-permute-start | bytes 1572872 | tf_op jit(solution)/shard_map/ppermute | solution.py:497
  81.3 33.0 %collective-permute-start.17 = (bf16[2048,128]{1,0:T(8,128)(2,1)S(1)}, bf16[2048,128]{1,0:T(8,128)(2,1)S(1)}, u32[]{:S(2)}, u32[]{:S(2)}) collective-permute-start(bf16[2048,128]{1,0:T(8,128)(2,1)S(1)} %collective-permute-done.16.w_x), channel_id=1, source_target_pairs={{0,1},{1,0},{2,3},{3,2},{4,5},{5,4},{6,7},{7,6},{8,9},{9,8},{10,11... | collective-permute-start | bytes 1572872 | tf_op jit(solution)/shard_map/ppermute | solution.py:500
  90.7 24.1 %collective-permute-start.19 = (bf16[1024,256]{1,0:T(8,128)(2,1)S(1)}, bf16[1024,256]{1,0:T(8,128)(2,1)S(1)}, u32[]{:S(2)}, u32[]{:S(2)}) collective-permute-start(bf16[1024,256]{1,0:T(8,128)(2,1)S(1)} %collective-permute-done.18.x0), channel_id=1, source_target_pairs={{0,1},{1,0},{2,3},{3,2},{4,5},{5,4},{6,7},{7,6},{8,9},{9,8},{10,11... | collective-permute-start | bytes 1572872 | tf_op jit(solution)/shard_map/ppermute | solution.py:500
  101.9 14.6 %collective-permute-start.13 = (bf16[256,1024]{1,0:T(8,128)(2,1)S(1)}, bf16[256,1024]{1,0:T(8,128)(2,1)S(1)}, u32[]{:S(2)}, u32[]{:S(2)}) collective-permute-start(bf16[256,1024]{1,0:T(8,128)(2,1)S(1)} %shard_map.127.l0.latent), channel_id=1, source_target_pairs={{0,4},{4,0},{8,12},{12,8},{1,5},{5,1},{9,13},{13,9},{2,6},{6,2},{1... | collective-permute-start | bytes 1572872 | tf_op jit(solution)/shard_map/ppermute | solution.py:487
  101.9 14.9 %collective-permute-start.15 = (bf16[256,1024]{1,0:T(8,128)(2,1)S(1)}, bf16[256,1024]{1,0:T(8,128)(2,1)S(1)}, u32[]{:S(2)}, u32[]{:S(2)}) collective-permute-start(bf16[256,1024]{1,0:T(8,128)(2,1)S(1)} %collective-permute-done.14.l2), channel_id=1, source_target_pairs={{0,4},{4,0},{8,12},{12,8},{1,5},{5,1},{9,13},{13,9},{2,6},{6,2},{1... | collective-permute-start | bytes 1572872 | tf_op jit(solution)/shard_map/ppermute | solution.py:487
  112.8 14.8 %collective-permute-start.21 = (bf16[1024,256]{1,0:T(8,128)(2,1)S(1)}, bf16[1024,256]{1,0:T(8,128)(2,1)S(1)}, u32[]{:S(2)}, u32[]{:S(2)}) collective-permute-start(bf16[1024,256]{1,0:T(8,128)(2,1)S(1)} %collective-permute-done.20.x1), channel_id=1, source_target_pairs={{0,1},{1,0},{2,3},{3,2},{4,5},{5,4},{6,7},{7,6},{8,9},{9,8},{10,11... | collective-permute-start | bytes 1572872 | tf_op jit(solution)/shard_map/ppermute | solution.py:500
  114.3 24.5 %collective-permute-start.24 = (bf16[256,1024]{1,0:T(8,128)(2,1)S(1)}, bf16[256,1024]{1,0:T(8,128)(2,1)S(1)}, u32[]{:S(2)}, u32[]{:S(2)}) collective-permute-start(bf16[256,1024]{1,0:T(8,128)(2,1)S(1)} %collective-permute-done.23.x0), channel_id=1, source_target_pairs={{0,1},{1,0},{2,3},{3,2},{4,5},{5,4},{6,7},{7,6},{8,9},{9,8},{10,11... | collective-permute-start | bytes 1572872 | tf_op jit(solution)/shard_map/ppermute | solution.py:500
  114.8 26.3 %collective-permute-start.26 = (bf16[128,1024]{1,0:T(8,128)(2,1)S(1)}, bf16[128,1024]{1,0:T(8,128)(2,1)S(1)}, u32[]{:S(2)}, u32[]{:S(2)}) collective-permute-start(bf16[128,1024]{1,0:T(8,128)(2,1)S(1)} %get-tuple-element.69), channel_id=1, source_target_pairs={{0,16},{16,0},{1,17},{17,1},{2,18},{18,2},{3,19},{19,3},{4,20},{20... | collective-permute-start | bytes 786440 | tf_op jit(solution)/shard_map/ppermute | solution.py:497
  116.5 24.6 %collective-permute-start.27 = (bf16[128,1024]{1,0:T(8,128)(2,1)S(1)}, bf16[128,1024]{1,0:T(8,128)(2,1)S(1)}, u32[]{:S(2)}, u32[]{:S(2)}) collective-permute-start(bf16[128,1024]{1,0:T(8,128)(2,1)S(1)} %get-tuple-element.70), channel_id=1, source_target_pairs={{0,16},{16,0},{1,17},{17,1},{2,18},{18,2},{3,19},{19,3},{4,20},{20... | collective-permute-start | bytes 786440 | tf_op jit(solution)/shard_map/ppermute | solution.py:497
  116.8 26.3 %collective-permute-start.28 = (bf16[128,1024]{1,0:T(8,128)(2,1)S(1)}, bf16[128,1024]{1,0:T(8,128)(2,1)S(1)}, u32[]{:S(2)}, u32[]{:S(2)}) collective-permute-start(bf16[128,1024]{1,0:T(8,128)(2,1)S(1)} %collective-permute-done.25.x1), channel_id=1, source_target_pairs={{0,1},{1,0},{2,3},{3,2},{4,5},{5,4},{6,7},{7,6},{8,9},{9,8},{10,11... | collective-permute-start | bytes 786440 | tf_op jit(solution)/shard_map/ppermute | solution.py:500
  127.6 5.1 %collective-permute-start.22 = (bf16[272,256]{1,0:T(8,128)(2,1)S(1)}, bf16[272,256]{1,0:T(8,128)(2,1)S(1)}, u32[]{:S(2)}, u32[]{:S(2)}) collective-permute-start(bf16[272,256]{1,0:T(8,128)(2,1)S(1)} %get-tuple-element.66.kv_own), channel_id=1, source_target_pairs={{0,16},{16,0},{1,17},{17,1},{2,18},{18,2},{3,19},{19,3},{4,20},{20... | collective-permute-start | bytes 417800 | tf_op jit(solution)/shard_map/ppermute | solution.py:497
  139.8 9.6 %collective-permute-start.30 = (bf16[256,1024]{1,0:T(8,128)(2,1)S(1)}, bf16[256,1024]{1,0:T(8,128)(2,1)S(1)}, u32[]{:S(2)}, u32[]{:S(2)}) collective-permute-start(bf16[256,1024]{1,0:T(8,128)(2,1)S(1)} %get-tuple-element.74), channel_id=1, source_target_pairs={{4,0},{12,8},{5,1},{13,9},{6,2},{14,10},{7,3},{15,11},{20,16},{28,... | collective-permute-start | bytes 1572872 | tf_op jit(solution)/shard_map/ppermute | solution.py:723
  144.2 9.7 %collective-permute-start.32 = (bf16[256,1024]{1,0:T(8,128)(2,1)S(1)}, bf16[256,1024]{1,0:T(8,128)(2,1)S(1)}, u32[]{:S(2)}, u32[]{:S(2)}) collective-permute-start(bf16[256,1024]{1,0:T(8,128)(2,1)S(1)} %get-tuple-element.76), channel_id=1, source_target_pairs={{0,4},{8,12},{1,5},{9,13},{2,6},{10,14},{3,7},{11,15},{16,20},{24,... | collective-permute-start | bytes 1572872 | tf_op jit(solution)/shard_map/ppermute | solution.py:723
  145.5 9.7 %collective-permute-start.34 = (bf16[256,512]{1,0:T(8,128)(2,1)S(1)}, bf16[256,512]{1,0:T(8,128)(2,1)S(1)}, u32[]{:S(2)}, u32[]{:S(2)}) collective-permute-start(bf16[256,512]{1,0:T(8,128)(2,1)S(1)} %get-tuple-element.77), channel_id=1, source_target_pairs={{0,16},{16,0},{1,17},{17,1},{2,18},{18,2},{3,19},{19,3},{4,20},{20... | collective-permute-start | bytes 786440 | tf_op jit(solution)/shard_map/ppermute | solution.py:497
  147.4 11.3 %collective-permute-start.35 = (bf16[256,512]{1,0:T(8,128)(2,1)S(1)}, bf16[256,512]{1,0:T(8,128)(2,1)S(1)}, u32[]{:S(2)}, u32[]{:S(2)}) collective-permute-start(bf16[256,512]{1,0:T(8,128)(2,1)S(1)} %get-tuple-element.78), channel_id=1, source_target_pairs={{0,16},{16,0},{1,17},{17,1},{2,18},{18,2},{3,19},{19,3},{4,20},{20... | collective-permute-start | bytes 786440 | tf_op jit(solution)/shard_map/ppermute | solution.py:497
  149.3 20.0 %collective-permute-start.29 = (bf16[256,1024]{1,0:T(8,128)(2,1)S(1)}, bf16[256,1024]{1,0:T(8,128)(2,1)S(1)}, u32[]{:S(2)}, u32[]{:S(2)}) collective-permute-start(bf16[256,1024]{1,0:T(8,128)(2,1)S(1)} %get-tuple-element.72), channel_id=1, source_target_pairs={{0,4},{4,0},{8,12},{12,8},{1,5},{5,1},{9,13},{13,9},{2,6},{6,2},{1... | collective-permute-start | bytes 1572872 | tf_op jit(solution)/shard_map/ppermute | solution.py:487
  150.1 19.2 %collective-permute-start.31 = (bf16[256,1024]{1,0:T(8,128)(2,1)S(1)}, bf16[256,1024]{1,0:T(8,128)(2,1)S(1)}, u32[]{:S(2)}, u32[]{:S(2)}) collective-permute-start(bf16[256,1024]{1,0:T(8,128)(2,1)S(1)} %shard_map.134), channel_id=1, source_target_pairs={{0,8},{8,0},{1,9},{9,1},{2,10},{10,2},{3,11},{11,3},{16,24},{24,16... | collective-permute-start | bytes 1572872 | tf_op jit(solution)/shard_map/ppermute | solution.py:725
  154.5 14.8 %collective-permute-start.33 = (bf16[256,1024]{1,0:T(8,128)(2,1)S(1)}, bf16[256,1024]{1,0:T(8,128)(2,1)S(1)}, u32[]{:S(2)}, u32[]{:S(2)}) collective-permute-start(bf16[256,1024]{1,0:T(8,128)(2,1)S(1)} %shard_map.136), channel_id=1, source_target_pairs={{4,12},{12,4},{5,13},{13,5},{6,14},{14,6},{7,15},{15,7},{20,28},{2... | collective-permute-start | bytes 1572872 | tf_op jit(solution)/shard_map/ppermute | solution.py:725
  155.2 9.2 %collective-permute-start.36 = (bf16[256,512]{1,0:T(8,128)(2,1)S(1)}, bf16[256,512]{1,0:T(8,128)(2,1)S(1)}, u32[]{:S(2)}, u32[]{:S(2)}) collective-permute-start(bf16[256,512]{1,0:T(8,128)(2,1)S(1)} %collective-permute-done.34.x0), channel_id=1, source_target_pairs={{0,1},{1,0},{2,3},{3,2},{4,5},{5,4},{6,7},{7,6},{8,9},{9,8},{10,11... | collective-permute-start | bytes 786440 | tf_op jit(solution)/shard_map/ppermute | solution.py:500
  158.7 10.6 %collective-permute-start.37 = (bf16[256,512]{1,0:T(8,128)(2,1)S(1)}, bf16[256,512]{1,0:T(8,128)(2,1)S(1)}, u32[]{:S(2)}, u32[]{:S(2)}) collective-permute-start(bf16[256,512]{1,0:T(8,128)(2,1)S(1)} %collective-permute-done.35.x1), channel_id=1, source_target_pairs={{0,1},{1,0},{2,3},{3,2},{4,5},{5,4},{6,7},{7,6},{8,9},{9,8},{10,11... | collective-permute-start | bytes 786440 | tf_op jit(solution)/shard_map/ppermute | solution.py:500
  170.7 1.6 collective-permute-start.38
  173.5 8.5 %collective-permute-start.39 = (bf16[256,512]{1,0:T(8,128)(2,1)S(1)}, bf16[256,512]{1,0:T(8,128)(2,1)S(1)}, u32[]{:S(2)}, u32[]{:S(2)}) collective-permute-start(bf16[256,512]{1,0:T(8,128)(2,1)S(1)} %get-tuple-element.82), channel_id=1, source_target_pairs={{0,8},{4,12},{8,0},{12,4},{1,9},{5,13},{9,1},{13,5},{2,10},{6,14},... | collective-permute-start | bytes 786440 | tf_op jit(solution)/shard_map/ppermute | solution.py:490
  173.8 5.5 %collective-permute-start.40 = (bf16[1,512]{1,0:T(2,128)(2,1)S(1)}, bf16[1,512]{1,0:T(2,128)(2,1)S(1)}, u32[]{:S(2)}, u32[]{:S(2)}) collective-permute-start(bf16[1,512]{1,0:T(2,128)(2,1)S(1)} %get-tuple-element.84), channel_id=1, source_target_pairs={{0,16},{4,20},{1,17},{5,21},{2,18},{6,22},{3,19},{7,23}} | collective-permute-start | bytes 3080 | tf_op jit(solution)/shard_map/ppermute | solution.py:753
  175.1 6.5 %collective-permute-start.41 = (bf16[1,512]{1,0:T(2,128)(2,1)S(1)}, bf16[1,512]{1,0:T(2,128)(2,1)S(1)}, u32[]{:S(2)}, u32[]{:S(2)}) collective-permute-start(bf16[1,512]{1,0:T(2,128)(2,1)S(1)} %get-tuple-element.84), channel_id=1, source_target_pairs={{8,16},{12,20},{9,17},{13,21},{10,18},{14,22},{11,19},{15,23}} | collective-permute-start | bytes 3080 | tf_op jit(solution)/shard_map/ppermute | solution.py:754
  182.9 1.6 collective-permute-start.42
  (5 other events, 57.4 us)

commit v2 on v1

--- a/solution.py
+++ b/solution.py
@@ -10,10 +10,15 @@
 
 HB = 64
 HEAD_SIZE = 128
+WIN = 512
 EPS = 1e-05
 LEAD = 32
 NEG = -1e30
 VMEM_LIMIT = 24 << 20
+S_CTX = "ctx"
+S_DP = "dp"
+S_TP = "tp"
+
 F32 = jnp.float32
 BF16 = jnp.bfloat16
 
@@ -472,32 +477,33 @@
     down_proj,
 ):
     nbytes, width = byte_embed.shape
-    n_tp = lax.axis_size("tp")
-    n_ctx = lax.axis_size("ctx")
-    n_dp = lax.axis_size("dp")
+    n_tp = lax.axis_size(S_TP)
+    n_ctx = lax.axis_size(S_CTX)
+    n_dp = lax.axis_size(S_DP)
+    assert 2 * nbytes == WIN and n_tp == 4
     half = width // 2
     slots = n_tp * nbytes // 4
-    t = lax.axis_index("tp")
-    c = lax.axis_index("ctx")
-    zp = lax.axis_index("dp") % 2
+    t = lax.axis_index(S_TP)
+    c = lax.axis_index(S_CTX)
+    zp = lax.axis_index(S_DP) % 2
     a, k = t // 2, t % 2
     where_k = lambda first, second: jnp.where(k == 0, first, second)
 
     def swap(x):
-        return lax.ppermute(x, "tp", [(i, i ^ 1) for i in range(n_tp)])
+        return lax.ppermute(x, S_TP, [(i, i ^ 1) for i in range(n_tp)])
 
     def cross(x):
-        return lax.ppermute(x, "tp", [(i, i ^ 2) for i in range(n_tp)])
+        return lax.ppermute(x, S_TP, [(i, i ^ 2) for i in range(n_tp)])
 
     def forward(x):
         n = n_ctx * n_tp
-        return lax.ppermute(x, ("ctx", "tp"), [(i, i + 2) for i in range(n - 2)])
+        return lax.ppermute(x, (S_CTX, S_TP), [(i, i + 2) for i in range(n - 2)])
 
     def flip(x):
-        return lax.ppermute(x, "ctx", [(0, 1), (1, 0)])
+        return lax.ppermute(x, S_CTX, [(0, 1), (1, 0)])
 
     def pair(x):
-        return lax.ppermute(x, "dp", [(i, i ^ 1) for i in range(n_dp)])
+        return lax.ppermute(x, S_DP, [(i, i ^ 1) for i in range(n_dp)])
 
     paired = n_ctx == 2
 
@@ -530,7 +536,7 @@
     extras = []
     for j in range(2):
         extras.append(
-            lax.ppermute(head, ("ctx", "tp"), [(g * n_tp, g * n_tp - 2 + j) for g in range(1, n_ctx)])
+            lax.ppermute(head, (S_CTX, S_TP), [(g * n_tp, g * n_tp - 2 + j) for g in range(1, n_ctx)])
         )
 
     chip_starts = call(join_kernel, place, (starts, swap(starts)), (None,) * 2, [shape((1, 2 * nbytes))])[0]
@@ -644,7 +650,7 @@
         whole = where_k(
             jnp.concatenate([pooled, pooled_other], axis=1), jnp.concatenate([pooled_other, pooled], axis=1)
         )
-        latent = dot(whole, lax.all_gather(up_proj, "ctx", axis=0, tiled=True)).astype(BF16)
+        latent = dot(whole, lax.all_gather(up_proj, S_CTX, axis=0, tiled=True)).astype(BF16)
 
     l2 = cross(latent)
     l1 = swap(latent)
@@ -695,9 +701,9 @@
             [lax.dynamic_index_in_dim(stacked, t ^ i, 0, keepdims=False) for i in range(n_tp)], axis=1
         )
         lnorm = normed_rows(lat, lat_gain)
-        used = lax.all_gather(totals[:1], "ctx", axis=0, tiled=True)
+        used = lax.all_gather(totals[:1], S_CTX, axis=0, tiled=True)
         rows_iota = jnp.arange(slots, dtype=jnp.int32)
-        gather = lambda w, axis: lax.all_gather(w, "ctx", axis=axis, tiled=True)
+        gather = lambda w, axis: lax.all_gather(w, S_CTX, axis=axis, tiled=True)
         query = dot(lnorm, gather(query_proj, 0)).astype(BF16)
         kv = jnp.concatenate([dot(lnorm, gather(key_proj, 0)), dot(lnorm, gather(value_matrix, 0))], axis=1)
         keys = gather(kv.astype(BF16), 0)
@@ -720,9 +726,9 @@
 
     far_recv = []
     for j, (full_block, low_block) in enumerate((far0, far1)):
-        got = lax.ppermute(low_block, "tp", [(i ^ 1, i) for i in range(n_tp) if i % 2 == j])
+        got = lax.ppermute(low_block, S_TP, [(i ^ 1, i) for i in range(n_tp) if i % 2 == j])
         far = call(far_kernel, place, (full_block, got), (None,) * 2, [shape((slots, out_cols))])[0]
-        far_recv.append(lax.ppermute(far, "tp", [(i, i ^ 2) for i in range(n_tp) if i % 2 == j]))
+        far_recv.append(lax.ppermute(far, S_TP, [(i, i ^ 2) for i in range(n_tp) if i % 2 == j]))
     near_recv = swap(near_send)
     if paired:
         down_send, down_keep = call(
@@ -750,8 +756,8 @@
     )
     sum_recv = cross(chip_low)
     ahead = lambda at: [(g * n_tp + at * 2 + j, (g + 1) * n_tp + j) for g in range(n_ctx - 1) for j in range(2)]
-    carry0 = lax.ppermute(trailing, ("ctx", "tp"), ahead(0))
-    carry1 = lax.ppermute(trailing, ("ctx", "tp"), ahead(1))
+    carry0 = lax.ppermute(trailing, (S_CTX, S_TP), ahead(0))
+    carry1 = lax.ppermute(trailing, (S_CTX, S_TP), ahead(1))
     kept, send = call(
         final_kernel,
         place,
@@ -767,18 +773,18 @@
 
 def solution(mesh):
     placed = (
-        P(("dp", "ctx", "tp"), None),
-        P(("dp", "ctx", "tp")),
+        P((S_DP, S_CTX, S_TP), None),
+        P((S_DP, S_CTX, S_TP)),
         P(),
         P(),
         P(),
-        P("ctx", "tp"),
+        P(S_CTX, S_TP),
         P(),
-        P("ctx", "tp"),
-        P("ctx", "tp"),
-        P("ctx", "tp"),
-        P("tp", "ctx"),
-        P("tp", "ctx"),
+        P(S_CTX, S_TP),
+        P(S_CTX, S_TP),
+        P(S_CTX, S_TP),
+        P(S_TP, S_CTX),
+        P(S_TP, S_CTX),
     )
 
-    return jax.shard_map(local, mesh=mesh, in_specs=placed, out_specs=P(("dp", "ctx", "tp"), None), check_vma=False)
+    return jax.shard_map(local, mesh=mesh, in_specs=placed, out_specs=P((S_DP, S_CTX, S_TP), None), check_vma=False)

time: 188 us -> 188 us (level)
  no operation moved by 1% of the time
where the time goes in v2:
time: 188 us; the launch traced here: 185 us
  waiting for transfers between devices  101 us (54%)
  starting transfers between devices  44.9 us (24%)
  Pallas kernels  38.1 us (20%)
    ppermute x11, waiting for transfers between devices, flip(): return lax.ppermute(x, S_CTX, [(0, 1), (1, 0)])  43.1 us
    pallas_call x22, Pallas kernels, call(): pl.pallas_call(body, out_shape=outs, grid_spec=pltpu.PrefetchScalarGridSp...  38.1 us
    ppermute x8, waiting for transfers between devices, pair(): return lax.ppermute(x, S_DP, [(i, i ^ 1) for i in range(n_dp)])  20.3 us
    ppermute x11, starting transfers between devices, flip(): return lax.ppermute(x, S_CTX, [(0, 1), (1, 0)])  13.9 us
    ppermute x1, waiting for transfers between devices, forward(): return lax.ppermute(x, (S_CTX, S_TP), [(i, i + 2) for i in range(n - 2)])  13.2 us
    ppermute x8, starting transfers between devices, pair(): return lax.ppermute(x, S_DP, [(i, i ^ 1) for i in range(n_dp)])  11.6 us
    ppermute x4, waiting for transfers between devices, cross(): return lax.ppermute(x, S_TP, [(i, i ^ 2) for i in range(n_tp)])  10.9 us
    ppermute x2, starting transfers between devices, local(): lax.ppermute(far, S_TP, [(i, i ^ 2) for i in range(n_tp) if i % 2 == j])  4.46 us
  transfers between devices with their start and end apart: 43, of which 22 were waited for; matrix products, arithmetic and copies ran while one was open for 0% of the time, Pallas kernels for 19%

profile of v2, /device:TPU:2, one launch (start us, length us, event | category | flops | bytes accessed | tf_op | source)
XLA Modules:
  0.0 185.4 jit_solution(16215032434634611533)
XLA Ops:
  0.0 3.5 %collective-permute-start = (bf16[256,1024]{1,0:T(8,128)(2,1)}, bf16[256,1024]{1,0:T(8,128)(2,1)S(1)}, u32[]{:S(2)}, u32[]{:S(2)}) collective-permute-start(bf16[256,1024]{1,0:T(8,128)(2,1)} %emb_own.1), channel_id=1, source_target_pairs={{0,8},{4,12},{8,16},{12,20},{16,24},{20,28},{1,9},{5,13},{9,17},{1... | collective-permute-start | bytes 1572872 | tf_op jit(solution)/shard_map/ppermute | solution.py:500
  3.6 13.2 %collective-permute-done.own = bf16[256,1024]{1,0:T(8,128)(2,1)S(1)} collective-permute-done((bf16[256,1024]{1,0:T(8,128)(2,1)}, bf16[256,1024]{1,0:T(8,128)(2,1)S(1)}, u32[]{:S(2)}, u32[]{:S(2)}) %collective-permute-start) | collective-permute-done | bytes 524320 | tf_op jit(solution)/shard_map/ppermute | solution.py:500
  16.9 2.0 %shard_map.119 = (bf16[48,1024]{1,0:T(8,128)(2,1)S(1)}, bf16[1,256]{1,0:T(2,128)(2,1)S(1)}, bf16[2048,128]{1,0:T(8,128)(2,1)S(1)}, bf16[256,1024]{1,0:T(8,128)(2,1)S(1)}) custom-call(s32[5]{0:T(128)S(1)} %stack.27.ids, bf16[256,1024]{1,0:T(8,128)(2,1)} %emb_own.1, s32[1,256]{1,0:T(1,128)} %bitcast.11, bf16[2048,128]{1,0:T(8,128)(2,1)} %wk.1, ...), custom_call_target="tpu_custom_call" | custom-call | flops 1000000 | bytes 3000000 | tf_op jit(solution)/shard_map/pallas_call | solution.py:43
  18.9 2.5 %collective-permute-start.3 = (bf16[48,1024]{1,0:T(8,128)(2,1)S(1)}, bf16[48,1024]{1,0:T(8,128)(2,1)S(1)}, u32[]{:S(2)}, u32[]{:S(2)}) collective-permute-start(bf16[48,1024]{1,0:T(8,128)(2,1)S(1)} %get-tuple-element.46), channel_id=1, source_target_pairs={{16,8},{17,9},{18,10},{19,11}} | collective-permute-start | bytes 294920 | tf_op jit(solution)/shard_map/ppermute | solution.py:539
  22.8 1.8 collective-permute-done.3.extra0
  24.6 2.1 %collective-permute-done.4.extra1 = bf16[48,1024]{1,0:T(8,128)(2,1)S(1)} collective-permute-done((bf16[48,1024]{1,0:T(8,128)(2,1)S(1)}, bf16[48,1024]{1,0:T(8,128)(2,1)S(1)}, u32[]{:S(2)}, u32[]{:S(2)}) %collective-permute-start.4) | collective-permute-done | bytes 98336 | tf_op jit(solution)/shard_map/ppermute | solution.py:539
  26.7 4.7 %shard_map.120 = (bf16[544,512]{1,0:T(8,128)(2,1)S(1)}, bf16[512,512]{1,0:T(8,128)(2,1)S(1)}, bf16[32,512]{1,0:T(8,128)(2,1)S(1)}, bf16[544,512]{1,0:T(8,128)(2,...) custom-call(s32[5]{0:T(128)S(1)} %stack.27.ids, bf16[256,1024]{1,0:T(8,128)(2,1)S(1)} %copy-done.4, ...), custom_call_target="tpu_custom_call" | custom-call | flops 1711276032 | bytes 3000000 | tf_op jit(solution)/shard_map/pallas_call | solution.py:43
  32.4 4.0 %shard_map.121.own0 = bf16[544,256]{1,0:T(8,128)(2,1)S(1)} custom-call(s32[5]{0:T(128)S(1)} %stack.27.ids, bf16[512,1024]{1,0:T(8,128)(2,1)S(1)} %shard_map.118.normed, bf16[1024,512]{1,0:T(8,128)(2,1)S(1)} %get-tuple-element.47.wk, bf16[1024,512]{1,0:T(8,128)(2,1)S(1)} %get-tuple-element.48.wv, bf16[544,512]{1,0:T(8,128)(2,1)S(1)} %get-tuple-element.49.q_ref, ...), custom_call_target="tpu_custom_call" | custom-call | flops 4000000000 | bytes 3000000 | tf_op jit(solution)/shard_map/pallas_call | solution.py:43
  36.4 4.0 %shard_map.122.own1 = bf16[544,256]{1,0:T(8,128)(2,1)S(1)} custom-call(s32[5]{0:T(128)S(1)} %stack.27.ids, bf16[512,1024]{1,0:T(8,128)(2,1)S(1)} %shard_map.118.normed, bf16[1024,512]{1,0:T(8,128)(2,1)S(1)} %get-tuple-element.47.wk, bf16[1024,512]{1,0:T(8,128)(2,1)S(1)} %get-tuple-element.48.wv, bf16[544,512]{1,0:T(8,128)(2,1)S(1)} %get-tuple-element.49.q_ref, ...), custom_call_target="tpu_custom_call" | custom-call | flops 4000000000 | bytes 3000000 | tf_op jit(solution)/shard_map/pallas_call | solution.py:43
  41.0 1.4 collective-permute-done.7.other
  43.0 3.6 %collective-permute-done.8.other = bf16[1,512]{1,0:T(2,128)(2,1)S(1)} collective-permute-done((bf16[1,512]{1,0:T(2,128)(2,1)S(1)}, bf16[1,512]{1,0:T(2,128)(2,1)S(1)}, u32[]{:S(2)}, u32[]{:S(2)}) %collective-permute-start.8) | collective-permute-done | bytes 1056 | tf_op jit(solution)/shard_map/ppermute | solution.py:496
  48.0 1.6 shard_map.125
  49.6 1.6 collective-permute-start.12
  51.3 6.9 %collective-permute-done.9.recv = bf16[256,640]{1,0:T(8,128)(2,1)S(1)} collective-permute-done((bf16[256,640]{1,0:T(8,128)(2,1)S(1)}, bf16[256,640]{1,0:T(8,128)(2,1)S(1)}, u32[]{:S(2)}, u32[]{:S(2)}) %collective-permute-start.9) | collective-permute-done | bytes 327712 | tf_op jit(solution)/shard_map/ppermute | solution.py:496
  59.0 2.0 %collective-permute-start.16 = (bf16[2048,128]{1,0:T(8,128)(2,1)S(1)}, bf16[2048,128]{1,0:T(8,128)(2,1)S(1)}, u32[]{:S(2)}, u32[]{:S(2)}) collective-permute-start(bf16[2048,128]{1,0:T(8,128)(2,1)S(1)} %get-tuple-element.61), channel_id=1, source_target_pairs={{0,16},{16,0},{1,17},{17,1},{2,18},{18,2},{3,19},{19,3},{4,20},{20... | collective-permute-start | bytes 1572872 | tf_op jit(solution)/shard_map/ppermute | solution.py:503
  61.9 1.9 %collective-permute-start.18 = (bf16[1024,256]{1,0:T(8,128)(2,1)S(1)}, bf16[1024,256]{1,0:T(8,128)(2,1)S(1)}, u32[]{:S(2)}, u32[]{:S(2)}) collective-permute-start(bf16[1024,256]{1,0:T(8,128)(2,1)S(1)} %get-tuple-element.64), channel_id=1, source_target_pairs={{0,16},{16,0},{1,17},{17,1},{2,18},{18,2},{3,19},{19,3},{4,20},{20... | collective-permute-start | bytes 1572872 | tf_op jit(solution)/shard_map/ppermute | solution.py:503
  63.8 2.0 %collective-permute-start.20 = (bf16[1024,256]{1,0:T(8,128)(2,1)S(1)}, bf16[1024,256]{1,0:T(8,128)(2,1)S(1)}, u32[]{:S(2)}, u32[]{:S(2)}) collective-permute-start(bf16[1024,256]{1,0:T(8,128)(2,1)S(1)} %get-tuple-element.65), channel_id=1, source_target_pairs={{0,16},{16,0},{1,17},{17,1},{2,18},{18,2},{3,19},{19,3},{4,20},{20... | collective-permute-start | bytes 1572872 | tf_op jit(solution)/shard_map/ppermute | solution.py:503
  67.5 11.9 %collective-permute-done.25.x1 = bf16[128,1024]{1,0:T(8,128)(2,1)S(1)} collective-permute-done((bf16[128,1024]{1,0:T(8,128)(2,1)S(1)}, bf16[128,1024]{1,0:T(8,128)(2,1)S(1)}, u32[]{:S(2)}, u32[]{:S(2)}) %collective-permute-start.25) | collective-permute-done | bytes 262176 | tf_op jit(solution)/shard_map/ppermute | solution.py:503
  79.4 1.9 %collective-permute-start.23 = (bf16[256,1024]{1,0:T(8,128)(2,1)S(1)}, bf16[256,1024]{1,0:T(8,128)(2,1)S(1)}, u32[]{:S(2)}, u32[]{:S(2)}) collective-permute-start(bf16[256,1024]{1,0:T(8,128)(2,1)S(1)} %get-tuple-element.67), channel_id=1, source_target_pairs={{0,16},{16,0},{1,17},{17,1},{2,18},{18,2},{3,19},{19,3},{4,20},{20... | collective-permute-start | bytes 1572872 | tf_op jit(solution)/shard_map/ppermute | solution.py:503
  81.3 1.6 collective-permute-start.17
  82.9 7.8 %collective-permute-done.18.x0 = bf16[1024,256]{1,0:T(8,128)(2,1)S(1)} collective-permute-done((bf16[1024,256]{1,0:T(8,128)(2,1)S(1)}, bf16[1024,256]{1,0:T(8,128)(2,1)S(1)}, u32[]{:S(2)}, u32[]{:S(2)}) %collective-permute-start.18) | collective-permute-done | bytes 524320 | tf_op jit(solution)/shard_map/ppermute | solution.py:503
  90.7 1.6 collective-permute-start.19
  92.2 9.7 %collective-permute-done.20.x1 = bf16[1024,256]{1,0:T(8,128)(2,1)S(1)} collective-permute-done((bf16[1024,256]{1,0:T(8,128)(2,1)S(1)}, bf16[1024,256]{1,0:T(8,128)(2,1)S(1)}, u32[]{:S(2)}, u32[]{:S(2)}) %collective-permute-start.20) | collective-permute-done | bytes 524320 | tf_op jit(solution)/shard_map/ppermute | solution.py:503
  102.4 10.3 %collective-permute-done.23.x0 = bf16[256,1024]{1,0:T(8,128)(2,1)S(1)} collective-permute-done((bf16[256,1024]{1,0:T(8,128)(2,1)S(1)}, bf16[256,1024]{1,0:T(8,128)(2,1)S(1)}, u32[]{:S(2)}, u32[]{:S(2)}) %collective-permute-start.23) | collective-permute-done | bytes 524320 | tf_op jit(solution)/shard_map/ppermute | solution.py:503
  112.8 1.6 collective-permute-start.21
  114.8 1.7 collective-permute-start.26
  116.8 1.6 collective-permute-start.28
  118.4 4.0 %shard_map.128 = (bf16[256,4096]{1,0:T(8,128)(2,1)S(1)}, f32[256,128]{1,0:T(8,128)S(1)}, bf16[272,256]{1,0:T(8,128)(2,1)S(1)}) custom-call(s32[5]{0:T(128)S(1)} %stack.27.ids, s32[2]{0:T(128)S(1)} %get-tuple-element.56.totals, bf16[256,1024]{1,0:T(8,128)(2,1)S(1)} %shard_map.127.l0.latent, bf16[256,1024]{1,0:T(8,128)(2,1)S(1)} %collective-permute-done.13.l1, ...), custom_call_target="tpu_custom_call" | custom-call | flops 1000000000 | bytes 6000000 | tf_op jit(solution)/shard_map/pallas_call | solution.py:43
  122.4 5.2 %collective-permute-done.21.z1 = bf16[1024,256]{1,0:T(8,128)(2,1)S(1)} collective-permute-done((bf16[1024,256]{1,0:T(8,128)(2,1)S(1)}, bf16[1024,256]{1,0:T(8,128)(2,1)S(1)}, u32[]{:S(2)}, u32[]{:S(2)}) %collective-permute-start.21) | collective-permute-done | bytes 524320 | tf_op jit(solution)/shard_map/ppermute | solution.py:506
  127.6 1.7 collective-permute-start.22
  129.3 1.8 shard_map.130.q_ref
  131.1 1.5 collective-permute-done.22.kv_other
  132.6 2.1 %shard_map.131.attn = bf16[256,512]{1,0:T(8,128)(2,1)S(1)} custom-call(s32[5]{0:T(128)S(1)} %stack.27.ids, s32[2]{0:T(128)S(1)} %get-tuple-element.56.totals, bf16[256,512]{1,0:T(8,128)(2,1)S(1)} %shard_map.130.q_ref, bf16[272,256]{1,0:T(8,128)(2,1)S(1)} %get-tuple-element.66.kv_own, bf16[272,256]{1,0:T(8,128)(2,1)S(1)} %collective-permute-done.22.kv_other), custom_call_target="tpu_custom_call" | custom-call | flops 500000000 | bytes 1000000 | tf_op jit(solution)/shard_map/pallas_call | solution.py:43
  134.7 4.1 %collective-permute-done.24.z0 = bf16[256,1024]{1,0:T(8,128)(2,1)S(1)} collective-permute-done((bf16[256,1024]{1,0:T(8,128)(2,1)S(1)}, bf16[256,1024]{1,0:T(8,128)(2,1)S(1)}, u32[]{:S(2)}, u32[]{:S(2)}) %collective-permute-start.24) | collective-permute-done | bytes 524320 | tf_op jit(solution)/shard_map/ppermute | solution.py:506
  141.1 2.1 %collective-permute-done.28.z1 = bf16[128,1024]{1,0:T(8,128)(2,1)S(1)} collective-permute-done((bf16[128,1024]{1,0:T(8,128)(2,1)S(1)}, bf16[128,1024]{1,0:T(8,128)(2,1)S(1)}, u32[]{:S(2)}, u32[]{:S(2)}) %collective-permute-start.28) | collective-permute-done | bytes 262176 | tf_op jit(solution)/shard_map/ppermute | solution.py:506
  145.5 1.9 %collective-permute-start.34 = (bf16[256,512]{1,0:T(8,128)(2,1)S(1)}, bf16[256,512]{1,0:T(8,128)(2,1)S(1)}, u32[]{:S(2)}, u32[]{:S(2)}) collective-permute-start(bf16[256,512]{1,0:T(8,128)(2,1)S(1)} %get-tuple-element.77), channel_id=1, source_target_pairs={{0,16},{16,0},{1,17},{17,1},{2,18},{18,2},{3,19},{19,3},{4,20},{20... | collective-permute-start | bytes 786440 | tf_op jit(solution)/shard_map/ppermute | solution.py:503
  147.6 1.7 shard_map.132
  150.1 3.8 %collective-permute-start.31 = (bf16[256,1024]{1,0:T(8,128)(2,1)S(1)}, bf16[256,1024]{1,0:T(8,128)(2,1)S(1)}, u32[]{:S(2)}, u32[]{:S(2)}) collective-permute-start(bf16[256,1024]{1,0:T(8,128)(2,1)S(1)} %shard_map.134), channel_id=1, source_target_pairs={{0,8},{8,0},{1,9},{9,1},{2,10},{10,2},{3,11},{11,3},{16,24},{24,16... | collective-permute-start | bytes 1572872 | tf_op jit(solution)/shard_map/ppermute | solution.py:731
  155.2 1.6 collective-permute-start.36
  156.8 1.9 %collective-permute-done.35.x1 = bf16[256,512]{1,0:T(8,128)(2,1)S(1)} collective-permute-done((bf16[256,512]{1,0:T(8,128)(2,1)S(1)}, bf16[256,512]{1,0:T(8,128)(2,1)S(1)}, u32[]{:S(2)}, u32[]{:S(2)}) %collective-permute-start.35) | collective-permute-done | bytes 262176 | tf_op jit(solution)/shard_map/ppermute | solution.py:503
  158.7 1.6 collective-permute-start.37
  160.3 4.1 %collective-permute-done.36.z0 = bf16[256,512]{1,0:T(8,128)(2,1)S(1)} collective-permute-done((bf16[256,512]{1,0:T(8,128)(2,1)S(1)}, bf16[256,512]{1,0:T(8,128)(2,1)S(1)}, u32[]{:S(2)}, u32[]{:S(2)}) %collective-permute-start.36) | collective-permute-done | bytes 262176 | tf_op jit(solution)/shard_map/ppermute | solution.py:506
  164.4 4.9 %collective-permute-done.37.z1 = bf16[256,512]{1,0:T(8,128)(2,1)S(1)} collective-permute-done((bf16[256,512]{1,0:T(8,128)(2,1)S(1)}, bf16[256,512]{1,0:T(8,128)(2,1)S(1)}, u32[]{:S(2)}, u32[]{:S(2)}) %collective-permute-start.37) | collective-permute-done | bytes 262176 | tf_op jit(solution)/shard_map/ppermute | solution.py:506
  169.3 1.4 shard_map.137
  170.8 1.5 collective-permute-done.38.recv
  176.4 2.9 %collective-permute-done.40.carry0 = bf16[1,512]{1,0:T(2,128)(2,1)S(1)} collective-permute-done((bf16[1,512]{1,0:T(2,128)(2,1)S(1)}, bf16[1,512]{1,0:T(2,128)(2,1)S(1)}, u32[]{:S(2)}, u32[]{:S(2)}) %collective-permute-start.40) | collective-permute-done | bytes 1056 | tf_op jit(solution)/shard_map/ppermute | solution.py:759
  179.3 2.3 %collective-permute-done.41.carry1 = bf16[1,512]{1,0:T(2,128)(2,1)S(1)} collective-permute-done((bf16[1,512]{1,0:T(2,128)(2,1)S(1)}, bf16[1,512]{1,0:T(2,128)(2,1)S(1)}, u32[]{:S(2)}, u32[]{:S(2)}) %collective-permute-start.41) | collective-permute-done | bytes 1056 | tf_op jit(solution)/shard_map/ppermute | solution.py:760
  183.0 1.5 collective-permute-done.42
  (82 shorter events, 23.0 us)
Async XLA Ops:
  0.0 26.7 %copy-start.4 = (bf16[256,1024]{1,0:T(8,128)(2,1)S(1)}, bf16[256,1024]{1,0:T(8,128)(2,1)}, u32[]{:S(2)}) copy-start(bf16[256,1024]{1,0:T(8,128)(2,1)} %emb_own.1) | copy-start | bytes 1572868
  0.0 26.7 %copy-start.7 = (f32[1024]{0:T(1024)S(1)}, f32[1024]{0:T(1024)}, u32[]{:S(2)}) copy-start(f32[1024]{0:T(1024)} %param.14) | copy-start | bytes 12292
  0.0 16.8 %collective-permute-start = (bf16[256,1024]{1,0:T(8,128)(2,1)}, bf16[256,1024]{1,0:T(8,128)(2,1)S(1)}, u32[]{:S(2)}, u32[]{:S(2)}) collective-permute-start(bf16[256,1024]{1,0:T(8,128)(2,1)} %emb_own.1), channel_id=1, source_target_pairs={{0,8},{4,12},{8,16},{12,20},{16,24},{20,28},{1,9},{5,13},{9,17},{1... | collective-permute-start | bytes 1572872 | tf_op jit(solution)/shard_map/ppermute | solution.py:500
  3.6 23.1 %collective-permute-start.2 = (bf16[256,1024]{1,0:T(8,128)(2,1)}, bf16[256,1024]{1,0:T(8,128)(2,1)S(1)}, u32[]{:S(2)}, u32[]{:S(2)}) collective-permute-start(bf16[256,1024]{1,0:T(8,128)(2,1)} %emb_own.1), channel_id=1, source_target_pairs={{0,4},{4,0},{8,12},{12,8},{1,5},{5,1},{9,13},{13,9},{2,6},{6,2},{1... | collective-permute-start | bytes 1572872 | tf_op jit(solution)/shard_map/ppermute | solution.py:493
  16.8 14.6 %collective-permute-start.1 = (bf16[256,1024]{1,0:T(8,128)(2,1)S(1)}, bf16[256,1024]{1,0:T(8,128)(2,1)S(1)}, u32[]{:S(2)}, u32[]{:S(2)}) collective-permute-start(bf16[256,1024]{1,0:T(8,128)(2,1)S(1)} %collective-permute-done.own), channel_id=1, source_target_pairs={{0,4},{4,0},{8,12},{12,8},{1,5},{5,1},{9,13},{13,9},{2,6},{6,2},{1... | collective-permute-start | bytes 1572872 | tf_op jit(solution)/shard_map/ppermute | solution.py:493
  18.9 5.7 %collective-permute-start.3 = (bf16[48,1024]{1,0:T(8,128)(2,1)S(1)}, bf16[48,1024]{1,0:T(8,128)(2,1)S(1)}, u32[]{:S(2)}, u32[]{:S(2)}) collective-permute-start(bf16[48,1024]{1,0:T(8,128)(2,1)S(1)} %get-tuple-element.46), channel_id=1, source_target_pairs={{16,8},{17,9},{18,10},{19,11}} | collective-permute-start | bytes 294920 | tf_op jit(solution)/shard_map/ppermute | solution.py:539
  21.4 5.3 %collective-permute-start.4 = (bf16[48,1024]{1,0:T(8,128)(2,1)S(1)}, bf16[48,1024]{1,0:T(8,128)(2,1)S(1)}, u32[]{:S(2)}, u32[]{:S(2)}) collective-permute-start(bf16[48,1024]{1,0:T(8,128)(2,1)S(1)} %get-tuple-element.46), channel_id=1, source_target_pairs={{16,12},{17,13},{18,14},{19,15}} | collective-permute-start | bytes 294920 | tf_op jit(solution)/shard_map/ppermute | solution.py:539
  22.7 26.9 %collective-permute-start.11 = (bf16[256,1024]{1,0:T(8,128)(2,1)S(1)}, bf16[256,1024]{1,0:T(8,128)(2,1)S(1)}, u32[]{:S(2)}, u32[]{:S(2)}) collective-permute-start(bf16[256,1024]{1,0:T(8,128)(2,1)S(1)} %get-tuple-element.60), channel_id=1, source_target_pairs={{0,16},{16,0},{1,17},{17,1},{2,18},{18,2},{3,19},{19,3},{4,20},{20... | collective-permute-start | bytes 1572872 | tf_op jit(solution)/shard_map/ppermute | solution.py:503
  40.4 7.5 %collective-permute-start.5 = (bf16[544,256]{1,0:T(8,128)(2,1)S(1)}, bf16[544,256]{1,0:T(8,128)(2,1)S(1)}, u32[]{:S(2)}, u32[]{:S(2)}) collective-permute-start(bf16[544,256]{1,0:T(8,128)(2,1)S(1)} %shard_map.121.own0), channel_id=1, source_target_pairs={{0,4},{4,0},{8,12},{12,8},{1,5},{5,1},{9,13},{13,9},{2,6},{6,2},{1... | collective-permute-start | bytes 835592 | tf_op jit(solution)/shard_map/ppermute | solution.py:493
  40.5 7.4 %collective-permute-start.6 = (bf16[544,256]{1,0:T(8,128)(2,1)S(1)}, bf16[544,256]{1,0:T(8,128)(2,1)S(1)}, u32[]{:S(2)}, u32[]{:S(2)}) collective-permute-start(bf16[544,256]{1,0:T(8,128)(2,1)S(1)} %shard_map.122.own1), channel_id=1, source_target_pairs={{0,4},{4,0},{8,12},{12,8},{1,5},{5,1},{9,13},{13,9},{2,6},{6,2},{1... | collective-permute-start | bytes 835592 | tf_op jit(solution)/shard_map/ppermute | solution.py:493
  41.0 1.4 collective-permute-start.7
  43.0 3.7 %collective-permute-start.8 = (bf16[1,512]{1,0:T(2,128)(2,1)S(1)}, bf16[1,512]{1,0:T(2,128)(2,1)S(1)}, u32[]{:S(2)}, u32[]{:S(2)}) collective-permute-start(bf16[1,512]{1,0:T(2,128)(2,1)S(1)} %shard_map.123.mine), channel_id=1, source_target_pairs={{0,8},{4,12},{8,0},{12,4},{1,9},{5,13},{9,1},{13,5},{2,10},{6,14},... | collective-permute-start | bytes 3080 | tf_op jit(solution)/shard_map/ppermute | solution.py:496
  49.5 8.7 %collective-permute-start.9 = (bf16[256,640]{1,0:T(8,128)(2,1)S(1)}, bf16[256,640]{1,0:T(8,128)(2,1)S(1)}, u32[]{:S(2)}, u32[]{:S(2)}) collective-permute-start(bf16[256,640]{1,0:T(8,128)(2,1)S(1)} %get-tuple-element.59), channel_id=1, source_target_pairs={{0,8},{4,12},{8,0},{12,4},{1,9},{5,13},{9,1},{13,5},{2,10},{6,14},... | collective-permute-start | bytes 983048 | tf_op jit(solution)/shard_map/ppermute | solution.py:496
  49.6 14.2 %collective-permute-start.12 = (bf16[256,1024]{1,0:T(8,128)(2,1)S(1)}, bf16[256,1024]{1,0:T(8,128)(2,1)S(1)}, u32[]{:S(2)}, u32[]{:S(2)}) collective-permute-start(bf16[256,1024]{1,0:T(8,128)(2,1)S(1)} %collective-permute-done.11.w_x), channel_id=1, source_target_pairs={{0,1},{1,0},{2,3},{3,2},{4,5},{5,4},{6,7},{7,6},{8,9},{9,8},{10,11... | collective-permute-start | bytes 1572872 | tf_op jit(solution)/shard_map/ppermute | solution.py:506
  58.9 6.9 %collective-permute-start.10 = (bf16[256,512]{1,0:T(8,128)(2,1)S(1)}, bf16[256,512]{1,0:T(8,128)(2,1)S(1)}, u32[]{:S(2)}, u32[]{:S(2)}) collective-permute-start(bf16[256,512]{1,0:T(8,128)(2,1)S(1)} %shard_map.126.half), channel_id=1, source_target_pairs={{0,4},{4,0},{8,12},{12,8},{1,5},{5,1},{9,13},{13,9},{2,6},{6,2},{1... | collective-permute-start | bytes 786440 | tf_op jit(solution)/shard_map/ppermute | solution.py:493
  59.0 22.4 %collective-permute-start.16 = (bf16[2048,128]{1,0:T(8,128)(2,1)S(1)}, bf16[2048,128]{1,0:T(8,128)(2,1)S(1)}, u32[]{:S(2)}, u32[]{:S(2)}) collective-permute-start(bf16[2048,128]{1,0:T(8,128)(2,1)S(1)} %get-tuple-element.61), channel_id=1, source_target_pairs={{0,16},{16,0},{1,17},{17,1},{2,18},{18,2},{3,19},{19,3},{4,20},{20... | collective-permute-start | bytes 1572872 | tf_op jit(solution)/shard_map/ppermute | solution.py:503
  61.7 56.7 %copy-start.5 = (bf16[2048,128]{1,0:T(8,128)(2,1)S(1)}, bf16[2048,128]{1,0:T(8,128)(2,1)}, u32[]{:S(2)}) copy-start(bf16[2048,128]{1,0:T(8,128)(2,1)} %wk.1) | copy-start | bytes 1572868
  61.7 56.7 %copy-start.6 = (bf16[2048,128]{1,0:T(8,128)(2,1)S(1)}, bf16[2048,128]{1,0:T(8,128)(2,1)}, u32[]{:S(2)}) copy-start(bf16[2048,128]{1,0:T(8,128)(2,1)} %wv.1) | copy-start | bytes 1572868
  61.7 56.7 %copy-start.8 = (f32[4096]{0:T(1024)S(1)}, f32[4096]{0:T(1024)}, u32[]{:S(2)}) copy-start(f32[4096]{0:T(1024)} %param.18) | copy-start | bytes 49156
  61.7 17.7 %collective-permute-start.25 = (bf16[128,1024]{1,0:T(8,128)(2,1)S(1)}, bf16[128,1024]{1,0:T(8,128)(2,1)S(1)}, u32[]{:S(2)}, u32[]{:S(2)}) collective-permute-start(bf16[128,1024]{1,0:T(8,128)(2,1)S(1)} %get-tuple-element.68), channel_id=1, source_target_pairs={{0,16},{16,0},{1,17},{17,1},{2,18},{18,2},{3,19},{19,3},{4,20},{20... | collective-permute-start | bytes 786440 | tf_op jit(solution)/shard_map/ppermute | solution.py:503
  61.9 28.8 %collective-permute-start.18 = (bf16[1024,256]{1,0:T(8,128)(2,1)S(1)}, bf16[1024,256]{1,0:T(8,128)(2,1)S(1)}, u32[]{:S(2)}, u32[]{:S(2)}) collective-permute-start(bf16[1024,256]{1,0:T(8,128)(2,1)S(1)} %get-tuple-element.64), channel_id=1, source_target_pairs={{0,16},{16,0},{1,17},{17,1},{2,18},{18,2},{3,19},{19,3},{4,20},{20... | collective-permute-start | bytes 1572872 | tf_op jit(solution)/shard_map/ppermute | solution.py:503
  63.8 38.1 %collective-permute-start.20 = (bf16[1024,256]{1,0:T(8,128)(2,1)S(1)}, bf16[1024,256]{1,0:T(8,128)(2,1)S(1)}, u32[]{:S(2)}, u32[]{:S(2)}) collective-permute-start(bf16[1024,256]{1,0:T(8,128)(2,1)S(1)} %get-tuple-element.65), channel_id=1, source_target_pairs={{0,16},{16,0},{1,17},{17,1},{2,18},{18,2},{3,19},{19,3},{4,20},{20... | collective-permute-start | bytes 1572872 | tf_op jit(solution)/shard_map/ppermute | solution.py:503
  67.1 34.8 %collective-permute-start.14 = (bf16[256,1024]{1,0:T(8,128)(2,1)S(1)}, bf16[256,1024]{1,0:T(8,128)(2,1)S(1)}, u32[]{:S(2)}, u32[]{:S(2)}) collective-permute-start(bf16[256,1024]{1,0:T(8,128)(2,1)S(1)} %shard_map.127.l0.latent), channel_id=1, source_target_pairs={{0,8},{4,12},{8,0},{12,4},{1,9},{5,13},{9,1},{13,5},{2,10},{6,14},... | collective-permute-start | bytes 1572872 | tf_op jit(solution)/shard_map/ppermute | solution.py:496
  79.4 33.3 %collective-permute-start.23 = (bf16[256,1024]{1,0:T(8,128)(2,1)S(1)}, bf16[256,1024]{1,0:T(8,128)(2,1)S(1)}, u32[]{:S(2)}, u32[]{:S(2)}) collective-permute-start(bf16[256,1024]{1,0:T(8,128)(2,1)S(1)} %get-tuple-element.67), channel_id=1, source_target_pairs={{0,16},{16,0},{1,17},{17,1},{2,18},{18,2},{3,19},{19,3},{4,20},{20... | collective-permute-start | bytes 1572872 | tf_op jit(solution)/shard_map/ppermute | solution.py:503
  81.3 33.0 %collective-permute-start.17 = (bf16[2048,128]{1,0:T(8,128)(2,1)S(1)}, bf16[2048,128]{1,0:T(8,128)(2,1)S(1)}, u32[]{:S(2)}, u32[]{:S(2)}) collective-permute-start(bf16[2048,128]{1,0:T(8,128)(2,1)S(1)} %collective-permute-done.16.w_x), channel_id=1, source_target_pairs={{0,1},{1,0},{2,3},{3,2},{4,5},{5,4},{6,7},{7,6},{8,9},{9,8},{10,11... | collective-permute-start | bytes 1572872 | tf_op jit(solution)/shard_map/ppermute | solution.py:506
  90.7 24.1 %collective-permute-start.19 = (bf16[1024,256]{1,0:T(8,128)(2,1)S(1)}, bf16[1024,256]{1,0:T(8,128)(2,1)S(1)}, u32[]{:S(2)}, u32[]{:S(2)}) collective-permute-start(bf16[1024,256]{1,0:T(8,128)(2,1)S(1)} %collective-permute-done.18.x0), channel_id=1, source_target_pairs={{0,1},{1,0},{2,3},{3,2},{4,5},{5,4},{6,7},{7,6},{8,9},{9,8},{10,11... | collective-permute-start | bytes 1572872 | tf_op jit(solution)/shard_map/ppermute | solution.py:506
  101.9 14.6 %collective-permute-start.13 = (bf16[256,1024]{1,0:T(8,128)(2,1)S(1)}, bf16[256,1024]{1,0:T(8,128)(2,1)S(1)}, u32[]{:S(2)}, u32[]{:S(2)}) collective-permute-start(bf16[256,1024]{1,0:T(8,128)(2,1)S(1)} %shard_map.127.l0.latent), channel_id=1, source_target_pairs={{0,4},{4,0},{8,12},{12,8},{1,5},{5,1},{9,13},{13,9},{2,6},{6,2},{1... | collective-permute-start | bytes 1572872 | tf_op jit(solution)/shard_map/ppermute | solution.py:493
  101.9 14.9 %collective-permute-start.15 = (bf16[256,1024]{1,0:T(8,128)(2,1)S(1)}, bf16[256,1024]{1,0:T(8,128)(2,1)S(1)}, u32[]{:S(2)}, u32[]{:S(2)}) collective-permute-start(bf16[256,1024]{1,0:T(8,128)(2,1)S(1)} %collective-permute-done.14.l2), channel_id=1, source_target_pairs={{0,4},{4,0},{8,12},{12,8},{1,5},{5,1},{9,13},{13,9},{2,6},{6,2},{1... | collective-permute-start | bytes 1572872 | tf_op jit(solution)/shard_map/ppermute | solution.py:493
  112.8 14.8 %collective-permute-start.21 = (bf16[1024,256]{1,0:T(8,128)(2,1)S(1)}, bf16[1024,256]{1,0:T(8,128)(2,1)S(1)}, u32[]{:S(2)}, u32[]{:S(2)}) collective-permute-start(bf16[1024,256]{1,0:T(8,128)(2,1)S(1)} %collective-permute-done.20.x1), channel_id=1, source_target_pairs={{0,1},{1,0},{2,3},{3,2},{4,5},{5,4},{6,7},{7,6},{8,9},{9,8},{10,11... | collective-permute-start | bytes 1572872 | tf_op jit(solution)/shard_map/ppermute | solution.py:506
  114.3 24.5 %collective-permute-start.24 = (bf16[256,1024]{1,0:T(8,128)(2,1)S(1)}, bf16[256,1024]{1,0:T(8,128)(2,1)S(1)}, u32[]{:S(2)}, u32[]{:S(2)}) collective-permute-start(bf16[256,1024]{1,0:T(8,128)(2,1)S(1)} %collective-permute-done.23.x0), channel_id=1, source_target_pairs={{0,1},{1,0},{2,3},{3,2},{4,5},{5,4},{6,7},{7,6},{8,9},{9,8},{10,11... | collective-permute-start | bytes 1572872 | tf_op jit(solution)/shard_map/ppermute | solution.py:506
  114.8 26.3 %collective-permute-start.26 = (bf16[128,1024]{1,0:T(8,128)(2,1)S(1)}, bf16[128,1024]{1,0:T(8,128)(2,1)S(1)}, u32[]{:S(2)}, u32[]{:S(2)}) collective-permute-start(bf16[128,1024]{1,0:T(8,128)(2,1)S(1)} %get-tuple-element.69), channel_id=1, source_target_pairs={{0,16},{16,0},{1,17},{17,1},{2,18},{18,2},{3,19},{19,3},{4,20},{20... | collective-permute-start | bytes 786440 | tf_op jit(solution)/shard_map/ppermute | solution.py:503
  116.5 24.6 %collective-permute-start.27 = (bf16[128,1024]{1,0:T(8,128)(2,1)S(1)}, bf16[128,1024]{1,0:T(8,128)(2,1)S(1)}, u32[]{:S(2)}, u32[]{:S(2)}) collective-permute-start(bf16[128,1024]{1,0:T(8,128)(2,1)S(1)} %get-tuple-element.70), channel_id=1, source_target_pairs={{0,16},{16,0},{1,17},{17,1},{2,18},{18,2},{3,19},{19,3},{4,20},{20... | collective-permute-start | bytes 786440 | tf_op jit(solution)/shard_map/ppermute | solution.py:503
  116.8 26.3 %collective-permute-start.28 = (bf16[128,1024]{1,0:T(8,128)(2,1)S(1)}, bf16[128,1024]{1,0:T(8,128)(2,1)S(1)}, u32[]{:S(2)}, u32[]{:S(2)}) collective-permute-start(bf16[128,1024]{1,0:T(8,128)(2,1)S(1)} %collective-permute-done.25.x1), channel_id=1, source_target_pairs={{0,1},{1,0},{2,3},{3,2},{4,5},{5,4},{6,7},{7,6},{8,9},{9,8},{10,11... | collective-permute-start | bytes 786440 | tf_op jit(solution)/shard_map/ppermute | solution.py:506
  127.6 5.1 %collective-permute-start.22 = (bf16[272,256]{1,0:T(8,128)(2,1)S(1)}, bf16[272,256]{1,0:T(8,128)(2,1)S(1)}, u32[]{:S(2)}, u32[]{:S(2)}) collective-permute-start(bf16[272,256]{1,0:T(8,128)(2,1)S(1)} %get-tuple-element.66.kv_own), channel_id=1, source_target_pairs={{0,16},{16,0},{1,17},{17,1},{2,18},{18,2},{3,19},{19,3},{4,20},{20... | collective-permute-start | bytes 417800 | tf_op jit(solution)/shard_map/ppermute | solution.py:503
  139.8 9.6 %collective-permute-start.30 = (bf16[256,1024]{1,0:T(8,128)(2,1)S(1)}, bf16[256,1024]{1,0:T(8,128)(2,1)S(1)}, u32[]{:S(2)}, u32[]{:S(2)}) collective-permute-start(bf16[256,1024]{1,0:T(8,128)(2,1)S(1)} %get-tuple-element.74), channel_id=1, source_target_pairs={{4,0},{12,8},{5,1},{13,9},{6,2},{14,10},{7,3},{15,11},{20,16},{28,... | collective-permute-start | bytes 1572872 | tf_op jit(solution)/shard_map/ppermute | solution.py:729
  144.2 9.7 %collective-permute-start.32 = (bf16[256,1024]{1,0:T(8,128)(2,1)S(1)}, bf16[256,1024]{1,0:T(8,128)(2,1)S(1)}, u32[]{:S(2)}, u32[]{:S(2)}) collective-permute-start(bf16[256,1024]{1,0:T(8,128)(2,1)S(1)} %get-tuple-element.76), channel_id=1, source_target_pairs={{0,4},{8,12},{1,5},{9,13},{2,6},{10,14},{3,7},{11,15},{16,20},{24,... | collective-permute-start | bytes 1572872 | tf_op jit(solution)/shard_map/ppermute | solution.py:729
  145.5 9.7 %collective-permute-start.34 = (bf16[256,512]{1,0:T(8,128)(2,1)S(1)}, bf16[256,512]{1,0:T(8,128)(2,1)S(1)}, u32[]{:S(2)}, u32[]{:S(2)}) collective-permute-start(bf16[256,512]{1,0:T(8,128)(2,1)S(1)} %get-tuple-element.77), channel_id=1, source_target_pairs={{0,16},{16,0},{1,17},{17,1},{2,18},{18,2},{3,19},{19,3},{4,20},{20... | collective-permute-start | bytes 786440 | tf_op jit(solution)/shard_map/ppermute | solution.py:503
  147.4 11.3 %collective-permute-start.35 = (bf16[256,512]{1,0:T(8,128)(2,1)S(1)}, bf16[256,512]{1,0:T(8,128)(2,1)S(1)}, u32[]{:S(2)}, u32[]{:S(2)}) collective-permute-start(bf16[256,512]{1,0:T(8,128)(2,1)S(1)} %get-tuple-element.78), channel_id=1, source_target_pairs={{0,16},{16,0},{1,17},{17,1},{2,18},{18,2},{3,19},{19,3},{4,20},{20... | collective-permute-start | bytes 786440 | tf_op jit(solution)/shard_map/ppermute | solution.py:503
  149.3 20.0 %collective-permute-start.29 = (bf16[256,1024]{1,0:T(8,128)(2,1)S(1)}, bf16[256,1024]{1,0:T(8,128)(2,1)S(1)}, u32[]{:S(2)}, u32[]{:S(2)}) collective-permute-start(bf16[256,1024]{1,0:T(8,128)(2,1)S(1)} %get-tuple-element.72), channel_id=1, source_target_pairs={{0,4},{4,0},{8,12},{12,8},{1,5},{5,1},{9,13},{13,9},{2,6},{6,2},{1... | collective-permute-start | bytes 1572872 | tf_op jit(solution)/shard_map/ppermute | solution.py:493
  150.1 19.2 %collective-permute-start.31 = (bf16[256,1024]{1,0:T(8,128)(2,1)S(1)}, bf16[256,1024]{1,0:T(8,128)(2,1)S(1)}, u32[]{:S(2)}, u32[]{:S(2)}) collective-permute-start(bf16[256,1024]{1,0:T(8,128)(2,1)S(1)} %shard_map.134), channel_id=1, source_target_pairs={{0,8},{8,0},{1,9},{9,1},{2,10},{10,2},{3,11},{11,3},{16,24},{24,16... | collective-permute-start | bytes 1572872 | tf_op jit(solution)/shard_map/ppermute | solution.py:731
  154.5 14.8 %collective-permute-start.33 = (bf16[256,1024]{1,0:T(8,128)(2,1)S(1)}, bf16[256,1024]{1,0:T(8,128)(2,1)S(1)}, u32[]{:S(2)}, u32[]{:S(2)}) collective-permute-start(bf16[256,1024]{1,0:T(8,128)(2,1)S(1)} %shard_map.136), channel_id=1, source_target_pairs={{4,12},{12,4},{5,13},{13,5},{6,14},{14,6},{7,15},{15,7},{20,28},{2... | collective-permute-start | bytes 1572872 | tf_op jit(solution)/shard_map/ppermute | solution.py:731
  155.2 9.2 %collective-permute-start.36 = (bf16[256,512]{1,0:T(8,128)(2,1)S(1)}, bf16[256,512]{1,0:T(8,128)(2,1)S(1)}, u32[]{:S(2)}, u32[]{:S(2)}) collective-permute-start(bf16[256,512]{1,0:T(8,128)(2,1)S(1)} %collective-permute-done.34.x0), channel_id=1, source_target_pairs={{0,1},{1,0},{2,3},{3,2},{4,5},{5,4},{6,7},{7,6},{8,9},{9,8},{10,11... | collective-permute-start | bytes 786440 | tf_op jit(solution)/shard_map/ppermute | solution.py:506
  158.7 10.6 %collective-permute-start.37 = (bf16[256,512]{1,0:T(8,128)(2,1)S(1)}, bf16[256,512]{1,0:T(8,128)(2,1)S(1)}, u32[]{:S(2)}, u32[]{:S(2)}) collective-permute-start(bf16[256,512]{1,0:T(8,128)(2,1)S(1)} %collective-permute-done.35.x1), channel_id=1, source_target_pairs={{0,1},{1,0},{2,3},{3,2},{4,5},{5,4},{6,7},{7,6},{8,9},{9,8},{10,11... | collective-permute-start | bytes 786440 | tf_op jit(solution)/shard_map/ppermute | solution.py:506
  170.7 1.6 collective-permute-start.38
  173.5 8.5 %collective-permute-start.39 = (bf16[256,512]{1,0:T(8,128)(2,1)S(1)}, bf16[256,512]{1,0:T(8,128)(2,1)S(1)}, u32[]{:S(2)}, u32[]{:S(2)}) collective-permute-start(bf16[256,512]{1,0:T(8,128)(2,1)S(1)} %get-tuple-element.82), channel_id=1, source_target_pairs={{0,8},{4,12},{8,0},{12,4},{1,9},{5,13},{9,1},{13,5},{2,10},{6,14},... | collective-permute-start | bytes 786440 | tf_op jit(solution)/shard_map/ppermute | solution.py:496
  173.8 5.5 %collective-permute-start.40 = (bf16[1,512]{1,0:T(2,128)(2,1)S(1)}, bf16[1,512]{1,0:T(2,128)(2,1)S(1)}, u32[]{:S(2)}, u32[]{:S(2)}) collective-permute-start(bf16[1,512]{1,0:T(2,128)(2,1)S(1)} %get-tuple-element.84), channel_id=1, source_target_pairs={{0,16},{4,20},{1,17},{5,21},{2,18},{6,22},{3,19},{7,23}} | collective-permute-start | bytes 3080 | tf_op jit(solution)/shard_map/ppermute | solution.py:759
  175.1 6.5 %collective-permute-start.41 = (bf16[1,512]{1,0:T(2,128)(2,1)S(1)}, bf16[1,512]{1,0:T(2,128)(2,1)S(1)}, u32[]{:S(2)}, u32[]{:S(2)}) collective-permute-start(bf16[1,512]{1,0:T(2,128)(2,1)S(1)} %get-tuple-element.84), channel_id=1, source_target_pairs={{8,16},{12,20},{9,17},{13,21},{10,18},{14,22},{11,19},{15,23}} | collective-permute-start | bytes 3080 | tf_op jit(solution)/shard_map/ppermute | solution.py:760
  182.9 1.6 collective-permute-start.42
  (5 other events, 57.4 us)
